TPU v7x, 1024 devices: a whole 8x8x8 slice. The times are simulated.
1024 devices in a mesh: span: 8 (over x), pitch: 8 (over y_lo, core), chord: 16 (over z, y_hi).
Axes of the slice: x: 8, y: 8 (y_hi: 2, y_lo: 4; y = y_hi * 4 + y_lo), z: 8, core: 2. Of those that a mesh axis runs over, the one named last changes fastest.
Arguments:
- adjoint_start: float32 [3, 128, 256, 2048], P(None, 'span', 'pitch', 'chord'), may hold values from -6 to 6
- sensitivity_source: float32 [3, 128, 256, 2048], P(None, 'span', 'pitch', 'chord'), may hold values from -6 to 6
- stiffness_class: int32 [128, 256, 2048], P('span', 'pitch', 'chord'), may hold values from 0 to 7
- stiffness_table: float32 [8], replicated, may hold values from 0.25 to 4
- wall_cell: int32 [4194304], P(('span', 'pitch', 'chord')), may hold values from 0 to 65535
- patch_owner: int32 [4194304, 1], P(('span', 'pitch', 'chord')), may hold values from 0 to 2047; in each aligned block of 4096 rows (0 to 4095, 4096 to 8191, ...) at most 4 rows name the same one
- wall_normal: float32 [3, 4194304], P(None, ('span', 'pitch', 'chord')), may hold values from -1 to 1
- mode_shape: float32 [8, 4194304], P(None, ('span', 'pitch', 'chord')), may hold values from -6 to 6
Outputs:
- adjoint: float32 [3, 128, 256, 2048], P(None, 'span', 'pitch', 'chord')
- patch_grad: float32 [8, 131072], P(None, ('span', 'pitch', 'chord'))
Inputs may be any that keep to these rules, and one draw needn't show every extreme that they name: `patch_owner`: within the rows of one device, no patch is named by more than 4 rows, a bound that some block reaches.
All inputs are finite; a program needn't handle non-finite values.
Results may differ from a plain program's by a relative error of at most 0.00018.
Values sent between devices are 32-bit elements; how exact they have to be, the bound alone decides.
No kernel may reach another device: no remote copies, remote signals or barrier semaphores. Data moves between devices by JAX's collectives and lax.ppermute only.
A program may use at most 32 MiB of HBM per device.

v0:
```python
import math

import jax
import jax.numpy as jnp
from jax import lax
from jax.sharding import PartitionSpec as P

PATCH_DEV = 128
CAP = 4
MODES = 8
SWEEPS = 3


MASS_SHIFT = 0.5
RELAXATION = 0.8
DIAGONAL_SUM = 10.5
LAME_WEIGHTS = ((3.0, 1.0, 1.0), (1.0, 3.0, 1.0), (1.0, 1.0, 3.0))


def with_halo(x, sides, width):
    for axis, dim in sides:
        size, length = (lax.axis_size(axis), x.shape[dim])
        up = [(i, (i + 1) % size) for i in range(size - 1)]
        down = [(j, i) for i, j in up]
        last = lax.slice_in_dim(x, length - width, length, axis=dim)
        leading = lax.slice_in_dim(x, 0, width, axis=dim)
        before = lax.ppermute(last, axis, up)
        after = lax.ppermute(leading, axis, down)
        x = jnp.concatenate([before, x, after], axis=dim)
    return x


def stiffness_from(classes, table):
    result = jnp.zeros(classes.shape, jnp.float32)
    for number in range(table.shape[0]):
        result = result + jnp.where(classes == number, table[number], 0.0)
    return result


def operator_image(padded):
    center = padded[:, 1:-1, 1:-1, 1:-1]
    along_span = 2.0 * center - padded[:, 2:, 1:-1, 1:-1] - padded[:, :-2, 1:-1, 1:-1]
    along_pitch = 2.0 * center - padded[:, 1:-1, 2:, 1:-1] - padded[:, 1:-1, :-2, 1:-1]
    along_chord = 2.0 * center - padded[:, 1:-1, 1:-1, 2:] - padded[:, 1:-1, 1:-1, :-2]
    weights = jnp.array(LAME_WEIGHTS, jnp.float32)
    image = MASS_SHIFT * center
    image = image + weights[:, 0][:, None, None, None] * along_span
    image = image + weights[:, 1][:, None, None, None] * along_pitch
    image = image + weights[:, 2][:, None, None, None] * along_chord
    return image


def relax_step(adjoint, source, stiffness, image):
    return adjoint + RELAXATION * (source - image) / (DIAGONAL_SUM * stiffness)


def pick_traction(field, wall_cell):
    depth = field.shape[3]
    planes = field.shape[1] * field.shape[2]
    plane_major = field.reshape(3, planes, depth).transpose(1, 0, 2).reshape(planes, 3 * depth)
    plane_index = wall_cell // depth
    depth_index = wall_cell % depth
    plane_onehot = (plane_index[:, None] == jnp.arange(planes, dtype=jnp.int32)[None]).astype(
        jnp.float32
    )
    selected = jnp.dot(
        plane_onehot,
        plane_major,
        precision=lax.Precision.HIGHEST,
        preferred_element_type=jnp.float32,
    )
    selected = selected.reshape(-1, 3, depth)
    depth_onehot = (depth_index[:, None] == jnp.arange(depth, dtype=jnp.int32)[None]).astype(
        jnp.float32
    )
    return jnp.sum(selected * depth_onehot[:, None, :], axis=2).T


def owner_weighted(contribution, owner_index, chord_count):
    owner_onehot = (
        owner_index[None, :] == jnp.arange(chord_count, dtype=jnp.int32)[:, None]
    ).astype(jnp.float32)
    weighted = contribution[:, None, :] * owner_onehot[None]
    return weighted.reshape(-1, contribution.shape[1])


def slot_ranks(target):
    total_rows = target.shape[0]
    block_rows = math.gcd(total_rows, 512)
    positions = jnp.arange(total_rows, dtype=jnp.int32)

    def earlier_equal(pieces):
        block_target, block_position = pieces
        matching = (block_target[:, None] == target[None]) & (
            positions[None] < block_position[:, None]
        )
        return jnp.sum(matching.astype(jnp.int32), axis=1)

    ranked = lax.map(
        earlier_equal, (target.reshape(-1, block_rows), positions.reshape(-1, block_rows))
    )
    return ranked.reshape(total_rows)


def body(
    adjoint_start,
    sensitivity_source,
    stiffness_class,
    stiffness_table,
    wall_cell,
    patch_owner,
    wall_normal,
    mode_shape,
):
    stiffness = stiffness_from(stiffness_class, stiffness_table)
    adjoint = adjoint_start
    for sweep_index in range(SWEEPS):
        product = stiffness[None] * adjoint
        padded = with_halo(product, (("span", 1), ("pitch", 2), ("chord", 3)), 1)
        adjoint = relax_step(adjoint, sensitivity_source, stiffness, operator_image(padded))
    traction = pick_traction(stiffness[None] * adjoint, wall_cell)
    normal_part = jnp.sum(wall_normal * traction, axis=0)
    contribution = mode_shape * normal_part[None]
    target = patch_owner[:, 0]
    chord_count = lax.axis_size("chord")
    owner_index = target // PATCH_DEV
    local_patch = target % PATCH_DEV
    weighted = owner_weighted(contribution, owner_index, chord_count)
    slot_index = local_patch * CAP + slot_ranks(target)
    slot_onehot = (
        slot_index[:, None] == jnp.arange(PATCH_DEV * CAP, dtype=jnp.int32)[None]
    ).astype(jnp.float32)
    buffer = jnp.dot(
        weighted, slot_onehot, precision=lax.Precision.HIGHEST, preferred_element_type=jnp.float32
    )
    buffer = buffer.reshape(MODES, chord_count, PATCH_DEV * CAP)
    arrived = lax.all_to_all(buffer, "chord", split_axis=1, concat_axis=1, tiled=True)
    patch_grad = arrived.reshape(MODES, chord_count, PATCH_DEV, CAP).sum(axis=(1, 3))
    return (adjoint, patch_grad)


def solution(mesh):
    in_specs = (
        P(None, "span", "pitch", "chord"),
        P(None, "span", "pitch", "chord"),
        P("span", "pitch", "chord"),
        P(),
        P(("span", "pitch", "chord")),
        P(("span", "pitch", "chord"), None),
        P(None, ("span", "pitch", "chord")),
        P(None, ("span", "pitch", "chord")),
    )
    out_specs = (P(None, "span", "pitch", "chord"), P(None, ("span", "pitch", "chord")))
    return jax.shard_map(body, mesh=mesh, in_specs=in_specs, out_specs=out_specs, check_vma=False)
```

profile of v0, /device:TPU:24, one launch (start us, length us, event | category | flops | bytes accessed | tf_op | source)
XLA Modules:
  0.0 194.7 jit_solution(782518186462734096)
XLA Ops:
  2.3 6.3 %broadcast_multiply_fusion.4 = (f32[16,32,128]{2,1,0:T(8,128)S(1)}, f32[16,32,128]{2,1,0:T(8,128)S(1)}) fusion(f32[]{:T(128)} %bitcast.7, s32[16,32,128]{2,1,0:T(8,128)} %param.15, f32[]{:T(128)} %bitcast.6, f32[]{:T(128)} %bitcast.5, f32[]{:T(128)} %bitcast.4, f32[]{:T(128)} %bitcast.3, f32[]{:T(128)} %bitcast.2, f32[]{:T(128)} %bitcast.1, f32[]{:T(128)} %bitcast), kind=kLoop, calls=%fused_computation.133 | loop fusion | flops 1572864 | bytes 786464 | tf_op jit(solution)/shard_map/mul | solution.py:54
  8.7 2.4 %collective-permute-start = (f32[3,1,32,128]{3,2,1,0:T(8,128)S(1)}, f32[3,1,32,128]{3,2,1,0:T(8,128)S(1)}, u32[]{:S(2)}, u32[]{:S(2)}) collective-permute-start(f32[3,1,32,128]{3,2,1,0:T(8,128)S(1)} %get-tuple-element.88), channel_id=1, source_target_pairs={{128,0},{256,128},{384,256},{512,384},{640,512},{768,640},{896,768... | collective-permute-start | bytes 147464 | tf_op jit(solution)/shard_map/ppermute | solution.py:28
  11.1 3.4 %collective-permute-start.1 = (f32[3,1,32,128]{3,2,1,0:T(8,128)S(1)}, f32[3,1,32,128]{3,2,1,0:T(8,128)S(1)}, u32[]{:S(2)}, u32[]{:S(2)}) collective-permute-start(f32[3,1,32,128]{3,2,1,0:T(8,128)S(1)} %get-tuple-element.87), channel_id=1, source_target_pairs={{0,128},{128,256},{256,384},{384,512},{512,640},{640,768},{768,896... | collective-permute-start | bytes 147464 | tf_op jit(solution)/shard_map/ppermute | solution.py:27
  14.6 3.7 %collective-permute-done.1 = f32[3,1,32,128]{3,2,1,0:T(8,128)S(1)} collective-permute-done((f32[3,1,32,128]{3,2,1,0:T(8,128)S(1)}, f32[3,1,32,128]{3,2,1,0:T(8,128)S(1)}, u32[]{:S(2)}, u32[]{:S(2)}) %collective-permute-start.1) | collective-permute-done | bytes 49184 | tf_op jit(solution)/shard_map/ppermute | solution.py:27
  20.3 2.4 %collective-permute-start.3 = (f32[3,18,1,128]{3,2,1,0:T(1,128)S(1)}, f32[3,18,1,128]{3,2,1,0:T(1,128)S(1)}, u32[]{:S(2)}, u32[]{:S(2)}) collective-permute-start(f32[3,18,1,128]{3,2,1,0:T(1,128)S(1)} %get-tuple-element.81), channel_id=1, source_target_pairs={{0,16},{16,32},{32,48},{48,64},{64,80},{80,96},{96,112},{1,17},{17... | collective-permute-start | bytes 82952 | tf_op jit(solution)/shard_map/ppermute | solution.py:27
  22.7 2.8 %collective-permute-done.3 = f32[3,18,1,128]{3,2,1,0:T(1,128)S(1)} collective-permute-done((f32[3,18,1,128]{3,2,1,0:T(1,128)S(1)}, f32[3,18,1,128]{3,2,1,0:T(1,128)S(1)}, u32[]{:S(2)}, u32[]{:S(2)}) %collective-permute-start.3) | collective-permute-done | bytes 27680 | tf_op jit(solution)/shard_map/ppermute | solution.py:27
  30.9 8.4 %collective-permute-start.5 = (f32[3,18,34,1]{2,3,1,0:T(1,128)S(1)}, f32[3,18,34,1]{2,3,1,0:T(1,128)S(1)}, u32[]{:S(2)}, u32[]{:S(2)}) collective-permute-start(f32[3,18,34,1]{2,3,1,0:T(1,128)S(1)} %copy.34), channel_id=1, source_target_pairs={{0,1},{1,2},{2,3},{3,4},{4,5},{5,6},{6,7},{7,8},{8,9},{9,10},{10,1... | collective-permute-start | bytes 22040 | tf_op jit(solution)/shard_map/ppermute | solution.py:27
  43.7 4.5 %broadcast_multiply_fusion.2 = (f32[3,16,32,128]{3,2,1,0:T(8,128)S(1)}, f32[3,16,32,128]{3,2,1,0:T(8,128)}) fusion(f32[16,32,128]{2,1,0:T(8,128)S(1)} %get-tuple-element.68, f32[3,16,32,128]{3,2,1,0:T(8,128)} %param.13, f32[16,32,128]{2,1,0:T(8,128)S(1)} %get-tuple-element.67, f32[3,16,32,128]{3,2,1,0:T(8,128)S(1)} %copy-done, ...), kind=kLoop, calls=%fused_computation.128 | loop fusion | flops 7274496 | bytes 4624772 | tf_op jit(solution)/shard_map/mul | solution.py:118
  48.2 1.9 collective-permute-start.6
  50.2 3.9 %collective-permute-start.7 = (f32[3,1,32,128]{3,2,1,0:T(8,128)S(1)}, f32[3,1,32,128]{3,2,1,0:T(8,128)S(1)}, u32[]{:S(2)}, u32[]{:S(2)}) collective-permute-start(f32[3,1,32,128]{3,2,1,0:T(8,128)S(1)} %get-tuple-element.85), channel_id=1, source_target_pairs={{0,128},{128,256},{256,384},{384,512},{512,640},{640,768},{768,896... | collective-permute-start | bytes 147464 | tf_op jit(solution)/shard_map/ppermute | solution.py:27
  54.1 16.4 %while.11 = (s32[]{:T(128)}, s32[8,512]{1,0:T(8,128)S(1)}, s32[8,512]{1,0:T(8,128)S(1)}, s32[4096,1]{0,1:T(1,128)S(1)}, s32[8,512]{1,0:T(8,128)S(1)}, /*index=5*/s32[]{:T(128)}, s32[]{:T(128)}) while((s32[]{:T(128)}, s32[8,512]{1,0:T(8,128)S(1)}, s32[8,512]{1,0:T(8,128)S(1)}, s32[4096,1]{0,1:T(1,128)S(1)}, s32[8,512]{1,0:T(8,128)S(1)}, ...), condition=%wide.region_4.5_spmd.clone, body=%wide.region_2.4_spmd.clone.sunk | while | flops 10485250 | bytes 34901 | solution.py:99
  54.1 1.9 %convert_reduce_fusion.2 = s32[512]{0:T(512)S(1)} fusion(s32[512]{0:T(512)S(1)} %bitcast.55, s32[4096]{0:T(1024)S(1)} %bitcast.52, s32[512]{0:T(512)S(1)} %bitcast.56), kind=kLoop, calls=%fused_computation.2.clone.1 | loop fusion | flops 10485248 | bytes 22528 | tf_op jit(solution)/shard_map/while/body/eval_jaxpr/reduce_sum | solution.py:97
  56.2 1.9 %convert_reduce_fusion.2 = s32[512]{0:T(512)S(1)} fusion(s32[512]{0:T(512)S(1)} %bitcast.55, s32[4096]{0:T(1024)S(1)} %bitcast.52, s32[512]{0:T(512)S(1)} %bitcast.56), kind=kLoop, calls=%fused_computation.2.clone.1 | loop fusion | flops 10485248 | bytes 22528 | tf_op jit(solution)/shard_map/while/body/eval_jaxpr/reduce_sum | solution.py:97
  58.2 1.9 %convert_reduce_fusion.2 = s32[512]{0:T(512)S(1)} fusion(s32[512]{0:T(512)S(1)} %bitcast.55, s32[4096]{0:T(1024)S(1)} %bitcast.52, s32[512]{0:T(512)S(1)} %bitcast.56), kind=kLoop, calls=%fused_computation.2.clone.1 | loop fusion | flops 10485248 | bytes 22528 | tf_op jit(solution)/shard_map/while/body/eval_jaxpr/reduce_sum | solution.py:97
  60.3 1.9 %convert_reduce_fusion.2 = s32[512]{0:T(512)S(1)} fusion(s32[512]{0:T(512)S(1)} %bitcast.55, s32[4096]{0:T(1024)S(1)} %bitcast.52, s32[512]{0:T(512)S(1)} %bitcast.56), kind=kLoop, calls=%fused_computation.2.clone.1 | loop fusion | flops 10485248 | bytes 22528 | tf_op jit(solution)/shard_map/while/body/eval_jaxpr/reduce_sum | solution.py:97
  62.3 1.9 %convert_reduce_fusion.2 = s32[512]{0:T(512)S(1)} fusion(s32[512]{0:T(512)S(1)} %bitcast.55, s32[4096]{0:T(1024)S(1)} %bitcast.52, s32[512]{0:T(512)S(1)} %bitcast.56), kind=kLoop, calls=%fused_computation.2.clone.1 | loop fusion | flops 10485248 | bytes 22528 | tf_op jit(solution)/shard_map/while/body/eval_jaxpr/reduce_sum | solution.py:97
  64.3 1.9 %convert_reduce_fusion.2 = s32[512]{0:T(512)S(1)} fusion(s32[512]{0:T(512)S(1)} %bitcast.55, s32[4096]{0:T(1024)S(1)} %bitcast.52, s32[512]{0:T(512)S(1)} %bitcast.56), kind=kLoop, calls=%fused_computation.2.clone.1 | loop fusion | flops 10485248 | bytes 22528 | tf_op jit(solution)/shard_map/while/body/eval_jaxpr/reduce_sum | solution.py:97
  66.4 1.9 %convert_reduce_fusion.2 = s32[512]{0:T(512)S(1)} fusion(s32[512]{0:T(512)S(1)} %bitcast.55, s32[4096]{0:T(1024)S(1)} %bitcast.52, s32[512]{0:T(512)S(1)} %bitcast.56), kind=kLoop, calls=%fused_computation.2.clone.1 | loop fusion | flops 10485248 | bytes 22528 | tf_op jit(solution)/shard_map/while/body/eval_jaxpr/reduce_sum | solution.py:97
  68.4 1.9 %convert_reduce_fusion.2 = s32[512]{0:T(512)S(1)} fusion(s32[512]{0:T(512)S(1)} %bitcast.55, s32[4096]{0:T(1024)S(1)} %bitcast.52, s32[512]{0:T(512)S(1)} %bitcast.56), kind=kLoop, calls=%fused_computation.2.clone.1 | loop fusion | flops 10485248 | bytes 22528 | tf_op jit(solution)/shard_map/while/body/eval_jaxpr/reduce_sum | solution.py:97
  72.5 2.4 %collective-permute-start.9 = (f32[3,18,1,128]{3,2,1,0:T(1,128)S(1)}, f32[3,18,1,128]{3,2,1,0:T(1,128)S(1)}, u32[]{:S(2)}, u32[]{:S(2)}) collective-permute-start(f32[3,18,1,128]{3,2,1,0:T(1,128)S(1)} %get-tuple-element.79), channel_id=1, source_target_pairs={{0,16},{16,32},{32,48},{48,64},{64,80},{80,96},{96,112},{1,17},{17... | collective-permute-start | bytes 82952 | tf_op jit(solution)/shard_map/ppermute | solution.py:27
  74.9 2.7 %collective-permute-done.9 = f32[3,18,1,128]{3,2,1,0:T(1,128)S(1)} collective-permute-done((f32[3,18,1,128]{3,2,1,0:T(1,128)S(1)}, f32[3,18,1,128]{3,2,1,0:T(1,128)S(1)}, u32[]{:S(2)}, u32[]{:S(2)}) %collective-permute-start.9) | collective-permute-done | bytes 27680 | tf_op jit(solution)/shard_map/ppermute | solution.py:27
  82.6 8.8 %collective-permute-start.11 = (f32[3,18,34,1]{2,3,1,0:T(1,128)S(1)}, f32[3,18,34,1]{2,3,1,0:T(1,128)S(1)}, u32[]{:S(2)}, u32[]{:S(2)}) collective-permute-start(f32[3,18,34,1]{2,3,1,0:T(1,128)S(1)} %copy.38), channel_id=1, source_target_pairs={{0,1},{1,2},{2,3},{3,4},{4,5},{5,6},{6,7},{7,8},{8,9},{9,10},{10,1... | collective-permute-start | bytes 22040 | tf_op jit(solution)/shard_map/ppermute | solution.py:27
  96.0 4.5 %broadcast_multiply_fusion.1 = (f32[3,16,32,128]{3,2,1,0:T(8,128)S(1)}, f32[3,16,32,128]{3,2,1,0:T(8,128)}) fusion(f32[16,32,128]{2,1,0:T(8,128)S(1)} %get-tuple-element.68, f32[3,16,32,128]{3,2,1,0:T(8,128)} %get-tuple-element.66, f32[16,32,128]{2,1,0:T(8,128)S(1)} %get-tuple-element.67, f32[3,16,32,128]{3,2,1,0:T(8,128)S(1)} %copy-done, ...), kind=kLoop, calls=%fused_computation.127 | loop fusion | flops 7274496 | bytes 4624772 | tf_op jit(solution)/shard_map/mul | solution.py:118
  100.6 9.3 %collective-permute-start.12 = (f32[3,1,32,128]{3,2,1,0:T(8,128)S(1)}, f32[3,1,32,128]{3,2,1,0:T(8,128)S(1)}, u32[]{:S(2)}, u32[]{:S(2)}) collective-permute-start(f32[3,1,32,128]{3,2,1,0:T(8,128)S(1)} %get-tuple-element.84), channel_id=1, source_target_pairs={{128,0},{256,128},{384,256},{512,384},{640,512},{768,640},{896,768... | collective-permute-start | bytes 147464 | tf_op jit(solution)/shard_map/ppermute | solution.py:28
  111.8 5.2 %collective-permute-done.13 = f32[3,1,32,128]{3,2,1,0:T(8,128)S(1)} collective-permute-done((f32[3,1,32,128]{3,2,1,0:T(8,128)S(1)}, f32[3,1,32,128]{3,2,1,0:T(8,128)S(1)}, u32[]{:S(2)}, u32[]{:S(2)}) %collective-permute-start.13) | collective-permute-done | bytes 49184 | tf_op jit(solution)/shard_map/ppermute | solution.py:27
  119.0 2.4 %collective-permute-start.15 = (f32[3,18,1,128]{3,2,1,0:T(1,128)S(1)}, f32[3,18,1,128]{3,2,1,0:T(1,128)S(1)}, u32[]{:S(2)}, u32[]{:S(2)}) collective-permute-start(f32[3,18,1,128]{3,2,1,0:T(1,128)S(1)} %get-tuple-element.77), channel_id=1, source_target_pairs={{0,16},{16,32},{32,48},{48,64},{64,80},{80,96},{96,112},{1,17},{17... | collective-permute-start | bytes 82952 | tf_op jit(solution)/shard_map/ppermute | solution.py:27
  121.5 2.7 %collective-permute-done.15 = f32[3,18,1,128]{3,2,1,0:T(1,128)S(1)} collective-permute-done((f32[3,18,1,128]{3,2,1,0:T(1,128)S(1)}, f32[3,18,1,128]{3,2,1,0:T(1,128)S(1)}, u32[]{:S(2)}, u32[]{:S(2)}) %collective-permute-start.15) | collective-permute-done | bytes 27680 | tf_op jit(solution)/shard_map/ppermute | solution.py:27
  130.8 8.6 %collective-permute-start.17 = (f32[3,18,34,1]{2,3,1,0:T(1,128)S(1)}, f32[3,18,34,1]{2,3,1,0:T(1,128)S(1)}, u32[]{:S(2)}, u32[]{:S(2)}) collective-permute-start(f32[3,18,34,1]{2,3,1,0:T(1,128)S(1)} %copy.42), channel_id=1, source_target_pairs={{0,1},{1,2},{2,3},{3,4},{4,5},{5,6},{6,7},{7,8},{8,9},{9,10},{10,1... | collective-permute-start | bytes 22040 | tf_op jit(solution)/shard_map/ppermute | solution.py:27
  142.5 4.5 %broadcast_multiply_fusion = (f32[3,16,32,128]{3,2,1,0:T(8,128)}, f32[3,16,32,128]{3,2,1,0:T(8,128)}) fusion(f32[16,32,128]{2,1,0:T(8,128)S(1)} %get-tuple-element.68, f32[3,16,32,128]{3,2,1,0:T(8,128)S(1)} %copy-done.3, f32[16,32,128]{2,1,0:T(8,128)S(1)} %get-tuple-element.67, f32[3,16,32,128]{3,2,1,0:T(8,128)S(1)} %copy-done, ...), kind=kLoop, calls=%fused_computation.126 | loop fusion | flops 7274496 | bytes 4624772 | tf_op jit(solution)/shard_map/mul | solution.py:121
  148.5 7.8 %multiply_reduce_fusion = f32[4096,3]{0,1:T(4,128)S(1)} fusion(s32[4096]{0:T(1024)S(1)} %get-tuple-element.90, f32[4096,128]{0,1:T(8,128)} %fusion.14, f32[512,3,128]{0,2,1:T(8,128)S(1)} %copy.44), kind=kOutput, calls=%fused_computation.12 | convolution fusion | flops 9668907008 | bytes 2949120 | tf_op jit(solution)/shard_map/dot_general | solution.py:66
  156.4 3.1 %fusion.7 = f32[8,16,512]{2,1,0:T(8,128)S(1)} fusion(s32[4096]{0:T(1024)S(1)} %bitcast.58, f32[16,4096]{1,0:T(8,128)S(1)} %fusion.63, f32[8,4096]{1,0:T(8,128)S(1)} %broadcast_multiply_fusion.5), kind=kOutput, calls=%fused_computation.11 | convolution fusion | flops 3223846912 | bytes 671744 | tf_op jit(solution)/shard_map/dot_general | solution.py:133
  159.7 34.1 %all_to_all.5 = f32[8,16,512]{2,0,1:T(8,128)S(1)} all-to-all(f32[8,16,512]{2,0,1:T(8,128)S(1)} %copy.45), channel_id=1, replica_groups=mesh['span'=8,'pitch'=8,'chord'=16] {'chord'}, dimensions={1} | all-to-all | bytes 524288 | tf_op jit(solution)/shard_map/all_to_all | solution.py:137
  (103 shorter events, 41.8 us)
Async XLA Ops:
  0.6 7.9 %copy-start.2 = (f32[3,16,32,128]{3,2,1,0:T(8,128)S(1)}, f32[3,16,32,128]{3,2,1,0:T(8,128)}, u32[]{:S(2)}) copy-start(f32[3,16,32,128]{3,2,1,0:T(8,128)} %param.13) | copy-start | bytes 2359300
  8.7 6.0 %collective-permute-start = (f32[3,1,32,128]{3,2,1,0:T(8,128)S(1)}, f32[3,1,32,128]{3,2,1,0:T(8,128)S(1)}, u32[]{:S(2)}, u32[]{:S(2)}) collective-permute-start(f32[3,1,32,128]{3,2,1,0:T(8,128)S(1)} %get-tuple-element.88), channel_id=1, source_target_pairs={{128,0},{256,128},{384,256},{512,384},{640,512},{768,640},{896,768... | collective-permute-start | bytes 147464 | tf_op jit(solution)/shard_map/ppermute | solution.py:28
  11.1 7.2 %collective-permute-start.1 = (f32[3,1,32,128]{3,2,1,0:T(8,128)S(1)}, f32[3,1,32,128]{3,2,1,0:T(8,128)S(1)}, u32[]{:S(2)}, u32[]{:S(2)}) collective-permute-start(f32[3,1,32,128]{3,2,1,0:T(8,128)S(1)} %get-tuple-element.87), channel_id=1, source_target_pairs={{0,128},{128,256},{256,384},{384,512},{512,640},{640,768},{768,896... | collective-permute-start | bytes 147464 | tf_op jit(solution)/shard_map/ppermute | solution.py:27
  18.4 4.3 %collective-permute-start.2 = (f32[3,18,1,128]{3,2,1,0:T(1,128)S(1)}, f32[3,18,1,128]{3,2,1,0:T(1,128)S(1)}, u32[]{:S(2)}, u32[]{:S(2)}) collective-permute-start(f32[3,18,1,128]{3,2,1,0:T(1,128)S(1)} %get-tuple-element.82), channel_id=1, source_target_pairs={{16,0},{32,16},{48,32},{64,48},{80,64},{96,80},{112,96},{17,1},{33... | collective-permute-start | bytes 82952 | tf_op jit(solution)/shard_map/ppermute | solution.py:28
  20.3 5.2 %collective-permute-start.3 = (f32[3,18,1,128]{3,2,1,0:T(1,128)S(1)}, f32[3,18,1,128]{3,2,1,0:T(1,128)S(1)}, u32[]{:S(2)}, u32[]{:S(2)}) collective-permute-start(f32[3,18,1,128]{3,2,1,0:T(1,128)S(1)} %get-tuple-element.81), channel_id=1, source_target_pairs={{0,16},{16,32},{32,48},{48,64},{64,80},{80,96},{96,112},{1,17},{17... | collective-permute-start | bytes 82952 | tf_op jit(solution)/shard_map/ppermute | solution.py:27
  27.3 3.1 %copy-start.1 = (f32[3,18,34,1]{3,2,1,0:T(8,128)S(1)}, f32[3,18,34,1]{3,2,1,0:T(8,128)}, u32[]{:S(2)}) copy-start(f32[3,18,34,1]{3,2,1,0:T(8,128)} %get-tuple-element.76) | copy-start | bytes 22036
  27.3 12.6 %copy-start.4 = (s32[4096,1]{0,1:T(1,128)S(1)}, s32[4096,1]{0,1:T(1,128)}, u32[]{:S(2)}) copy-start(s32[4096,1]{0,1:T(1,128)} %param.18) | copy-start | bytes 49156
  29.2 11.5 %collective-permute-start.4 = (f32[3,18,34,1]{2,3,1,0:T(1,128)S(1)}, f32[3,18,34,1]{2,3,1,0:T(1,128)S(1)}, u32[]{:S(2)}, u32[]{:S(2)}) collective-permute-start(f32[3,18,34,1]{2,3,1,0:T(1,128)S(1)} %copy.32), channel_id=1, source_target_pairs={{1,0},{2,1},{3,2},{4,3},{5,4},{6,5},{7,6},{8,7},{9,8},{10,9},{11,1... | collective-permute-start | bytes 22040 | tf_op jit(solution)/shard_map/ppermute | solution.py:28
  30.9 11.2 %collective-permute-start.5 = (f32[3,18,34,1]{2,3,1,0:T(1,128)S(1)}, f32[3,18,34,1]{2,3,1,0:T(1,128)S(1)}, u32[]{:S(2)}, u32[]{:S(2)}) collective-permute-start(f32[3,18,34,1]{2,3,1,0:T(1,128)S(1)} %copy.34), channel_id=1, source_target_pairs={{0,1},{1,2},{2,3},{3,4},{4,5},{5,6},{6,7},{7,8},{8,9},{9,10},{10,1... | collective-permute-start | bytes 22040 | tf_op jit(solution)/shard_map/ppermute | solution.py:27
  40.6 3.1 %copy-start = (f32[3,16,32,128]{3,2,1,0:T(8,128)S(1)}, f32[3,16,32,128]{3,2,1,0:T(8,128)}, u32[]{:S(2)}) copy-start(f32[3,16,32,128]{3,2,1,0:T(8,128)} %param.14) | copy-start | bytes 2359300
  40.6 3.0 %copy-start.8 = (f32[3]{0:T(128)S(1)}, f32[3]{0:T(128)}, u32[]{:S(2)}) copy-start(f32[3]{0:T(128)} %constant.83) | copy-start | bytes 40
  40.7 3.0 %copy-start.9 = (f32[3]{0:T(128)S(1)}, f32[3]{0:T(128)}, u32[]{:S(2)}) copy-start(f32[3]{0:T(128)} %constant.85) | copy-start | bytes 40
  40.7 3.0 %copy-start.10 = (f32[3]{0:T(128)S(1)}, f32[3]{0:T(128)}, u32[]{:S(2)}) copy-start(f32[3]{0:T(128)} %constant.87) | copy-start | bytes 40
  48.2 26.7 %copy-start.7 = (s32[4096]{0:T(1024)S(1)}, s32[4096]{0:T(1024)}, u32[]{:S(2)}) copy-start(s32[4096]{0:T(1024)} %param.17) | copy-start | bytes 49156
  48.2 22.2 %collective-permute-start.6 = (f32[3,1,32,128]{3,2,1,0:T(8,128)S(1)}, f32[3,1,32,128]{3,2,1,0:T(8,128)S(1)}, u32[]{:S(2)}, u32[]{:S(2)}) collective-permute-start(f32[3,1,32,128]{3,2,1,0:T(8,128)S(1)} %get-tuple-element.86), channel_id=1, source_target_pairs={{128,0},{256,128},{384,256},{512,384},{640,512},{768,640},{896,768... | collective-permute-start | bytes 147464 | tf_op jit(solution)/shard_map/ppermute | solution.py:28
  50.2 20.3 %collective-permute-start.7 = (f32[3,1,32,128]{3,2,1,0:T(8,128)S(1)}, f32[3,1,32,128]{3,2,1,0:T(8,128)S(1)}, u32[]{:S(2)}, u32[]{:S(2)}) collective-permute-start(f32[3,1,32,128]{3,2,1,0:T(8,128)S(1)} %get-tuple-element.85), channel_id=1, source_target_pairs={{0,128},{128,256},{256,384},{384,512},{512,640},{640,768},{768,896... | collective-permute-start | bytes 147464 | tf_op jit(solution)/shard_map/ppermute | solution.py:27
  70.5 4.4 %collective-permute-start.8 = (f32[3,18,1,128]{3,2,1,0:T(1,128)S(1)}, f32[3,18,1,128]{3,2,1,0:T(1,128)S(1)}, u32[]{:S(2)}, u32[]{:S(2)}) collective-permute-start(f32[3,18,1,128]{3,2,1,0:T(1,128)S(1)} %get-tuple-element.80), channel_id=1, source_target_pairs={{16,0},{32,16},{48,32},{64,48},{80,64},{96,80},{112,96},{17,1},{33... | collective-permute-start | bytes 82952 | tf_op jit(solution)/shard_map/ppermute | solution.py:28
  72.5 5.2 %collective-permute-start.9 = (f32[3,18,1,128]{3,2,1,0:T(1,128)S(1)}, f32[3,18,1,128]{3,2,1,0:T(1,128)S(1)}, u32[]{:S(2)}, u32[]{:S(2)}) collective-permute-start(f32[3,18,1,128]{3,2,1,0:T(1,128)S(1)} %get-tuple-element.79), channel_id=1, source_target_pairs={{0,16},{16,32},{32,48},{48,64},{64,80},{80,96},{96,112},{1,17},{17... | collective-permute-start | bytes 82952 | tf_op jit(solution)/shard_map/ppermute | solution.py:27
  80.9 12.2 %collective-permute-start.10 = (f32[3,18,34,1]{2,3,1,0:T(1,128)S(1)}, f32[3,18,34,1]{2,3,1,0:T(1,128)S(1)}, u32[]{:S(2)}, u32[]{:S(2)}) collective-permute-start(f32[3,18,34,1]{2,3,1,0:T(1,128)S(1)} %copy.36), channel_id=1, source_target_pairs={{1,0},{2,1},{3,2},{4,3},{5,4},{6,5},{7,6},{8,7},{9,8},{10,9},{11,1... | collective-permute-start | bytes 22040 | tf_op jit(solution)/shard_map/ppermute | solution.py:28
  82.6 11.9 %collective-permute-start.11 = (f32[3,18,34,1]{2,3,1,0:T(1,128)S(1)}, f32[3,18,34,1]{2,3,1,0:T(1,128)S(1)}, u32[]{:S(2)}, u32[]{:S(2)}) collective-permute-start(f32[3,18,34,1]{2,3,1,0:T(1,128)S(1)} %copy.38), channel_id=1, source_target_pairs={{0,1},{1,2},{2,3},{3,4},{4,5},{5,6},{6,7},{7,8},{8,9},{9,10},{10,1... | collective-permute-start | bytes 22040 | tf_op jit(solution)/shard_map/ppermute | solution.py:27
  100.6 11.2 %collective-permute-start.12 = (f32[3,1,32,128]{3,2,1,0:T(8,128)S(1)}, f32[3,1,32,128]{3,2,1,0:T(8,128)S(1)}, u32[]{:S(2)}, u32[]{:S(2)}) collective-permute-start(f32[3,1,32,128]{3,2,1,0:T(8,128)S(1)} %get-tuple-element.84), channel_id=1, source_target_pairs={{128,0},{256,128},{384,256},{512,384},{640,512},{768,640},{896,768... | collective-permute-start | bytes 147464 | tf_op jit(solution)/shard_map/ppermute | solution.py:28
  109.8 7.2 %collective-permute-start.13 = (f32[3,1,32,128]{3,2,1,0:T(8,128)S(1)}, f32[3,1,32,128]{3,2,1,0:T(8,128)S(1)}, u32[]{:S(2)}, u32[]{:S(2)}) collective-permute-start(f32[3,1,32,128]{3,2,1,0:T(8,128)S(1)} %get-tuple-element.83), channel_id=1, source_target_pairs={{0,128},{128,256},{256,384},{384,512},{512,640},{640,768},{768,896... | collective-permute-start | bytes 147464 | tf_op jit(solution)/shard_map/ppermute | solution.py:27
  117.1 4.4 %collective-permute-start.14 = (f32[3,18,1,128]{3,2,1,0:T(1,128)S(1)}, f32[3,18,1,128]{3,2,1,0:T(1,128)S(1)}, u32[]{:S(2)}, u32[]{:S(2)}) collective-permute-start(f32[3,18,1,128]{3,2,1,0:T(1,128)S(1)} %get-tuple-element.78), channel_id=1, source_target_pairs={{16,0},{32,16},{48,32},{64,48},{80,64},{96,80},{112,96},{17,1},{33... | collective-permute-start | bytes 82952 | tf_op jit(solution)/shard_map/ppermute | solution.py:28
  119.0 5.2 %collective-permute-start.15 = (f32[3,18,1,128]{3,2,1,0:T(1,128)S(1)}, f32[3,18,1,128]{3,2,1,0:T(1,128)S(1)}, u32[]{:S(2)}, u32[]{:S(2)}) collective-permute-start(f32[3,18,1,128]{3,2,1,0:T(1,128)S(1)} %get-tuple-element.77), channel_id=1, source_target_pairs={{0,16},{16,32},{32,48},{48,64},{64,80},{80,96},{96,112},{1,17},{17... | collective-permute-start | bytes 82952 | tf_op jit(solution)/shard_map/ppermute | solution.py:27
  127.8 11.7 %collective-permute-start.16 = (f32[3,18,34,1]{2,3,1,0:T(1,128)S(1)}, f32[3,18,34,1]{2,3,1,0:T(1,128)S(1)}, u32[]{:S(2)}, u32[]{:S(2)}) collective-permute-start(f32[3,18,34,1]{2,3,1,0:T(1,128)S(1)} %copy.40), channel_id=1, source_target_pairs={{1,0},{2,1},{3,2},{4,3},{5,4},{6,5},{7,6},{8,7},{9,8},{10,9},{11,1... | collective-permute-start | bytes 22040 | tf_op jit(solution)/shard_map/ppermute | solution.py:28
  130.8 10.2 %collective-permute-start.17 = (f32[3,18,34,1]{2,3,1,0:T(1,128)S(1)}, f32[3,18,34,1]{2,3,1,0:T(1,128)S(1)}, u32[]{:S(2)}, u32[]{:S(2)}) collective-permute-start(f32[3,18,34,1]{2,3,1,0:T(1,128)S(1)} %copy.42), channel_id=1, source_target_pairs={{0,1},{1,2},{2,3},{3,4},{4,5},{5,6},{6,7},{7,8},{8,9},{9,10},{10,1... | collective-permute-start | bytes 22040 | tf_op jit(solution)/shard_map/ppermute | solution.py:27
  139.5 3.0 %copy-start.3 = (f32[3,16,32,128]{3,2,1,0:T(8,128)S(1)}, f32[3,16,32,128]{3,2,1,0:T(8,128)}, u32[]{:S(2)}) copy-start(f32[3,16,32,128]{3,2,1,0:T(8,128)} %get-tuple-element.64) | copy-start | bytes 2359300
  148.4 7.8 %copy-start.6 = (f32[3,4096]{1,0:T(4,128)S(1)}, f32[3,4096]{1,0:T(4,128)}, u32[]{:S(2)}) copy-start(f32[3,4096]{1,0:T(4,128)} %param.19) | copy-start | bytes 147460
  148.4 7.9 %copy-start.5 = (f32[8,4096]{1,0:T(8,128)S(1)}, f32[8,4096]{1,0:T(8,128)}, u32[]{:S(2)}) copy-start(f32[8,4096]{1,0:T(8,128)} %param.20) | copy-start | bytes 393220
where the time goes:
time: 196 us; the launch traced here: 195 us
  starting transfers between devices  65.6 us (33%)
  other arithmetic  38.7 us (20%)
  blocking collectives  34.1 us (17%)
  local copies, waits for them, and re-layouts  26.8 us (14%)
  waiting for transfers between devices  17.2 us (9%)
  matrix products  10.9 us (6%)
    ppermute x9, starting transfers between devices, with_halo(): before = lax.ppermute(last, axis, up)  42.4 us
    all_to_all x1, blocking collectives, body(): lax.all_to_all(buffer, 'chord', split_axis=1, concat_axis=1, tiled=True)  34.1 us
    ppermute x9, starting transfers between devices, with_halo(): after = lax.ppermute(leading, axis, down)  23.3 us
    ppermute x9, waiting for transfers between devices, with_halo(): before = lax.ppermute(last, axis, up)  17.1 us
    reduce_sum x8, other arithmetic, earlier_equal(): return jnp.sum(matching.astype(jnp.int32), axis=1)  15.6 us
    slice x6, local copies, waits for them, and re-layouts, with_halo(): leading = lax.slice_in_dim(x, 0, width, axis=dim)  10 us
    mul x3, other arithmetic, body(): product = stiffness[None] * adjoint  9.11 us
    dot_general x1, matrix products, pick_traction(): jnp.dot(plane_onehot, plane_major, precision=lax.Precision.HIGHEST, prefe...  7.8 us
  transfers between devices with their start and end apart: 18, of which 6 were waited for; matrix products, arithmetic and copies ran while one was open for 13% of the time, Pallas kernels for 0%

commit v1 on v0

v1 whole, which is shorter than its diff:
```python
import functools

import jax
import jax.numpy as jnp
from jax import lax
from jax.experimental import pallas as pl
from jax.experimental.pallas import tpu as pltpu
from jax.sharding import PartitionSpec as P

CX, CY, CZ = 16, 32, 128
PATCH_DEV = 128
MODES = 8
CHORD = 16
WALL = 4096

MASS_SHIFT = 0.5
RELAXATION = 0.8
DIAGONAL_SUM = 10.5
LAME_WEIGHTS = ((3.0, 1.0, 1.0), (1.0, 3.0, 1.0), (1.0, 1.0, 3.0))

STEP = RELAXATION / DIAGONAL_SUM
OWN = 1.0 - STEP * (MASS_SHIFT + 2.0 * sum(LAME_WEIGHTS[0]))
PULL = tuple(tuple(STEP * weight for weight in row) for row in LAME_WEIGHTS)

GX, GY = 24, 48
LANES = 120
ROWS = 512

VMEM = pl.BlockSpec(memory_space=pltpu.VMEM)
SMEM = pl.BlockSpec(memory_space=pltpu.SMEM)


def iota(shape, dim):
    return lax.broadcasted_iota(jnp.int32, shape, dim)


def shifted_lanes(v):
    lane = iota(v.shape, v.ndim - 1)
    before = jnp.where(lane == 0, 0.0, pltpu.roll(v, 1, v.ndim - 1))
    after = jnp.where(lane == CZ - 1, 0.0, pltpu.roll(v, CZ - 1, v.ndim - 1))
    return before + after


def pick(table, classes):
    low, mid, high = (classes & 1) == 1, (classes & 2) == 2, (classes & 4) == 4
    pairs = [jnp.where(low, table[2 * i + 1], table[2 * i]) for i in range(4)]
    return jnp.where(high, jnp.where(mid, pairs[3], pairs[2]), jnp.where(mid, pairs[1], pairs[0]))


def open_sides():
    sides = []
    for axis in ("span", "pitch", "chord"):
        position, size = lax.axis_index(axis), lax.axis_size(axis)
        sides.append(jnp.where(position > 0, 1.0, 0.0).astype(jnp.float32))
        sides.append(jnp.where(position < size - 1, 1.0, 0.0).astype(jnp.float32))
    return sides


def sweep_kernel(
    table, start, source, classes, inner, y_low, y_high, x_out, z_low, z_high, p0, p1, p2, q, cs
):
    x_lo, x_hi, y_lo, y_hi, z_lo, z_hi = open_sides()
    shape = (GY, CZ)
    row, lane = iota(shape, 0), iota(shape, 1)
    keep = jnp.where(row < 8, y_lo, jnp.where(row >= 8 + CY, y_hi, 1.0))
    ends = (lane == 0) | (lane == CZ - 1)
    gate = jnp.where(lane == 0, z_lo, jnp.where(lane == CZ - 1, z_hi, 0.0))
    zeros = jnp.zeros(shape, jnp.float32)

    def clear(ref, planes):
        for c in range(3):
            for x in planes:
                ref[c, x] = zeros

    clear(p0, (2, 3, 20, 21))
    clear(p1, (1, 2, 21, 22))
    clear(p2, (0, 1, 22, 23))
    clear(q, (1, 2, 21, 22))
    clear(cs, (1, 2, 3, 20, 21, 22))

    def column(parts, x):
        total = zeros
        for c in range(3):
            total = total + pltpu.roll(jnp.where(ends, parts[c], 0.0), 2 * c + 1, 1)
        return pltpu.roll(total, 6 * (x - 2), 1)

    def across(ref, c, x):
        here = ref[c, x]
        planes = ref[c, x - 1] + ref[c, x + 1]
        lines = pltpu.roll(here, 1, 0) + pltpu.roll(here, GY - 1, 0)
        side = jnp.where(x < 4, x_lo, jnp.where(x >= 4 + CX, x_hi, 1.0))
        return here, (OWN * here + PULL[c][0] * planes + PULL[c][1] * lines) * (keep * side)

    def load(i, total):
        x = i + 4
        k = pick(table, classes[i])
        parts = []
        for c in range(3):
            for ref, value in ((p0, k * start[c, i]), (cs, STEP * source[c, i])):
                ref[c, x, 0:8, :] = jnp.zeros((8, CZ), jnp.float32)
                ref[c, x, 8 : 8 + CY, :] = value
                ref[c, x, 8 + CY : GY, :] = jnp.zeros((8, CZ), jnp.float32)
            parts.append(p0[c, x])
        return total + column(parts, x)

    col0 = lax.fori_loop(0, CX, load, zeros)

    def first(x, total):
        parts = []
        for c in range(3):
            here, flat = across(p0, c, x)
            new = flat + PULL[c][2] * shifted_lanes(here) + cs[c, x]
            p1[c, x] = new
            q[c, x] = flat + new
            parts.append(new)
        return total + column(parts, x)

    col1 = lax.fori_loop(3, 21, first, zeros)

    def second(x, total):
        parts = []
        for c in range(3):
            here, flat = across(p1, c, x)
            new = flat + PULL[c][2] * shifted_lanes(here) + cs[c, x]
            new = new + (PULL[c][2] * PULL[c][2] * gate) * p0[c, x]
            p2[c, x] = new
            parts.append(new)
        return total + column(parts, x)

    col2 = lax.fori_loop(2, 22, second, zeros)

    plane = (lane * 43) >> 8
    component = ((lane - 6 * plane) >> 1)
    lower = (lane & 1) == 1
    pull = [jnp.where(component == d, PULL[d][d], PULL[d][(d + 1) % 3]) for d in range(3)]
    side = jnp.where(plane < 2, x_lo, jnp.where(plane >= 2 + CX, x_hi, 1.0))
    side = jnp.where(lane < LANES, side, 0.0) * keep
    inside = jnp.where(lower, z_lo, z_hi)

    def flat_columns(v):
        planes = pltpu.roll(v, 6, 1) + pltpu.roll(v, CZ - 6, 1)
        lines = pltpu.roll(v, 1, 0) + pltpu.roll(v, GY - 1, 0)
        return (OWN * v + pull[0] * planes + pull[1] * lines) * side

    t1 = flat_columns(col0)
    out1 = inside * pull[2] * (
        flat_columns(t1) + flat_columns(col1) + col2 + pull[2] * pull[2] * col0
    )
    out2 = inside * pull[2] * pull[2] * (2.0 * t1 + col1)
    out3 = inside * pull[2] * pull[2] * pull[2] * col0
    z_low[0:GY, :] = jnp.where(lower, out1, pltpu.roll(out2, CZ - 1, 1))
    z_high[0:GY, :] = jnp.where(lower, pltpu.roll(out2, 1, 1), out1)
    near, far = out3[8:24, :], out3[24:40, :]
    half = lower[8:24, :]
    z_low[GY : GY + 16, :] = jnp.where(half, near, pltpu.roll(far, CZ - 1, 1))
    z_high[GY : GY + 16, :] = jnp.where(half, pltpu.roll(far, 1, 1), near)

    def third(x):
        values = []
        for c in range(3):
            here, flat = across(p2, c, x)
            new = flat + PULL[c][2] * shifted_lanes(here) + cs[c, x]
            new = new + (PULL[c][2] * PULL[c][2] * gate) * q[c, x]
            y_low[c, x] = new[0:8, :]
            y_high[c, x] = new[8 + CY : GY, :]
            values.append(new[8 : 8 + CY, :])
        return values

    for i, x in enumerate((1, 2, 3, 20, 21, 22)):
        for c, value in enumerate(third(x)):
            x_out[c, i] = value

    def middle(x, carry):
        for c, value in enumerate(third(x)):
            inner[c, x - 4] = value
        return carry

    lax.fori_loop(4, 20, middle, 0)


def chord_part(z_next, z_prev, c, x, start, size):
    lane = iota((size, CZ), 1)
    base = 6 * (x - 2) + 2 * c
    rows = slice(start, start + size)
    above = pltpu.roll(z_next[rows, :], (126 - base) % CZ, 1)
    below = pltpu.roll(z_prev[rows, :], (-base) % CZ, 1)
    return jnp.where(lane >= 126, above, jnp.where(lane < 2, below, 0.0))


def third_chord_part(z_next, z_prev, c, x, half):
    lane = iota((16, CZ), 1)
    base = 6 * (x - 2) + 2 * c
    above = pltpu.roll(z_next[GY : GY + 16, :], (124 + half - base) % CZ, 1)
    below = pltpu.roll(z_prev[GY : GY + 16, :], (2 - half - base) % CZ, 1)
    return jnp.where(lane == 125, above, jnp.where(lane == 2, below, 0.0))


def pitch_kernel(y_low, y_high, z_next, z_prev, low, high):
    for c in range(3):
        for x in range(1, 23):
            for tile, out, start, first in ((y_low, low, 0, 5), (y_high, high, 40, 0)):
                value = tile[c, x]
                if 2 <= x < 22:
                    value = value + chord_part(z_next, z_prev, c, x, start, 8)
                for j in range(3):
                    out[c, j, x : x + 1, :] = value[first + j : first + j + 1, :]


def pitch_rows(y_next, y_prev, c, x):
    row = iota((8, CZ), 0)
    bottom = jnp.zeros((8, CZ), jnp.float32)
    top = jnp.zeros((8, CZ), jnp.float32)
    for j in range(3):
        bottom = jnp.where(row == j, y_prev[c, j, x : x + 1, :], bottom)
        top = jnp.where(row == 5 + j, y_next[c, j, x : x + 1, :], top)
    return bottom, top


def span_kernel(x_out, z_next, z_prev, y_next, y_prev, low, high):
    for c in range(3):
        for i, x in enumerate((1, 2, 3, 20, 21, 22)):
            out, j = (low, i) if i < 3 else (high, i - 3)
            value = x_out[c, i]
            if 2 <= x < 22:
                value = value + chord_part(z_next, z_prev, c, x, 8, CY)
            out[c, j] = value
            bottom, top = pitch_rows(y_next, y_prev, c, x)
            out[c, j, 0:8, :] += bottom
            out[c, j, 24:32, :] += top


def wall_kernel(
    inverse, inner, classes, z_next, z_prev, y_next, y_prev, x_next, x_prev,
    wall_cell, patch_owner, wall_normal, mode_shape,
    adjoint, sums, plane_major, field,
):
    for x in range(CX):
        ratio = pick(inverse, classes[x])
        for c in range(3):
            value = inner[c, x] + chord_part(z_next, z_prev, c, x + 4, 8, CY)
            bottom, top = pitch_rows(y_next, y_prev, c, x + 4)
            near = third_chord_part(z_next, z_prev, c, x + 4, 0)
            far = third_chord_part(z_next, z_prev, c, x + 4, 1)
            zeros = jnp.zeros((8, CZ), jnp.float32)
            value = value + jnp.concatenate([near, far], axis=0)
            value = value + jnp.concatenate([bottom, zeros, zeros, top], axis=0)
            if x < 3:
                value = value + x_prev[c, x]
            if x >= CX - 3:
                value = value + x_next[c, x - (CX - 3)]
            adjoint[c, x] = value * ratio
            plane_major[c, CY * x : CY * (x + 1), :] = value

    for c in range(3):
        for g in range(4):
            block = plane_major[c, 128 * g : 128 * (g + 1), :].T
            first = block.astype(jnp.bfloat16)
            second = (block - first.astype(jnp.float32)).astype(jnp.bfloat16)
            field[256 * c : 256 * c + 128, 128 * g : 128 * (g + 1)] = first
            field[256 * c + 128 : 256 * c + 256, 128 * g : 128 * (g + 1)] = second

    def rows(step, total):
        here = pl.ds(pl.multiple_of(step * ROWS, ROWS), ROWS)
        cell, owner = wall_cell[:, here], patch_owner[:, here]
        planes = (iota((CX * CY, ROWS), 0) == (cell >> 7)).astype(jnp.bfloat16)
        picked = jnp.dot(field[...], planes, preferred_element_type=jnp.float32)
        value = jnp.zeros((CZ, ROWS), jnp.float32)
        for c in range(3):
            part = picked[256 * c : 256 * c + 128] + picked[256 * c + 128 : 256 * c + 256]
            value = value + wall_normal[c : c + 1, here] * part
        value = jnp.where(iota((CZ, ROWS), 0) == (cell & 127), value, 0.0)
        share = mode_shape[:, here] * jnp.sum(value, axis=0, keepdims=True)
        device = owner >> 7
        spread = jnp.concatenate([jnp.where(device == o, share, 0.0) for o in range(CHORD)], axis=0)
        first = spread.astype(jnp.bfloat16)
        second = (spread - first.astype(jnp.float32)).astype(jnp.bfloat16)
        patches = (iota((PATCH_DEV, ROWS), 0) == (owner & 127)).astype(jnp.bfloat16)
        both = jnp.concatenate([first, second], axis=0)
        return total + lax.dot_general(
            both, patches, (((1,), (1,)), ((), ())), preferred_element_type=jnp.float32
        )

    height = CHORD * MODES
    total = lax.fori_loop(0, WALL // ROWS, rows, jnp.zeros((2 * height, PATCH_DEV), jnp.float32))
    sums[...] = total[0:height] + total[height : 2 * height]


def call(kernel, outs, operands, scratch=(), smem=0, flops=0):
    shapes = tuple(jax.ShapeDtypeStruct(shape, jnp.float32) for shape in outs)
    moved = sum(4 * o.size for o in operands) + sum(4 * s.size for s in shapes)
    return pl.pallas_call(
        kernel,
        out_shape=shapes,
        in_specs=[SMEM] * smem + [VMEM] * (len(operands) - smem),
        out_specs=tuple(VMEM for _ in outs),
        scratch_shapes=list(scratch),
        cost_estimate=pl.CostEstimate(flops=flops, bytes_accessed=moved, transcendentals=0),
        compiler_params=pltpu.CompilerParams(vmem_limit_bytes=40 << 20),
    )(*operands)


def swap(low, high, axis):
    size = lax.axis_size(axis)
    up = [(i, i + 1) for i in range(size - 1)]
    down = [(j, i) for i, j in up]
    return lax.ppermute(low, axis, down), lax.ppermute(high, axis, up)


def body(
    adjoint_start,
    sensitivity_source,
    stiffness_class,
    stiffness_table,
    wall_cell,
    patch_owner,
    wall_normal,
    mode_shape,
):
    grown = pltpu.VMEM((3, GX, GY, CZ), jnp.float32)
    inner, y_low, y_high, x_out, z_low, z_high = call(
        sweep_kernel,
        ((3, CX, CY, CZ), (3, GX, 8, CZ), (3, GX, 8, CZ), (3, 6, CY, CZ), (GY + 16, CZ), (GY + 16, CZ)),
        (stiffness_table, adjoint_start, sensitivity_source, stiffness_class),
        scratch=(grown,) * 5,
        smem=1,
    )
    z_next, z_prev = swap(z_low, z_high, "chord")
    low, high = call(
        pitch_kernel, ((3, 3, GX, CZ), (3, 3, GX, CZ)), (y_low, y_high, z_next, z_prev)
    )
    y_next, y_prev = swap(low, high, "pitch")
    low, high = call(
        span_kernel, ((3, 3, CY, CZ), (3, 3, CY, CZ)), (x_out, z_next, z_prev, y_next, y_prev)
    )
    x_next, x_prev = swap(low, high, "span")
    adjoint, sums = call(
        wall_kernel,
        ((3, CX, CY, CZ), (CHORD * MODES, PATCH_DEV)),
        (
            1.0 / stiffness_table, inner, stiffness_class, z_next, z_prev, y_next, y_prev, x_next,
            x_prev, wall_cell.reshape(1, WALL), patch_owner.reshape(1, WALL), wall_normal, mode_shape,
        ),
        scratch=(
            pltpu.VMEM((3, CX * CY, CZ), jnp.float32),
            pltpu.VMEM((6 * CZ, CX * CY), jnp.bfloat16),
        ),
        smem=1,
    )
    sums = sums.reshape(CHORD, MODES, PATCH_DEV)
    arrived = lax.all_to_all(sums, "chord", split_axis=0, concat_axis=0, tiled=True)
    return adjoint, arrived.sum(axis=0)


def solution(mesh):
    in_specs = (
        P(None, "span", "pitch", "chord"),
        P(None, "span", "pitch", "chord"),
        P("span", "pitch", "chord"),
        P(),
        P(("span", "pitch", "chord")),
        P(("span", "pitch", "chord"), None),
        P(None, ("span", "pitch", "chord")),
        P(None, ("span", "pitch", "chord")),
    )
    out_specs = (P(None, "span", "pitch", "chord"), P(None, ("span", "pitch", "chord")))
    return jax.shard_map(body, mesh=mesh, in_specs=in_specs, out_specs=out_specs, check_vma=False)
```

time: 196 us -> 94.9 us (0.48)
  starting transfers between devices: 65.6 us -> 19.9 us
  other arithmetic: 38.7 us -> 0.61 us
  Pallas kernels: 0 us -> 24.3 us
  local copies, waits for them, and re-layouts: 26.8 us -> 3.89 us
  matrix products: 10.9 us -> 0 us
  waiting for transfers between devices: 17.2 us -> 10 us
    ppermute x18 -> x6, starting transfers between devices: 65.6 us -> 19.9 us  [swap(): return (lax.ppermute(low, axis, down), lax.ppermute(high, axis, up))]
    pallas_call x0 -> x4, Pallas kernels: none -> 24.3 us  [call(): pl.pallas_call(kernel, out_shape=shapes, in_specs=[SMEM] * smem + [VMEM]...]
    mul x6 -> x0, other arithmetic: 19.9 us -> none  [the longest x3 9.11 us: body(): product = stiffness[None] * adjoint]
    reduce_sum x11 -> x1, other arithmetic: 15.8 us -> 0.61 us  [body(): return (adjoint, arrived.sum(axis=0))]
    slice x13 -> x0, local copies, waits for them, and re-layouts: 14.3 us -> none  [the longest x6 10 us: with_halo(): leading = lax.slice_in_dim(x, 0, width, axis=dim)]
    dot_general x2 -> x0, matrix products: 10.9 us -> none  [the longest x1 7.8 us: pick_traction(): jnp.dot(plane_onehot, plane_major, precision=lax.Precision.HIGHEST, prefe...]
    ppermute x6 -> x0, local copies, waits for them, and re-layouts: 8.99 us -> none  [the longest x3 4.53 us: with_halo(): before = lax.ppermute(last, axis, up)]
    ppermute x18 -> x6, waiting for transfers between devices: 17.2 us -> 10 us  [swap(): return (lax.ppermute(low, axis, down), lax.ppermute(high, axis, up))]
  transfers between devices with their start and end apart: 18 -> 6, of which waited for: 6 -> 4; matrix products, arithmetic and copies ran while one was open for 13% -> 0% of each run, Pallas kernels for 0% -> 0%
where the time goes in v1:
time: 94.9 us; the launch traced here: 94.5 us
  blocking collectives  34.9 us (37%)
  Pallas kernels  24.3 us (26%)
  starting transfers between devices  19.9 us (21%)
  waiting for transfers between devices  10 us (11%)
  local copies, waits for them, and re-layouts  3.89 us (4%)
    all_to_all x1, blocking collectives, body(): lax.all_to_all(sums, 'chord', split_axis=0, concat_axis=0, tiled=True)  34.9 us
    pallas_call x4, Pallas kernels, call(): pl.pallas_call(kernel, out_shape=shapes, in_specs=[SMEM] * smem + [VMEM]...  24.3 us
    ppermute x6, starting transfers between devices, swap(): return (lax.ppermute(low, axis, down), lax.ppermute(high, axis, up))  19.9 us
    ppermute x6, waiting for transfers between devices, swap(): return (lax.ppermute(low, axis, down), lax.ppermute(high, axis, up))  10 us
    unnamed x18, local copies, waits for them, and re-layouts  3.89 us
  transfers between devices with their start and end apart: 6, of which 4 were waited for; matrix products, arithmetic and copies ran while one was open for 0% of the time, Pallas kernels for 0%

profile of v1, /device:TPU:24, one launch (start us, length us, event | category | flops | bytes accessed | tf_op | source)
XLA Modules:
  0.0 94.5 jit_solution(6625040680046170352)
XLA Ops:
  0.6 0.0 copy-start
  0.6 0.9 copy-done
  1.6 0.0 copy-start.2
  1.6 1.1 %copy-done.2 = f32[3,16,32,128]{3,2,1,0:T(8,128)S(1)} copy-done((f32[3,16,32,128]{3,2,1,0:T(8,128)S(1)}, f32[3,16,32,128]{3,2,1,0:T(8,128)}, u32[]{:S(2)}) %copy-start.2) | copy-done | bytes 786456
  2.7 0.0 copy-start.3
  2.7 1.1 %copy-done.3 = f32[3,16,32,128]{3,2,1,0:T(8,128)S(1)} copy-done((f32[3,16,32,128]{3,2,1,0:T(8,128)S(1)}, f32[3,16,32,128]{3,2,1,0:T(8,128)}, u32[]{:S(2)}) %copy-start.3) | copy-done | bytes 786456
  3.9 0.0 copy-start.8
  3.9 0.7 copy-done.8
  4.5 15.0 %shard_map.95 = (f32[3,16,32,128]{3,2,1,0:T(8,128)S(1)}, f32[3,24,8,128]{3,2,1,0:T(8,128)S(1)}, f32[3,24,8,128]{3,2,1,0:T(8,128)S(1)}, f32[3,6,32,128]{3,2,1,0:T...) custom-call(f32[8]{0:T(128)S(1)} %copy-done.8, f32[3,16,32,128]{3,2,1,0:T(8,128)S(1)} %copy-done.2, ...), custom_call_target="tpu_custom_call" | custom-call | bytes 3571744 | tf_op jit(solution)/shard_map/pallas_call | solution.py:291
  19.5 1.3 %collective-permute-start = (f32[64,128]{1,0:T(8,128)S(1)}, f32[64,128]{1,0:T(8,128)S(1)}, u32[]{:S(2)}, u32[]{:S(2)}) collective-permute-start(f32[64,128]{1,0:T(8,128)S(1)} %get-tuple-element.15), channel_id=1, source_target_pairs={{1,0},{2,1},{3,2},{4,3},{5,4},{6,5},{7,6},{8,7},{9,8},{10,9},{11,1... | collective-permute-start | bytes 98312 | tf_op jit(solution)/shard_map/ppermute | solution.py:306
  20.8 8.5 %collective-permute-start.1 = (f32[64,128]{1,0:T(8,128)S(1)}, f32[64,128]{1,0:T(8,128)S(1)}, u32[]{:S(2)}, u32[]{:S(2)}) collective-permute-start(f32[64,128]{1,0:T(8,128)S(1)} %get-tuple-element.16), channel_id=1, source_target_pairs={{0,1},{1,2},{2,3},{3,4},{4,5},{5,6},{6,7},{7,8},{8,9},{9,10},{10,1... | collective-permute-start | bytes 98312 | tf_op jit(solution)/shard_map/ppermute | solution.py:306
  29.3 0.0 collective-permute-done.z_next
  29.3 1.6 %collective-permute-done.1.z_prev = f32[64,128]{1,0:T(8,128)S(1)} collective-permute-done((f32[64,128]{1,0:T(8,128)S(1)}, f32[64,128]{1,0:T(8,128)S(1)}, u32[]{:S(2)}, u32[]{:S(2)}) %collective-permute-start.1) | collective-permute-done | bytes 32800 | tf_op jit(solution)/shard_map/ppermute | solution.py:306
  30.8 0.3 shard_map.96
  31.2 1.9 %collective-permute-start.2 = (f32[3,3,24,128]{3,2,1,0:T(8,128)S(1)}, f32[3,3,24,128]{3,2,1,0:T(8,128)S(1)}, u32[]{:S(2)}, u32[]{:S(2)}) collective-permute-start(f32[3,3,24,128]{3,2,1,0:T(8,128)S(1)} %get-tuple-element.19), channel_id=1, source_target_pairs={{16,0},{32,16},{48,32},{64,48},{80,64},{96,80},{112,96},{17,1},{33... | collective-permute-start | bytes 331784 | tf_op jit(solution)/shard_map/ppermute | solution.py:306
  33.1 2.4 %collective-permute-start.3 = (f32[3,3,24,128]{3,2,1,0:T(8,128)S(1)}, f32[3,3,24,128]{3,2,1,0:T(8,128)S(1)}, u32[]{:S(2)}, u32[]{:S(2)}) collective-permute-start(f32[3,3,24,128]{3,2,1,0:T(8,128)S(1)} %get-tuple-element.20), channel_id=1, source_target_pairs={{0,16},{16,32},{32,48},{48,64},{64,80},{80,96},{96,112},{1,17},{17... | collective-permute-start | bytes 331784 | tf_op jit(solution)/shard_map/ppermute | solution.py:306
  35.5 0.0 collective-permute-done.2.y_next
  35.5 3.6 %collective-permute-done.3.y_prev = f32[3,3,24,128]{3,2,1,0:T(8,128)S(1)} collective-permute-done((f32[3,3,24,128]{3,2,1,0:T(8,128)S(1)}, f32[3,3,24,128]{3,2,1,0:T(8,128)S(1)}, u32[]{:S(2)}, u32[]{:S(2)}) %collective-permute-start.3) | collective-permute-done | bytes 110624 | tf_op jit(solution)/shard_map/ppermute | solution.py:306
  39.2 0.0 copy-start.7
  39.2 0.2 shard_map.97
  39.4 2.4 %collective-permute-start.4 = (f32[3,3,32,128]{3,2,1,0:T(8,128)S(1)}, f32[3,3,32,128]{3,2,1,0:T(8,128)S(1)}, u32[]{:S(2)}, u32[]{:S(2)}) collective-permute-start(f32[3,3,32,128]{3,2,1,0:T(8,128)S(1)} %get-tuple-element.22), channel_id=1, source_target_pairs={{128,0},{256,128},{384,256},{512,384},{640,512},{768,640},{896,768... | collective-permute-start | bytes 442376 | tf_op jit(solution)/shard_map/ppermute | solution.py:306
  41.8 3.4 %collective-permute-start.5 = (f32[3,3,32,128]{3,2,1,0:T(8,128)S(1)}, f32[3,3,32,128]{3,2,1,0:T(8,128)S(1)}, u32[]{:S(2)}, u32[]{:S(2)}) collective-permute-start(f32[3,3,32,128]{3,2,1,0:T(8,128)S(1)} %get-tuple-element.23), channel_id=1, source_target_pairs={{0,128},{128,256},{256,384},{384,512},{512,640},{640,768},{768,896... | collective-permute-start | bytes 442376 | tf_op jit(solution)/shard_map/ppermute | solution.py:306
  45.2 1.3 %collective-permute-done.4.x_next = f32[3,3,32,128]{3,2,1,0:T(8,128)S(1)} collective-permute-done((f32[3,3,32,128]{3,2,1,0:T(8,128)S(1)}, f32[3,3,32,128]{3,2,1,0:T(8,128)S(1)}, u32[]{:S(2)}, u32[]{:S(2)}) %collective-permute-start.4) | collective-permute-done | bytes 147488 | tf_op jit(solution)/shard_map/ppermute | solution.py:306
  46.5 3.5 %collective-permute-done.5.x_prev = f32[3,3,32,128]{3,2,1,0:T(8,128)S(1)} collective-permute-done((f32[3,3,32,128]{3,2,1,0:T(8,128)S(1)}, f32[3,3,32,128]{3,2,1,0:T(8,128)S(1)}, u32[]{:S(2)}, u32[]{:S(2)}) %collective-permute-start.5) | collective-permute-done | bytes 147488 | tf_op jit(solution)/shard_map/ppermute | solution.py:306
  50.0 0.0 copy-done.1
  50.1 0.0 copy-done.4
  50.1 0.0 copy-done.5
  50.1 0.0 copy-done.6
  50.1 0.0 copy-done.7
  50.1 8.9 %shard_map.98 = (f32[3,16,32,128]{3,2,1,0:T(8,128)}, f32[128,128]{1,0:T(8,128)S(1)}) custom-call(f32[8]{0:T(128)S(1)} %broadcast_divide_fusion.inverse, f32[3,16,32,128]{3,2,1,0:T(8,128)S(1)} %get-tuple-element.14.inner, s32[16,32,128]{2,1,0:T(8,128)S(1)} %copy-done.1, f32[64,128]{1,0:T(8,128)S(1)} %collective-permute-done.z_next, ...), custom_call_target="tpu_custom_call" | custom-call | bytes 2695200 | tf_op jit(solution)/shard_map/pallas_call | solution.py:291
  58.9 34.9 %all_to_all.5 = f32[16,8,128]{2,1,0:T(8,128)S(1)} all-to-all(f32[16,8,128]{2,1,0:T(8,128)S(1)} %bitcast.3), channel_id=1, replica_groups=mesh['span'=8,'pitch'=8,'chord'=16] {'chord'}, dimensions={0} | all-to-all | bytes 131072 | tf_op jit(solution)/shard_map/all_to_all | solution.py:350
  93.9 0.6 reduce_sum.9
  (5 shorter events, 0.0 us)
Async XLA Ops:
  0.6 1.0 %copy-start = (s32[16,32,128]{2,1,0:T(8,128)S(1)}, s32[16,32,128]{2,1,0:T(8,128)}, u32[]{:S(2)}) copy-start(s32[16,32,128]{2,1,0:T(8,128)} %classes.3) | copy-start | bytes 786436
  1.6 1.1 %copy-start.2 = (f32[3,16,32,128]{3,2,1,0:T(8,128)S(1)}, f32[3,16,32,128]{3,2,1,0:T(8,128)}, u32[]{:S(2)}) copy-start(f32[3,16,32,128]{3,2,1,0:T(8,128)} %start.1) | copy-start | bytes 2359300
  2.7 1.1 %copy-start.3 = (f32[3,16,32,128]{3,2,1,0:T(8,128)S(1)}, f32[3,16,32,128]{3,2,1,0:T(8,128)}, u32[]{:S(2)}) copy-start(f32[3,16,32,128]{3,2,1,0:T(8,128)} %source.1) | copy-start | bytes 2359300
  3.9 0.7 copy-start.8
  19.5 9.8 %collective-permute-start = (f32[64,128]{1,0:T(8,128)S(1)}, f32[64,128]{1,0:T(8,128)S(1)}, u32[]{:S(2)}, u32[]{:S(2)}) collective-permute-start(f32[64,128]{1,0:T(8,128)S(1)} %get-tuple-element.15), channel_id=1, source_target_pairs={{1,0},{2,1},{3,2},{4,3},{5,4},{6,5},{7,6},{8,7},{9,8},{10,9},{11,1... | collective-permute-start | bytes 98312 | tf_op jit(solution)/shard_map/ppermute | solution.py:306
  20.8 10.0 %collective-permute-start.1 = (f32[64,128]{1,0:T(8,128)S(1)}, f32[64,128]{1,0:T(8,128)S(1)}, u32[]{:S(2)}, u32[]{:S(2)}) collective-permute-start(f32[64,128]{1,0:T(8,128)S(1)} %get-tuple-element.16), channel_id=1, source_target_pairs={{0,1},{1,2},{2,3},{3,4},{4,5},{5,6},{6,7},{7,8},{8,9},{9,10},{10,1... | collective-permute-start | bytes 98312 | tf_op jit(solution)/shard_map/ppermute | solution.py:306
  31.2 4.3 %collective-permute-start.2 = (f32[3,3,24,128]{3,2,1,0:T(8,128)S(1)}, f32[3,3,24,128]{3,2,1,0:T(8,128)S(1)}, u32[]{:S(2)}, u32[]{:S(2)}) collective-permute-start(f32[3,3,24,128]{3,2,1,0:T(8,128)S(1)} %get-tuple-element.19), channel_id=1, source_target_pairs={{16,0},{32,16},{48,32},{64,48},{80,64},{96,80},{112,96},{17,1},{33... | collective-permute-start | bytes 331784 | tf_op jit(solution)/shard_map/ppermute | solution.py:306
  33.1 6.1 %collective-permute-start.3 = (f32[3,3,24,128]{3,2,1,0:T(8,128)S(1)}, f32[3,3,24,128]{3,2,1,0:T(8,128)S(1)}, u32[]{:S(2)}, u32[]{:S(2)}) collective-permute-start(f32[3,3,24,128]{3,2,1,0:T(8,128)S(1)} %get-tuple-element.20), channel_id=1, source_target_pairs={{0,16},{16,32},{32,48},{48,64},{64,80},{80,96},{96,112},{1,17},{17... | collective-permute-start | bytes 331784 | tf_op jit(solution)/shard_map/ppermute | solution.py:306
  39.2 10.9 %copy-start.1 = (s32[16,32,128]{2,1,0:T(8,128)S(1)}, s32[16,32,128]{2,1,0:T(8,128)}, u32[]{:S(2)}) copy-start(s32[16,32,128]{2,1,0:T(8,128)} %classes.3) | copy-start | bytes 786436
  39.2 10.9 %copy-start.4 = (f32[8,4096]{1,0:T(8,128)S(1)}, f32[8,4096]{1,0:T(8,128)}, u32[]{:S(2)}) copy-start(f32[8,4096]{1,0:T(8,128)} %mode_shape.1) | copy-start | bytes 393220
  39.2 10.9 %copy-start.5 = (f32[3,4096]{1,0:T(4,128)S(1)}, f32[3,4096]{1,0:T(4,128)}, u32[]{:S(2)}) copy-start(f32[3,4096]{1,0:T(4,128)} %wall_normal.1) | copy-start | bytes 147460
  39.2 10.9 %copy-start.6 = (s32[4096]{0:T(1024)S(1)}, s32[4096]{0:T(1024)}, u32[]{:S(2)}) copy-start(s32[4096]{0:T(1024)} %param.12) | copy-start | bytes 49156
  39.2 10.9 %copy-start.7 = (s32[4096,1]{0,1:T(1,128)S(1)}, s32[4096,1]{0,1:T(1,128)}, u32[]{:S(2)}) copy-start(s32[4096,1]{0,1:T(1,128)} %param.13) | copy-start | bytes 49156
  39.4 7.1 %collective-permute-start.4 = (f32[3,3,32,128]{3,2,1,0:T(8,128)S(1)}, f32[3,3,32,128]{3,2,1,0:T(8,128)S(1)}, u32[]{:S(2)}, u32[]{:S(2)}) collective-permute-start(f32[3,3,32,128]{3,2,1,0:T(8,128)S(1)} %get-tuple-element.22), channel_id=1, source_target_pairs={{128,0},{256,128},{384,256},{512,384},{640,512},{768,640},{896,768... | collective-permute-start | bytes 442376 | tf_op jit(solution)/shard_map/ppermute | solution.py:306
  41.8 8.2 %collective-permute-start.5 = (f32[3,3,32,128]{3,2,1,0:T(8,128)S(1)}, f32[3,3,32,128]{3,2,1,0:T(8,128)S(1)}, u32[]{:S(2)}, u32[]{:S(2)}) collective-permute-start(f32[3,3,32,128]{3,2,1,0:T(8,128)S(1)} %get-tuple-element.23), channel_id=1, source_target_pairs={{0,128},{128,256},{256,384},{384,512},{512,640},{640,768},{768,896... | collective-permute-start | bytes 442376 | tf_op jit(solution)/shard_map/ppermute | solution.py:306

commit v2 on v1

v2 whole, which is shorter than its diff:
```python
import functools

import jax
import jax.numpy as jnp
from jax import lax
from jax.experimental import pallas as pl
from jax.experimental.pallas import tpu as pltpu
from jax.sharding import PartitionSpec as P

CX, CY, CZ = 16, 32, 128
PATCH_DEV = 128
MODES = 8
CHORD = 16
WALL = 4096

MASS_SHIFT = 0.5
RELAXATION = 0.8
DIAGONAL_SUM = 10.5
LAME_WEIGHTS = ((3.0, 1.0, 1.0), (1.0, 3.0, 1.0), (1.0, 1.0, 3.0))

STEP = RELAXATION / DIAGONAL_SUM
OWN = 1.0 - STEP * (MASS_SHIFT + 2.0 * sum(LAME_WEIGHTS[0]))
PULL = tuple(tuple(STEP * weight for weight in row) for row in LAME_WEIGHTS)

GX, GY = 24, 48
FIRST, MIDDLE, LAST = 6, 24, 42
HALF = MIDDLE - FIRST
ROWS = 2048
STEP_X = 4

VMEM = pl.BlockSpec(memory_space=pltpu.VMEM)
SMEM = pl.BlockSpec(memory_space=pltpu.SMEM)
HBM = pl.BlockSpec(memory_space=pltpu.HBM)


def iota(shape, dim):
    return lax.broadcasted_iota(jnp.int32, shape, dim)


def shifted_lanes(v):
    lane = iota(v.shape, v.ndim - 1)
    before = jnp.where(lane == 0, 0.0, pltpu.roll(v, 1, v.ndim - 1))
    after = jnp.where(lane == CZ - 1, 0.0, pltpu.roll(v, CZ - 1, v.ndim - 1))
    return before + after


def pick(table, classes):
    low, mid, high = (classes & 1) == 1, (classes & 2) == 2, (classes & 4) == 4
    pairs = [jnp.where(low, table[2 * i + 1], table[2 * i]) for i in range(4)]
    return jnp.where(high, jnp.where(mid, pairs[3], pairs[2]), jnp.where(mid, pairs[1], pairs[0]))


def open_sides():
    sides = []
    for axis in ("span", "pitch", "chord"):
        position, size = lax.axis_index(axis), lax.axis_size(axis)
        sides.append(jnp.where(position > 0, 1.0, 0.0).astype(jnp.float32))
        sides.append(jnp.where(position < size - 1, 1.0, 0.0).astype(jnp.float32))
    return sides


def slots(shape):
    lane = iota(shape, len(shape) - 1)
    plane = (lane * 43) >> 8
    return plane, lane - 6 * plane


def column_kernel(
    table_in, start, source, classes, p0, cs, z_low, z_high,
    table, y_in, s_in, c_in, beyond, sems, table_sem,
):
    table_copy = pltpu.make_async_copy(table_in, table, table_sem)
    table_copy.start()
    copies = []
    for g in range(CX // STEP_X):
        part = pl.ds(g * STEP_X, STEP_X)
        copies.append(
            [
                pltpu.make_async_copy(classes.at[part], c_in.at[part], sems.at[0, g]),
                pltpu.make_async_copy(start.at[:, part], y_in.at[:, part], sems.at[1, g]),
                pltpu.make_async_copy(source.at[:, part], s_in.at[:, part], sems.at[2, g]),
            ]
        )
        for copy in copies[-1]:
            copy.start()
    x_lo, x_hi, y_lo, y_hi, z_lo, z_hi = open_sides()

    lane = iota((CY, CZ), 1)
    edge = (lane < 3) | (lane >= CZ - 3)
    values = [jnp.zeros((CY, CZ), jnp.float32) for _ in range(3)]
    pushes = [jnp.zeros((CY, CZ), jnp.float32) for _ in range(3)]
    table_copy.wait()
    for x in range(CX):
        if x % STEP_X == 0:
            for copy in copies[x // STEP_X]:
                copy.wait()
        k = pick(table, c_in[x])
        shift = (6 * (x + 2) + 3) % CZ
        for c in range(3):
            value = k * y_in[c, x]
            push = STEP * s_in[c, x]
            p0[c, x] = value
            cs[c, x] = push
            values[c] = values[c] + pltpu.roll(jnp.where(edge, value, 0.0), shift, 1)
            pushes[c] = pushes[c] + pltpu.roll(jnp.where(edge, push, 0.0), shift, 1)

    shape = (GY, CZ)
    plane, slot = slots(shape)
    row = iota(shape, 0)
    keep = jnp.where(row < 8, y_lo, jnp.where(row >= 8 + CY, y_hi, 1.0))
    side = jnp.where(plane < 2, x_lo, jnp.where(plane >= 2 + CX, x_hi, 1.0))
    side = jnp.where(plane < 20, side, 0.0) * keep
    at_high, at_low = slot == 2, slot == 3
    gate = jnp.where(at_high, z_hi, jnp.where(at_low, z_lo, 0.0))
    no_before, no_after = (slot == 0) | (slot == 3), (slot == 2) | (slot == 5)
    pad = jnp.zeros((8, CZ), jnp.float32)
    _, packed_slot = slots((HALF, CZ))

    for c in range(3):
        along = PULL[c][2]

        def flat(v):
            planes = pltpu.roll(v, 6, 1) + pltpu.roll(v, CZ - 6, 1)
            lines = pltpu.roll(v, 1, 0) + pltpu.roll(v, GY - 1, 0)
            return (OWN * v + PULL[c][0] * planes + PULL[c][1] * lines) * side

        def beside(v):
            before = jnp.where(no_before, 0.0, pltpu.roll(v, 1, 1))
            after = jnp.where(no_after, 0.0, pltpu.roll(v, CZ - 1, 1))
            return along * (before + after)

        v0 = jnp.concatenate([pad, values[c], pad], axis=0)
        push = jnp.concatenate([pad, pushes[c], pad], axis=0)
        t1 = flat(v0)
        v1 = t1 + beside(v0) + push
        t2 = flat(v1)
        v2 = t2 + beside(v1) + push + (along * along) * gate * v0
        out1 = along * gate * (flat(t1) + t2 + v2 + (along * along) * v0)
        out2 = (along * along) * gate * (2.0 * t1 + v1)
        out3 = (along * along * along) * gate * v0
        given = jnp.zeros(shape, jnp.float32)
        for far, out in ((1, out1), (2, out2), (3, out3)):
            given = given + pltpu.roll(jnp.where(at_low, out, 0.0), CZ - far, 1)
            given = given + pltpu.roll(jnp.where(at_high, out, 0.0), far, 1)
        beyond[c] = given
        top, rest = beyond[c, FIRST:MIDDLE, :], beyond[c, MIDDLE:LAST, :]
        rows = slice(HALF * c, HALF * (c + 1))
        z_low[rows, :] = jnp.where(packed_slot < 3, top, pltpu.roll(rest, 3, 1))
        z_high[rows, :] = jnp.where(packed_slot >= 3, rest, pltpu.roll(top, CZ - 3, 1))
    for out in (z_low, z_high):
        out[3 * HALF : 56, :] = jnp.zeros((56 - 3 * HALF, CZ), jnp.float32)


def sweep_kernel(p0_in, cs_in, inner, y_low, y_high, x_out, p0, p1, p2, q, cs):
    x_lo, x_hi, y_lo, y_hi, z_lo, z_hi = open_sides()
    shape = (GY, CZ)
    row, lane = iota(shape, 0), iota(shape, 1)
    keep = jnp.where(row < 8, y_lo, jnp.where(row >= 8 + CY, y_hi, 1.0))
    gate = jnp.where(lane == 0, z_lo, jnp.where(lane == CZ - 1, z_hi, 0.0))
    zeros = jnp.zeros(shape, jnp.float32)

    def clear(ref, planes):
        for c in range(3):
            for x in planes:
                ref[c, x] = zeros

    clear(p0, (2, 3, 20, 21))
    clear(p1, (1, 2, 21, 22))
    clear(p2, (0, 1, 22, 23))
    clear(q, (1, 2, 21, 22))
    clear(cs, (1, 2, 3, 20, 21, 22))
    pad = jnp.zeros((8, CZ), jnp.float32)
    for x in range(CX):
        for c in range(3):
            for ref, given in ((p0, p0_in), (cs, cs_in)):
                ref[c, x + 4, 0:8, :] = pad
                ref[c, x + 4, 8 : 8 + CY, :] = given[c, x]
                ref[c, x + 4, 8 + CY : GY, :] = pad

    def across(ref, c, x):
        here = ref[c, x]
        planes = ref[c, x - 1] + ref[c, x + 1]
        lines = pltpu.roll(here, 1, 0) + pltpu.roll(here, GY - 1, 0)
        side = jnp.where(x < 4, x_lo, jnp.where(x >= 4 + CX, x_hi, 1.0))
        return here, (OWN * here + PULL[c][0] * planes + PULL[c][1] * lines) * (keep * side)

    def first(x, carry):
        for c in range(3):
            here, flat = across(p0, c, x)
            new = flat + PULL[c][2] * shifted_lanes(here) + cs[c, x]
            p1[c, x] = new
            q[c, x] = flat + new
        return carry

    lax.fori_loop(3, 21, first, 0, unroll=True)

    def second(x, carry):
        for c in range(3):
            here, flat = across(p1, c, x)
            new = flat + PULL[c][2] * shifted_lanes(here) + cs[c, x]
            p2[c, x] = new + (PULL[c][2] * PULL[c][2] * gate) * p0[c, x]
        return carry

    lax.fori_loop(2, 22, second, 0, unroll=True)

    def third(x):
        values = []
        for c in range(3):
            here, flat = across(p2, c, x)
            new = flat + PULL[c][2] * shifted_lanes(here) + cs[c, x]
            new = new + (PULL[c][2] * PULL[c][2] * gate) * q[c, x]
            y_low[c, x] = new[0:8, :]
            y_high[c, x] = new[8 + CY : GY, :]
            values.append(new[8 : 8 + CY, :])
        return values

    for i, x in enumerate((1, 2, 3, 20, 21, 22)):
        for c, value in enumerate(third(x)):
            x_out[c, i] = value

    def middle(x, carry):
        for c, value in enumerate(third(x)):
            inner[c, x - 4] = value
        return carry

    lax.fori_loop(4, 20, middle, 0, unroll=True)


def unpack(z_next, z_prev, columns):
    _, slot = slots((HALF, CZ))
    for c in range(3):
        rows = slice(HALF * c, HALF * (c + 1))
        above, below = z_next[rows, :], z_prev[rows, :]
        columns[c, 0:8, :] = jnp.zeros((8, CZ), jnp.float32)
        columns[c, GY - 8 : GY, :] = jnp.zeros((8, CZ), jnp.float32)
        columns[c, FIRST:MIDDLE, :] = jnp.where(slot < 3, above, pltpu.roll(below, 3, 1))
        columns[c, MIDDLE:LAST, :] = jnp.where(slot < 3, pltpu.roll(above, CZ - 3, 1), below)


def chord_part(columns, c, x, start, size):
    lane = iota((size, CZ), 1)
    placed = pltpu.roll(columns[c, start : start + size, :], (CZ - 3 - 6 * (x - 2)) % CZ, 1)
    return jnp.where((lane < 3) | (lane >= CZ - 3), placed, 0.0)


def pitch_kernel(y_low, y_high, z_next, z_prev, low, high, columns):
    unpack(z_next, z_prev, columns)
    for c in range(3):
        for x in range(1, 23):
            for tile, out, start, first in ((y_low, low, 0, 5), (y_high, high, 40, 0)):
                value = tile[c, x]
                if 2 <= x < 22:
                    value = value + chord_part(columns, c, x, start, 8)
                for j in range(3):
                    out[c, j, x : x + 1, :] = value[first + j : first + j + 1, :]


def pitch_rows(y_next, y_prev, c, x):
    row = iota((8, CZ), 0)
    bottom = jnp.zeros((8, CZ), jnp.float32)
    top = jnp.zeros((8, CZ), jnp.float32)
    for j in range(3):
        bottom = jnp.where(row == j, y_prev[c, j, x : x + 1, :], bottom)
        top = jnp.where(row == 5 + j, y_next[c, j, x : x + 1, :], top)
    return bottom, top


def span_kernel(x_out, z_next, z_prev, y_next, y_prev, low, high, columns):
    unpack(z_next, z_prev, columns)
    for c in range(3):
        for i, x in enumerate((1, 2, 3, 20, 21, 22)):
            out, j = (low, i) if i < 3 else (high, i - 3)
            value = x_out[c, i]
            if 2 <= x < 22:
                value = value + chord_part(columns, c, x, 8, CY)
            out[c, j] = value
            bottom, top = pitch_rows(y_next, y_prev, c, x)
            out[c, j, 0:8, :] += bottom
            out[c, j, 24:32, :] += top


def finish_planes(planes, inner, z_next, z_prev, y_next, y_prev, ratio_of, columns, values, part, field, span):
    unpack(z_next, z_prev, columns)
    zeros = jnp.zeros((8, CZ), jnp.float32)
    for i, x in enumerate(planes):
        ratio = ratio_of(x)
        for c in range(3):
            value = inner[c, x] + chord_part(columns, c, x + 4, 8, CY)
            bottom, top = pitch_rows(y_next, y_prev, c, x + 4)
            value = value + jnp.concatenate([bottom, zeros, zeros, top], axis=0)
            value = span(value, c, x)
            values[c, i] = value * ratio
            part[c, CY * i : CY * (i + 1), :] = value
    for c in range(3):
        for g in range(CY * len(planes) // 128):
            block = part[c, 128 * g : 128 * (g + 1), :].T
            first = block.astype(jnp.bfloat16)
            second = (block - first.astype(jnp.float32)).astype(jnp.bfloat16)
            field[256 * c : 256 * c + 128, 128 * g : 128 * (g + 1)] = first
            field[256 * c + 128 : 256 * c + 256, 128 * g : 128 * (g + 1)] = second


def normal_share(field, place, cell, normals):
    count = place.shape[1]
    planes = (iota((field.shape[1], count), 0) == place).astype(jnp.bfloat16)
    picked = jnp.dot(field[...], planes, preferred_element_type=jnp.float32)
    value = jnp.zeros((CZ, count), jnp.float32)
    for c in range(3):
        part = picked[256 * c : 256 * c + 128] + picked[256 * c + 128 : 256 * c + 256]
        value = value + normals[c : c + 1] * part
    value = jnp.where(iota((CZ, count), 0) == (cell & 127), value, 0.0)
    return jnp.sum(value, axis=0, keepdims=True)


def middle_kernel(
    inverse, inner, classes, z_next, z_prev, y_next, y_prev, wall_cell, wall_normal,
    adjoint, share, columns, values, part, field, sem,
):
    def as_is(value, c, x):
        return value

    finish_planes(
        range(4, 12), inner, z_next, z_prev, y_next, y_prev,
        lambda x: pick(inverse, classes[x]), columns, values, part, field, as_is,
    )
    copy = pltpu.make_async_copy(values, adjoint.at[:, 4:12], sem)
    copy.start()
    for step in range(WALL // ROWS):
        here = slice(step * ROWS, (step + 1) * ROWS)
        cell = wall_cell[:, here]
        share[:, here] = normal_share(field, (cell >> 7) - 128, cell, wall_normal[:, here])
    copy.wait()


def wall_kernel(
    inverse, given, inner, classes, z_next, z_prev, y_next, y_prev, x_next, x_prev, share,
    wall_cell, patch_owner, wall_normal, mode_shape,
    adjoint, sums, columns, values, part, field, sems,
):
    def span(value, c, x):
        if x < 3:
            return value + x_prev[c, x]
        if x >= CX - 3:
            return value + x_next[c, x - (CX - 3)]
        return value

    finish_planes(
        (0, 1, 2, 3, 12, 13, 14, 15), inner, z_next, z_prev, y_next, y_prev,
        lambda x: pick(inverse, classes[x]), columns, values, part, field, span,
    )
    copies = [
        pltpu.make_async_copy(values.at[:, 0:4], adjoint.at[:, 0:4], sems.at[0]),
        pltpu.make_async_copy(values.at[:, 4:8], adjoint.at[:, 12:16], sems.at[1]),
    ]
    for copy in copies:
        copy.start()
    height = CHORD * MODES
    total = jnp.zeros((2 * height, PATCH_DEV), jnp.float32)
    for step in range(WALL // ROWS):
        here = slice(step * ROWS, (step + 1) * ROWS)
        cell, owner = wall_cell[:, here], patch_owner[:, here]
        plane = cell >> 7
        place = jnp.where(plane < 128, plane, jnp.where(plane >= 384, plane - 256, -1))
        normal = share[:, here] + normal_share(field, place, cell, wall_normal[:, here])
        parts = mode_shape[:, here] * normal
        device = owner >> 7
        spread = jnp.concatenate([jnp.where(device == o, parts, 0.0) for o in range(CHORD)], axis=0)
        first = spread.astype(jnp.bfloat16)
        second = (spread - first.astype(jnp.float32)).astype(jnp.bfloat16)
        patches = (iota((PATCH_DEV, ROWS), 0) == (owner & 127)).astype(jnp.bfloat16)
        both = jnp.concatenate([first, second], axis=0)
        total = total + lax.dot_general(
            both, patches, (((1,), (1,)), ((), ())), preferred_element_type=jnp.float32
        )
    sums[...] = total[0:height] + total[height : 2 * height]
    for copy in copies:
        copy.wait()


def call(kernel, outs, operands, spaces, scratch=(), out_spaces=None, aliases=None, flops=0):
    spec = {"h": HBM, "s": SMEM, "v": VMEM}
    shapes = tuple(jax.ShapeDtypeStruct(shape, jnp.float32) for shape in outs)
    moved = sum(4 * o.size for o in operands) + sum(4 * s.size for s in shapes)
    operands = [
        pltpu.with_memory_space_constraint(o, pltpu.HBM) if space == "h" else o
        for o, space in zip(operands, spaces)
    ]
    return pl.pallas_call(
        kernel,
        out_shape=shapes,
        in_specs=[spec[space] for space in spaces],
        out_specs=tuple(spec[space] for space in out_spaces or "v" * len(outs)),
        scratch_shapes=list(scratch),
        input_output_aliases=aliases or {},
        cost_estimate=pl.CostEstimate(flops=flops, bytes_accessed=moved, transcendentals=0),
        compiler_params=pltpu.CompilerParams(vmem_limit_bytes=40 << 20),
    )(*operands)


def swap(low, high, axis):
    size = lax.axis_size(axis)
    up = [(i, i + 1) for i in range(size - 1)]
    down = [(j, i) for i, j in up]
    return lax.ppermute(low, axis, down), lax.ppermute(high, axis, up)


def body(
    adjoint_start,
    sensitivity_source,
    stiffness_class,
    stiffness_table,
    wall_cell,
    patch_owner,
    wall_normal,
    mode_shape,
):
    block, columns = (3, CX, CY, CZ), pltpu.VMEM((3, GY, CZ), jnp.float32)
    grown = pltpu.VMEM((3, GX, GY, CZ), jnp.float32)
    p0, cs, z_low, z_high = call(
        column_kernel,
        (block, block, (56, CZ), (56, CZ)),
        (stiffness_table, adjoint_start, sensitivity_source, stiffness_class),
        "hhhh",
        scratch=(
            pltpu.SMEM((8,), jnp.float32),
            pltpu.VMEM(block, jnp.float32),
            pltpu.VMEM(block, jnp.float32),
            pltpu.VMEM((CX, CY, CZ), jnp.int32),
            columns,
            pltpu.SemaphoreType.DMA((3, CX // STEP_X)),
            pltpu.SemaphoreType.DMA,
        ),
    )
    z_next, z_prev = swap(z_low, z_high, "chord")
    inner, y_low, y_high, x_out = call(
        sweep_kernel,
        (block, (3, GX, 8, CZ), (3, GX, 8, CZ), (3, 6, CY, CZ)),
        (p0, cs),
        "vv",
        scratch=(grown,) * 5,
        flops=1 << 25,
    )
    slab = (3, 3, GX, CZ)
    low, high = call(
        pitch_kernel, (slab, slab), (y_low, y_high, z_next, z_prev), "vvvv", scratch=(columns,)
    )
    y_next, y_prev = swap(low, high, "pitch")
    slab = (3, 3, CY, CZ)
    low, high = call(
        span_kernel, (slab, slab), (x_out, z_next, z_prev, y_next, y_prev), "vvvvv", scratch=(columns,)
    )
    x_next, x_prev = swap(low, high, "span")
    inverse, cells = 1.0 / stiffness_table, wall_cell.reshape(1, WALL)
    given = (z_next, z_prev, y_next, y_prev)
    work = (
        columns,
        pltpu.VMEM((3, CX // 2, CY, CZ), jnp.float32),
        pltpu.VMEM((3, CX // 2 * CY, CZ), jnp.float32),
        pltpu.VMEM((6 * CZ, CX // 2 * CY), jnp.bfloat16),
    )
    adjoint, share = call(
        middle_kernel,
        (block, (1, WALL)),
        (inverse, inner, stiffness_class, *given, cells, wall_normal),
        "svvvvvvvv",
        scratch=(*work, pltpu.SemaphoreType.DMA),
        out_spaces="hv",
        flops=1 << 30,
    )
    adjoint, sums = call(
        wall_kernel,
        (block, (CHORD * MODES, PATCH_DEV)),
        (
            inverse, adjoint, inner, stiffness_class, *given, x_next, x_prev, share,
            cells, patch_owner.reshape(1, WALL), wall_normal, mode_shape,
        ),
        "shvvvvvvvvvvvvv",
        scratch=(*work, pltpu.SemaphoreType.DMA((2,))),
        out_spaces="hv",
        aliases={1: 0},
        flops=1 << 30,
    )
    sums = sums.reshape(CHORD, MODES, PATCH_DEV)
    arrived = lax.all_to_all(sums, "chord", split_axis=0, concat_axis=0, tiled=True)
    return adjoint, arrived.sum(axis=0)


def solution(mesh):
    in_specs = (
        P(None, "span", "pitch", "chord"),
        P(None, "span", "pitch", "chord"),
        P("span", "pitch", "chord"),
        P(),
        P(("span", "pitch", "chord")),
        P(("span", "pitch", "chord"), None),
        P(None, ("span", "pitch", "chord")),
        P(None, ("span", "pitch", "chord")),
    )
    out_specs = (P(None, "span", "pitch", "chord"), P(None, ("span", "pitch", "chord")))
    return jax.shard_map(body, mesh=mesh, in_specs=in_specs, out_specs=out_specs, check_vma=False)
```

time: 94.9 us -> 74.7 us (0.79)
  Pallas kernels: 24.3 us -> 13.7 us
  waiting for transfers between devices: 10 us -> 5.14 us
  local copies, waits for them, and re-layouts: 3.89 us -> 0.03 us
    pallas_call x4 -> x6, Pallas kernels: 24.3 us -> 13.7 us  [call(): pl.pallas_call(kernel, out_shape=shapes, in_specs=[spec[space] for space...]
    ppermute x6, waiting for transfers between devices: 10 us -> 5.14 us  [swap(): return (lax.ppermute(low, axis, down), lax.ppermute(high, axis, up))]
    unnamed x18 -> x12, local copies, waits for them, and re-layouts: 3.89 us -> 0.03 us
  transfers between devices with their start and end apart: 6 -> 6, of which waited for: 4 -> 2; matrix products, arithmetic and copies ran while one was open for 0% -> 0% of each run, Pallas kernels for 0% -> 8%
where the time goes in v2:
time: 74.7 us; the launch traced here: 74.4 us
  blocking collectives  34.2 us (46%)
  starting transfers between devices  19.9 us (27%)
  Pallas kernels  13.7 us (18%)
  waiting for transfers between devices  5.14 us (7%)
  between operations  0.82 us (1%)
    all_to_all x1, blocking collectives, body(): lax.all_to_all(sums, 'chord', split_axis=0, concat_axis=0, tiled=True)  34.2 us
    ppermute x6, starting transfers between devices, swap(): return (lax.ppermute(low, axis, down), lax.ppermute(high, axis, up))  19.9 us
    pallas_call x6, Pallas kernels, call(): pl.pallas_call(kernel, out_shape=shapes, in_specs=[spec[space] for space...  13.7 us
    ppermute x6, waiting for transfers between devices, swap(): return (lax.ppermute(low, axis, down), lax.ppermute(high, axis, up))  5.14 us
  transfers between devices with their start and end apart: 6, of which 2 were waited for; matrix products, arithmetic and copies ran while one was open for 0% of the time, Pallas kernels for 8%

profile of v2, /device:TPU:24, one launch (start us, length us, event | category | flops | bytes accessed | tf_op | source)
XLA Modules:
  0.0 74.4 jit_solution(12254875034197315648)
XLA Ops:
  0.6 2.6 %shard_map.95 = (f32[3,16,32,128]{3,2,1,0:T(8,128)S(1)}, f32[3,16,32,128]{3,2,1,0:T(8,128)S(1)}, f32[56,128]{1,0:T(8,128)S(1)}, f32[56,128]{1,0:T(8,128)S(1)}) custom-call(f32[8]{0:T(128)} %table_in.1, f32[3,16,32,128]{3,2,1,0:T(8,128)} %start.1, f32[3,16,32,128]{3,2,1,0:T(8,128)} %source.1, s32[16,32,128]{2,1,0:T(8,128)} %classes.5), custom_call_target="tpu_custom_call" | custom-call | bytes 3465248 | tf_op jit(solution)/shard_map/pallas_call | solution.py:388
  3.2 1.3 %collective-permute-start = (f32[56,128]{1,0:T(8,128)S(1)}, f32[56,128]{1,0:T(8,128)S(1)}, u32[]{:S(2)}, u32[]{:S(2)}) collective-permute-start(f32[56,128]{1,0:T(8,128)S(1)} %get-tuple-element.21), channel_id=1, source_target_pairs={{1,0},{2,1},{3,2},{4,3},{5,4},{6,5},{7,6},{8,7},{9,8},{10,9},{11,1... | collective-permute-start | bytes 86024 | tf_op jit(solution)/shard_map/ppermute | solution.py:404
  4.5 8.5 %collective-permute-start.1 = (f32[56,128]{1,0:T(8,128)S(1)}, f32[56,128]{1,0:T(8,128)S(1)}, u32[]{:S(2)}, u32[]{:S(2)}) collective-permute-start(f32[56,128]{1,0:T(8,128)S(1)} %get-tuple-element.22), channel_id=1, source_target_pairs={{0,1},{1,2},{2,3},{3,4},{4,5},{5,6},{6,7},{7,8},{8,9},{9,10},{10,1... | collective-permute-start | bytes 86024 | tf_op jit(solution)/shard_map/ppermute | solution.py:404
  13.0 2.6 %shard_map.96 = (f32[3,16,32,128]{3,2,1,0:T(8,128)S(1)}, f32[3,24,8,128]{3,2,1,0:T(8,128)S(1)}, f32[3,24,8,128]{3,2,1,0:T(8,128)S(1)}, f32[3,6,32,128]{3,2,1,0:T(8,128)S(1)}) custom-call(f32[3,16,32,128]{3,2,1,0:T(8,128)S(1)} %get-tuple-element.18.p0_in, f32[3,16,32,128]{3,2,1,0:T(8,128)S(1)} %get-tuple-element.19.cs_in), custom_call_target="tpu_custom_call" | custom-call | flops 33554432 | bytes 3244032 | tf_op jit(solution)/shard_map/pallas_call | solution.py:388
  15.6 0.0 collective-permute-done.z_next
  15.6 0.0 collective-permute-done.1.z_prev
  15.7 0.3 shard_map.97
  15.9 1.9 %collective-permute-start.2 = (f32[3,3,24,128]{3,2,1,0:T(8,128)S(1)}, f32[3,3,24,128]{3,2,1,0:T(8,128)S(1)}, u32[]{:S(2)}, u32[]{:S(2)}) collective-permute-start(f32[3,3,24,128]{3,2,1,0:T(8,128)S(1)} %get-tuple-element.25), channel_id=1, source_target_pairs={{16,0},{32,16},{48,32},{64,48},{80,64},{96,80},{112,96},{17,1},{33... | collective-permute-start | bytes 331784 | tf_op jit(solution)/shard_map/ppermute | solution.py:404
  17.9 2.4 %collective-permute-start.3 = (f32[3,3,24,128]{3,2,1,0:T(8,128)S(1)}, f32[3,3,24,128]{3,2,1,0:T(8,128)S(1)}, u32[]{:S(2)}, u32[]{:S(2)}) collective-permute-start(f32[3,3,24,128]{3,2,1,0:T(8,128)S(1)} %get-tuple-element.26), channel_id=1, source_target_pairs={{0,16},{16,32},{32,48},{48,64},{64,80},{80,96},{96,112},{1,17},{17... | collective-permute-start | bytes 331784 | tf_op jit(solution)/shard_map/ppermute | solution.py:404
  20.3 0.0 collective-permute-done.2.y_next
  20.3 3.6 %collective-permute-done.3.y_prev = f32[3,3,24,128]{3,2,1,0:T(8,128)S(1)} collective-permute-done((f32[3,3,24,128]{3,2,1,0:T(8,128)S(1)}, f32[3,3,24,128]{3,2,1,0:T(8,128)S(1)}, u32[]{:S(2)}, u32[]{:S(2)}) %collective-permute-start.3) | collective-permute-done | bytes 110624 | tf_op jit(solution)/shard_map/ppermute | solution.py:404
  23.9 0.0 copy-start
  23.9 0.0 copy-start.2
  23.9 0.0 copy-start.3
  23.9 0.2 shard_map.99
  24.1 0.0 copy-start.5
  24.2 2.4 %collective-permute-start.4 = (f32[3,3,32,128]{3,2,1,0:T(8,128)S(1)}, f32[3,3,32,128]{3,2,1,0:T(8,128)S(1)}, u32[]{:S(2)}, u32[]{:S(2)}) collective-permute-start(f32[3,3,32,128]{3,2,1,0:T(8,128)S(1)} %get-tuple-element.29), channel_id=1, source_target_pairs={{128,0},{256,128},{384,256},{512,384},{640,512},{768,640},{896,768... | collective-permute-start | bytes 442376 | tf_op jit(solution)/shard_map/ppermute | solution.py:404
  26.6 3.4 %collective-permute-start.5 = (f32[3,3,32,128]{3,2,1,0:T(8,128)S(1)}, f32[3,3,32,128]{3,2,1,0:T(8,128)S(1)}, u32[]{:S(2)}, u32[]{:S(2)}) collective-permute-start(f32[3,3,32,128]{3,2,1,0:T(8,128)S(1)} %get-tuple-element.30), channel_id=1, source_target_pairs={{0,128},{128,256},{256,384},{384,512},{512,640},{640,768},{768,896... | collective-permute-start | bytes 442376 | tf_op jit(solution)/shard_map/ppermute | solution.py:404
  30.0 0.0 copy-done.5
  30.0 0.0 copy-done
  30.0 0.0 copy-done.2
  30.1 0.0 copy-done.3
  30.1 0.0 copy-start.1
  30.1 0.0 copy-start.4
  30.1 3.3 %shard_map.98 = (f32[3,16,32,128]{3,2,1,0:T(8,128)}, f32[1,4096]{1,0:T(1,128)S(1)}) custom-call(f32[8]{0:T(128)S(1)} %broadcast_divide_fusion.inverse, f32[3,16,32,128]{3,2,1,0:T(8,128)S(1)} %get-tuple-element.20.inner, s32[16,32,128]{2,1,0:T(8,128)S(1)} %copy-done, f32[56,128]{1,0:T(8,128)S(1)} %collective-permute-done.z_next, ...), custom_call_target="tpu_custom_call" | custom-call | flops 1073741824 | bytes 2195488 | tf_op jit(solution)/shard_map/pallas_call | solution.py:388
  33.4 0.0 collective-permute-done.4.x_next
  33.4 1.5 %collective-permute-done.5.x_prev = f32[3,3,32,128]{3,2,1,0:T(8,128)S(1)} collective-permute-done((f32[3,3,32,128]{3,2,1,0:T(8,128)S(1)}, f32[3,3,32,128]{3,2,1,0:T(8,128)S(1)}, u32[]{:S(2)}, u32[]{:S(2)}) %collective-permute-start.5) | collective-permute-done | bytes 147488 | tf_op jit(solution)/shard_map/ppermute | solution.py:404
  34.9 0.0 copy-done.1
  34.9 0.0 copy-done.4
  34.9 4.8 %shard_map.100 = (f32[3,16,32,128]{3,2,1,0:T(8,128)}, f32[128,128]{1,0:T(8,128)S(1)}) custom-call(f32[8]{0:T(128)S(1)} %broadcast_divide_fusion.inverse, f32[3,16,32,128]{3,2,1,0:T(8,128)} %get-tuple-element.27.given, f32[3,16,32,128]{3,2,1,0:T(8,128)S(1)} %get-tuple-element.20.inner, s32[16,32,128]{2,1,0:T(8,128)S(1)} %copy-done, ...), custom_call_target="tpu_custom_call", output_to_operand_aliasing={{0}: (1, {})} | custom-call | flops 1073741824 | bytes 3489824 | tf_op jit(solution)/shard_map/pallas_call | solution.py:388
  39.6 34.2 %all_to_all.5 = f32[16,8,128]{2,1,0:T(8,128)S(1)} all-to-all(f32[16,8,128]{2,1,0:T(8,128)S(1)} %bitcast.3), channel_id=1, replica_groups=mesh['span'=8,'pitch'=8,'chord'=16] {'chord'}, dimensions={0} | all-to-all | bytes 131072 | tf_op jit(solution)/shard_map/all_to_all | solution.py:484
  73.8 0.6 reduce_sum.9
  (1 shorter events, 0.0 us)
Async XLA Ops:
  3.2 12.4 %collective-permute-start = (f32[56,128]{1,0:T(8,128)S(1)}, f32[56,128]{1,0:T(8,128)S(1)}, u32[]{:S(2)}, u32[]{:S(2)}) collective-permute-start(f32[56,128]{1,0:T(8,128)S(1)} %get-tuple-element.21), channel_id=1, source_target_pairs={{1,0},{2,1},{3,2},{4,3},{5,4},{6,5},{7,6},{8,7},{9,8},{10,9},{11,1... | collective-permute-start | bytes 86024 | tf_op jit(solution)/shard_map/ppermute | solution.py:404
  4.5 11.1 %collective-permute-start.1 = (f32[56,128]{1,0:T(8,128)S(1)}, f32[56,128]{1,0:T(8,128)S(1)}, u32[]{:S(2)}, u32[]{:S(2)}) collective-permute-start(f32[56,128]{1,0:T(8,128)S(1)} %get-tuple-element.22), channel_id=1, source_target_pairs={{0,1},{1,2},{2,3},{3,4},{4,5},{5,6},{6,7},{7,8},{8,9},{9,10},{10,1... | collective-permute-start | bytes 86024 | tf_op jit(solution)/shard_map/ppermute | solution.py:404
  15.9 4.3 %collective-permute-start.2 = (f32[3,3,24,128]{3,2,1,0:T(8,128)S(1)}, f32[3,3,24,128]{3,2,1,0:T(8,128)S(1)}, u32[]{:S(2)}, u32[]{:S(2)}) collective-permute-start(f32[3,3,24,128]{3,2,1,0:T(8,128)S(1)} %get-tuple-element.25), channel_id=1, source_target_pairs={{16,0},{32,16},{48,32},{64,48},{80,64},{96,80},{112,96},{17,1},{33... | collective-permute-start | bytes 331784 | tf_op jit(solution)/shard_map/ppermute | solution.py:404
  17.9 6.1 %collective-permute-start.3 = (f32[3,3,24,128]{3,2,1,0:T(8,128)S(1)}, f32[3,3,24,128]{3,2,1,0:T(8,128)S(1)}, u32[]{:S(2)}, u32[]{:S(2)}) collective-permute-start(f32[3,3,24,128]{3,2,1,0:T(8,128)S(1)} %get-tuple-element.26), channel_id=1, source_target_pairs={{0,16},{16,32},{32,48},{48,64},{64,80},{80,96},{96,112},{1,17},{17... | collective-permute-start | bytes 331784 | tf_op jit(solution)/shard_map/ppermute | solution.py:404
  23.9 6.1 %copy-start = (s32[16,32,128]{2,1,0:T(8,128)S(1)}, s32[16,32,128]{2,1,0:T(8,128)}, u32[]{:S(2)}) copy-start(s32[16,32,128]{2,1,0:T(8,128)} %classes.5) | copy-start | bytes 786436
  23.9 6.1 %copy-start.2 = (f32[3,4096]{1,0:T(4,128)S(1)}, f32[3,4096]{1,0:T(4,128)}, u32[]{:S(2)}) copy-start(f32[3,4096]{1,0:T(4,128)} %wall_normal.3) | copy-start | bytes 147460
  23.9 6.1 %copy-start.3 = (s32[4096]{0:T(1024)S(1)}, s32[4096]{0:T(1024)}, u32[]{:S(2)}) copy-start(s32[4096]{0:T(1024)} %param.12) | copy-start | bytes 49156
  24.1 5.9 %copy-start.5 = (f32[8]{0:T(128)S(1)}, f32[8]{0:T(128)}, u32[]{:S(2)}) copy-start(f32[8]{0:T(128)} %table_in.1) | copy-start | bytes 100
  24.2 9.2 %collective-permute-start.4 = (f32[3,3,32,128]{3,2,1,0:T(8,128)S(1)}, f32[3,3,32,128]{3,2,1,0:T(8,128)S(1)}, u32[]{:S(2)}, u32[]{:S(2)}) collective-permute-start(f32[3,3,32,128]{3,2,1,0:T(8,128)S(1)} %get-tuple-element.29), channel_id=1, source_target_pairs={{128,0},{256,128},{384,256},{512,384},{640,512},{768,640},{896,768... | collective-permute-start | bytes 442376 | tf_op jit(solution)/shard_map/ppermute | solution.py:404
  26.6 8.2 %collective-permute-start.5 = (f32[3,3,32,128]{3,2,1,0:T(8,128)S(1)}, f32[3,3,32,128]{3,2,1,0:T(8,128)S(1)}, u32[]{:S(2)}, u32[]{:S(2)}) collective-permute-start(f32[3,3,32,128]{3,2,1,0:T(8,128)S(1)} %get-tuple-element.30), channel_id=1, source_target_pairs={{0,128},{128,256},{256,384},{384,512},{512,640},{640,768},{768,896... | collective-permute-start | bytes 442376 | tf_op jit(solution)/shard_map/ppermute | solution.py:404
  30.1 4.8 %copy-start.1 = (f32[8,4096]{1,0:T(8,128)S(1)}, f32[8,4096]{1,0:T(8,128)}, u32[]{:S(2)}) copy-start(f32[8,4096]{1,0:T(8,128)} %mode_shape.1) | copy-start | bytes 393220
  30.1 4.8 %copy-start.4 = (s32[4096,1]{0,1:T(1,128)S(1)}, s32[4096,1]{0,1:T(1,128)}, u32[]{:S(2)}) copy-start(s32[4096,1]{0,1:T(1,128)} %param.13) | copy-start | bytes 49156

commit v3 on v2

--- a/solution.py
+++ b/solution.py
@@ -66,7 +66,7 @@
 
 
 def column_kernel(
-    table_in, start, source, classes, p0, cs, z_low, z_high,
+    table_in, start, source, classes, p0, cs, stiffness, z_low, z_high,
     table, y_in, s_in, c_in, beyond, sems, table_sem,
 ):
     table_copy = pltpu.make_async_copy(table_in, table, table_sem)
@@ -95,6 +95,7 @@
             for copy in copies[x // STEP_X]:
                 copy.wait()
         k = pick(table, c_in[x])
+        stiffness[x] = k
         shift = (6 * (x + 2) + 3) % CZ
         for c in range(3):
             value = k * y_in[c, x]
@@ -279,11 +280,11 @@
             out[c, j, 24:32, :] += top
 
 
-def finish_planes(planes, inner, z_next, z_prev, y_next, y_prev, ratio_of, columns, values, part, field, span):
+def finish_planes(planes, inner, z_next, z_prev, y_next, y_prev, stiffness, columns, values, part, field, span):
     unpack(z_next, z_prev, columns)
     zeros = jnp.zeros((8, CZ), jnp.float32)
     for i, x in enumerate(planes):
-        ratio = ratio_of(x)
+        ratio = 1.0 / stiffness[x]
         for c in range(3):
             value = inner[c, x] + chord_part(columns, c, x + 4, 8, CY)
             bottom, top = pitch_rows(y_next, y_prev, c, x + 4)
@@ -300,9 +301,21 @@
             field[256 * c + 128 : 256 * c + 256, 128 * g : 128 * (g + 1)] = second
 
 
-def normal_share(field, place, cell, normals):
-    count = place.shape[1]
-    planes = (iota((field.shape[1], count), 0) == place).astype(jnp.bfloat16)
+def marks(length, place):
+    return (iota((length, place.shape[1]), 0) == place).astype(jnp.bfloat16)
+
+
+def mark_kernel(wall_cell, patch_owner, after, planes, patches):
+    for step in range(WALL // 512):
+        here = slice(step * 512, (step + 1) * 512)
+        plane = wall_cell[:, here] >> 7
+        place = jnp.where(plane < 128, plane, jnp.where(plane >= 384, plane - 256, -1))
+        planes[:, here] = marks(256, place)
+        patches[here, :] = marks(PATCH_DEV, patch_owner[:, here] & 127).T
+
+
+def normal_share(field, planes, cell, normals):
+    count = cell.shape[1]
     picked = jnp.dot(field[...], planes, preferred_element_type=jnp.float32)
     value = jnp.zeros((CZ, count), jnp.float32)
     for c in range(3):
@@ -313,7 +326,7 @@
 
 
 def middle_kernel(
-    inverse, inner, classes, z_next, z_prev, y_next, y_prev, wall_cell, wall_normal,
+    inner, stiffness, z_next, z_prev, y_next, y_prev, wall_cell, wall_normal,
     adjoint, share, columns, values, part, field, sem,
 ):
     def as_is(value, c, x):
@@ -321,20 +334,22 @@
 
     finish_planes(
         range(4, 12), inner, z_next, z_prev, y_next, y_prev,
-        lambda x: pick(inverse, classes[x]), columns, values, part, field, as_is,
+        stiffness, columns, values, part, field, as_is,
     )
     copy = pltpu.make_async_copy(values, adjoint.at[:, 4:12], sem)
     copy.start()
     for step in range(WALL // ROWS):
         here = slice(step * ROWS, (step + 1) * ROWS)
         cell = wall_cell[:, here]
-        share[:, here] = normal_share(field, (cell >> 7) - 128, cell, wall_normal[:, here])
+        share[:, here] = normal_share(
+            field, marks(256, (cell >> 7) - 128), cell, wall_normal[:, here]
+        )
     copy.wait()
 
 
 def wall_kernel(
-    inverse, given, inner, classes, z_next, z_prev, y_next, y_prev, x_next, x_prev, share,
-    wall_cell, patch_owner, wall_normal, mode_shape,
+    given, inner, stiffness, z_next, z_prev, y_next, y_prev, x_next, x_prev, share,
+    wall_cell, patch_owner, wall_normal, mode_shape, planes, patches,
     adjoint, sums, columns, values, part, field, sems,
 ):
     def span(value, c, x):
@@ -346,7 +361,7 @@
 
     finish_planes(
         (0, 1, 2, 3, 12, 13, 14, 15), inner, z_next, z_prev, y_next, y_prev,
-        lambda x: pick(inverse, classes[x]), columns, values, part, field, span,
+        stiffness, columns, values, part, field, span,
     )
     copies = [
         pltpu.make_async_copy(values.at[:, 0:4], adjoint.at[:, 0:4], sems.at[0]),
@@ -359,27 +374,24 @@
     for step in range(WALL // ROWS):
         here = slice(step * ROWS, (step + 1) * ROWS)
         cell, owner = wall_cell[:, here], patch_owner[:, here]
-        plane = cell >> 7
-        place = jnp.where(plane < 128, plane, jnp.where(plane >= 384, plane - 256, -1))
-        normal = share[:, here] + normal_share(field, place, cell, wall_normal[:, here])
+        normal = share[:, here] + normal_share(field, planes[:, here], cell, wall_normal[:, here])
         parts = mode_shape[:, here] * normal
         device = owner >> 7
         spread = jnp.concatenate([jnp.where(device == o, parts, 0.0) for o in range(CHORD)], axis=0)
         first = spread.astype(jnp.bfloat16)
         second = (spread - first.astype(jnp.float32)).astype(jnp.bfloat16)
-        patches = (iota((PATCH_DEV, ROWS), 0) == (owner & 127)).astype(jnp.bfloat16)
         both = jnp.concatenate([first, second], axis=0)
-        total = total + lax.dot_general(
-            both, patches, (((1,), (1,)), ((), ())), preferred_element_type=jnp.float32
-        )
+        total = total + jnp.dot(both, patches[here, :], preferred_element_type=jnp.float32)
     sums[...] = total[0:height] + total[height : 2 * height]
     for copy in copies:
         copy.wait()
 
 
-def call(kernel, outs, operands, spaces, scratch=(), out_spaces=None, aliases=None, flops=0):
+def call(
+    kernel, outs, operands, spaces, scratch=(), out_spaces=None, aliases=None, flops=0, kind=jnp.float32
+):
     spec = {"h": HBM, "s": SMEM, "v": VMEM}
-    shapes = tuple(jax.ShapeDtypeStruct(shape, jnp.float32) for shape in outs)
+    shapes = tuple(jax.ShapeDtypeStruct(shape, kind) for shape in outs)
     moved = sum(4 * o.size for o in operands) + sum(4 * s.size for s in shapes)
     operands = [
         pltpu.with_memory_space_constraint(o, pltpu.HBM) if space == "h" else o
@@ -397,11 +409,16 @@
     )(*operands)
 
 
-def swap(low, high, axis):
-    size = lax.axis_size(axis)
-    up = [(i, i + 1) for i in range(size - 1)]
-    down = [(j, i) for i, j in up]
-    return lax.ppermute(low, axis, down), lax.ppermute(high, axis, up)
+def pairs(axis):
+    return [(i, i + 1) for i in range(lax.axis_size(axis) - 1)]
+
+
+def from_next(low, axis):
+    return lax.ppermute(low, axis, [(j, i) for i, j in pairs(axis)])
+
+
+def from_previous(high, axis):
+    return lax.ppermute(high, axis, pairs(axis))
 
 
 def body(
@@ -416,9 +433,9 @@
 ):
     block, columns = (3, CX, CY, CZ), pltpu.VMEM((3, GY, CZ), jnp.float32)
     grown = pltpu.VMEM((3, GX, GY, CZ), jnp.float32)
-    p0, cs, z_low, z_high = call(
+    p0, cs, stiffness, z_low, z_high = call(
         column_kernel,
-        (block, block, (56, CZ), (56, CZ)),
+        (block, block, (CX, CY, CZ), (56, CZ), (56, CZ)),
         (stiffness_table, adjoint_start, sensitivity_source, stiffness_class),
         "hhhh",
         scratch=(
@@ -431,7 +448,7 @@
             pltpu.SemaphoreType.DMA,
         ),
     )
-    z_next, z_prev = swap(z_low, z_high, "chord")
+    z_next = from_next(z_low, "chord")
     inner, y_low, y_high, x_out = call(
         sweep_kernel,
         (block, (3, GX, 8, CZ), (3, GX, 8, CZ), (3, 6, CY, CZ)),
@@ -440,17 +457,28 @@
         scratch=(grown,) * 5,
         flops=1 << 25,
     )
+    z_high, y_low = lax.optimization_barrier((z_high, y_low))
+    z_prev = from_previous(z_high, "chord")
+    cells, owners = wall_cell.reshape(1, WALL), patch_owner.reshape(1, WALL)
+    planes, patches = call(
+        mark_kernel,
+        ((256, WALL), (WALL, PATCH_DEV)),
+        (cells, owners, y_low),
+        "vvv",
+        flops=1 << 25,
+        kind=jnp.bfloat16,
+    )
+    y_low, planes, patches = lax.optimization_barrier((y_low, planes, patches))
     slab = (3, 3, GX, CZ)
     low, high = call(
         pitch_kernel, (slab, slab), (y_low, y_high, z_next, z_prev), "vvvv", scratch=(columns,)
     )
-    y_next, y_prev = swap(low, high, "pitch")
+    y_next, y_prev = from_next(low, "pitch"), from_previous(high, "pitch")
     slab = (3, 3, CY, CZ)
     low, high = call(
         span_kernel, (slab, slab), (x_out, z_next, z_prev, y_next, y_prev), "vvvvv", scratch=(columns,)
     )
-    x_next, x_prev = swap(low, high, "span")
-    inverse, cells = 1.0 / stiffness_table, wall_cell.reshape(1, WALL)
+    x_next, x_prev = from_next(low, "span"), from_previous(high, "span")
     given = (z_next, z_prev, y_next, y_prev)
     work = (
         columns,
@@ -461,8 +489,8 @@
     adjoint, share = call(
         middle_kernel,
         (block, (1, WALL)),
-        (inverse, inner, stiffness_class, *given, cells, wall_normal),
-        "svvvvvvvv",
+        (inner, stiffness, *given, cells, wall_normal),
+        "vvvvvvvv",
         scratch=(*work, pltpu.SemaphoreType.DMA),
         out_spaces="hv",
         flops=1 << 30,
@@ -471,13 +499,13 @@
         wall_kernel,
         (block, (CHORD * MODES, PATCH_DEV)),
         (
-            inverse, adjoint, inner, stiffness_class, *given, x_next, x_prev, share,
-            cells, patch_owner.reshape(1, WALL), wall_normal, mode_shape,
+            adjoint, inner, stiffness, *given, x_next, x_prev, share,
+            cells, owners, wall_normal, mode_shape, planes, patches,
         ),
-        "shvvvvvvvvvvvvv",
+        "hvvvvvvvvvvvvvvv",
         scratch=(*work, pltpu.SemaphoreType.DMA((2,))),
         out_spaces="hv",
-        aliases={1: 0},
+        aliases={0: 0},
         flops=1 << 30,
     )
     sums = sums.reshape(CHORD, MODES, PATCH_DEV)

time: 74.7 us -> 75.9 us (1.016)
  the two profiles are of different devices: /device:TPU:24 before, /device:TPU:56 now
where the time goes in v3:
time: 75.9 us; the launch traced here: 75.6 us
  blocking collectives  34.9 us (46%)
  starting transfers between devices  20.1 us (26%)
  Pallas kernels  13 us (17%)
  waiting for transfers between devices  6.15 us (8%)
  between operations  0.81 us (1%)
    all_to_all x1, blocking collectives, body(): lax.all_to_all(sums, 'chord', split_axis=0, concat_axis=0, tiled=True)  34.9 us
    ppermute x3, starting transfers between devices, from_previous(): return lax.ppermute(high, axis, pairs(axis))  14.3 us
    pallas_call x7, Pallas kernels, call(): pl.pallas_call(kernel, out_shape=shapes, in_specs=[spec[space] for space...  13 us
    ppermute x3, waiting for transfers between devices, from_previous(): return lax.ppermute(high, axis, pairs(axis))  6.14 us
    ppermute x3, starting transfers between devices, from_next(): return lax.ppermute(low, axis, [(j, i) for i, j in pairs(axis)])  5.79 us
  transfers between devices with their start and end apart: 6, of which 3 were waited for; matrix products, arithmetic and copies ran while one was open for 0% of the time, Pallas kernels for 9%

profile of v3, /device:TPU:56, one launch (start us, length us, event | category | flops | bytes accessed | tf_op | source)
XLA Modules:
  0.0 75.6 jit_solution(2199155827760928435)
XLA Ops:
  0.6 0.0 copy-start.3
  0.6 0.0 copy-start.2
  0.7 0.0 copy-start.1
  0.7 2.6 %shard_map.95 = (f32[3,16,32,128]{3,2,1,0:T(8,128)S(1)}, f32[3,16,32,128]{3,2,1,0:T(8,128)S(1)}, f32[16,32,128]{2,1,0:T(8,128)S(1)}, f32[56,128]{1,0:T(8,128)S(1)}, f32[56,128]{1,0:T(8,128)S(1)}) custom-call(f32[8]{0:T(128)} %table_in.1, f32[3,16,32,128]{3,2,1,0:T(8,128)} %start.1, f32[3,16,32,128]{3,2,1,0:T(8,128)} %source.1, s32[16,32,128]{2,1,0:T(8,128)} %classes.1), custom_call_target="tpu_custom_call" | custom-call | bytes 3727392 | tf_op jit(solution)/shard_map/pallas_call | solution.py:400
  3.3 1.3 %collective-permute-start = (f32[56,128]{1,0:T(8,128)S(1)}, f32[56,128]{1,0:T(8,128)S(1)}, u32[]{:S(2)}, u32[]{:S(2)}) collective-permute-start(f32[56,128]{1,0:T(8,128)S(1)} %get-tuple-element.30), channel_id=1, source_target_pairs={{1,0},{2,1},{3,2},{4,3},{5,4},{6,5},{7,6},{8,7},{9,8},{10,9},{11,1... | collective-permute-start | bytes 86024 | tf_op jit(solution)/shard_map/ppermute | solution.py:417
  4.6 2.6 %shard_map.96 = (f32[3,16,32,128]{3,2,1,0:T(8,128)S(1)}, f32[3,24,8,128]{3,2,1,0:T(8,128)S(1)}, f32[3,24,8,128]{3,2,1,0:T(8,128)S(1)}, f32[3,6,32,128]{3,2,1,0:T(8,128)S(1)}) custom-call(f32[3,16,32,128]{3,2,1,0:T(8,128)S(1)} %get-tuple-element.26.p0_in, f32[3,16,32,128]{3,2,1,0:T(8,128)S(1)} %get-tuple-element.27.cs_in), custom_call_target="tpu_custom_call" | custom-call | flops 33554432 | bytes 3244032 | tf_op jit(solution)/shard_map/pallas_call | solution.py:400
  7.2 8.5 %collective-permute-start.1 = (f32[56,128]{1,0:T(8,128)S(1)}, f32[56,128]{1,0:T(8,128)S(1)}, u32[]{:S(2)}, u32[]{:S(2)}) collective-permute-start(f32[56,128]{1,0:T(8,128)S(1)} %get-tuple-element.33), channel_id=1, source_target_pairs={{0,1},{1,2},{2,3},{3,4},{4,5},{5,6},{6,7},{7,8},{8,9},{9,10},{10,1... | collective-permute-start | bytes 86024 | tf_op jit(solution)/shard_map/ppermute | solution.py:421
  15.7 0.0 copy-done.3
  15.7 0.0 copy-done.2
  15.7 1.1 %shard_map.97 = (bf16[256,4096]{1,0:T(8,128)(2,1)S(1)}, bf16[4096,128]{1,0:T(8,128)(2,1)S(1)}) custom-call(s32[1,4096]{1,0:T(1,128)S(1)} %bitcast.3, s32[1,4096]{1,0:T(1,128)S(1)} %bitcast.6, f32[3,24,8,128]{3,2,1,0:T(8,128)S(1)} %get-tuple-element.37.after.y_low), custom_call_target="tpu_custom_call" | custom-call | flops 33554432 | bytes 6619136 | tf_op jit(solution)/shard_map/pallas_call | solution.py:400
  16.8 0.0 collective-permute-done.z_next
  16.8 0.4 collective-permute-done.1.z_prev
  17.2 0.3 shard_map.98
  17.5 1.9 %collective-permute-start.2 = (f32[3,3,24,128]{3,2,1,0:T(8,128)S(1)}, f32[3,3,24,128]{3,2,1,0:T(8,128)S(1)}, u32[]{:S(2)}, u32[]{:S(2)}) collective-permute-start(f32[3,3,24,128]{3,2,1,0:T(8,128)S(1)} %get-tuple-element.39), channel_id=1, source_target_pairs={{16,0},{32,16},{48,32},{64,48},{80,64},{96,80},{112,96},{17,1},{33... | collective-permute-start | bytes 331784 | tf_op jit(solution)/shard_map/ppermute | solution.py:417
  19.4 2.4 %collective-permute-start.3 = (f32[3,3,24,128]{3,2,1,0:T(8,128)S(1)}, f32[3,3,24,128]{3,2,1,0:T(8,128)S(1)}, u32[]{:S(2)}, u32[]{:S(2)}) collective-permute-start(f32[3,3,24,128]{3,2,1,0:T(8,128)S(1)} %get-tuple-element.40), channel_id=1, source_target_pairs={{0,16},{16,32},{32,48},{48,64},{64,80},{80,96},{96,112},{1,17},{17... | collective-permute-start | bytes 331784 | tf_op jit(solution)/shard_map/ppermute | solution.py:421
  21.9 0.0 collective-permute-done.2.y_next
  21.9 3.6 %collective-permute-done.3.y_prev = f32[3,3,24,128]{3,2,1,0:T(8,128)S(1)} collective-permute-done((f32[3,3,24,128]{3,2,1,0:T(8,128)S(1)}, f32[3,3,24,128]{3,2,1,0:T(8,128)S(1)}, u32[]{:S(2)}, u32[]{:S(2)}) %collective-permute-start.3) | collective-permute-done | bytes 110624 | tf_op jit(solution)/shard_map/ppermute | solution.py:421
  25.5 0.2 shard_map.100
  25.7 0.0 copy-start
  25.7 2.6 %collective-permute-start.4 = (f32[3,3,32,128]{3,2,1,0:T(8,128)S(1)}, f32[3,3,32,128]{3,2,1,0:T(8,128)S(1)}, u32[]{:S(2)}, u32[]{:S(2)}) collective-permute-start(f32[3,3,32,128]{3,2,1,0:T(8,128)S(1)} %get-tuple-element.43), channel_id=1, source_target_pairs={{128,0},{256,128},{384,256},{512,384},{640,512},{768,640},{896,768... | collective-permute-start | bytes 442376 | tf_op jit(solution)/shard_map/ppermute | solution.py:417
  28.3 3.4 %collective-permute-start.5 = (f32[3,3,32,128]{3,2,1,0:T(8,128)S(1)}, f32[3,3,32,128]{3,2,1,0:T(8,128)S(1)}, u32[]{:S(2)}, u32[]{:S(2)}) collective-permute-start(f32[3,3,32,128]{3,2,1,0:T(8,128)S(1)} %get-tuple-element.44), channel_id=1, source_target_pairs={{0,128},{128,256},{256,384},{384,512},{512,640},{640,768},{768,896... | collective-permute-start | bytes 442376 | tf_op jit(solution)/shard_map/ppermute | solution.py:421
  31.7 0.0 copy-done.1
  31.7 2.7 %shard_map.99 = (f32[3,16,32,128]{3,2,1,0:T(8,128)}, f32[1,4096]{1,0:T(1,128)S(1)}) custom-call(f32[3,16,32,128]{3,2,1,0:T(8,128)S(1)} %get-tuple-element.28.inner, f32[16,32,128]{2,1,0:T(8,128)S(1)} %get-tuple-element.29.stiffness, f32[56,128]{1,0:T(8,128)S(1)} %collective-permute-done.z_next, f32[56,128]{1,0:T(8,128)S(1)} %collective-permute-done.1.z_prev, ...), custom_call_target="tpu_custom_call" | custom-call | flops 1073741824 | bytes 2195456 | tf_op jit(solution)/shard_map/pallas_call | solution.py:400
  34.4 0.0 collective-permute-done.4.x_next
  34.5 2.1 %collective-permute-done.5.x_prev = f32[3,3,32,128]{3,2,1,0:T(8,128)S(1)} collective-permute-done((f32[3,3,32,128]{3,2,1,0:T(8,128)S(1)}, f32[3,3,32,128]{3,2,1,0:T(8,128)S(1)}, u32[]{:S(2)}, u32[]{:S(2)}) %collective-permute-start.5) | collective-permute-done | bytes 147488 | tf_op jit(solution)/shard_map/ppermute | solution.py:421
  36.6 0.0 copy-done
  36.6 3.5 %shard_map.101 = (f32[3,16,32,128]{3,2,1,0:T(8,128)}, f32[128,128]{1,0:T(8,128)S(1)}) custom-call(f32[3,16,32,128]{3,2,1,0:T(8,128)} %get-tuple-element.41.given, f32[3,16,32,128]{3,2,1,0:T(8,128)S(1)} %get-tuple-element.28.inner, f32[16,32,128]{2,1,0:T(8,128)S(1)} %get-tuple-element.29.stiffness, ...), custom_call_target="tpu_custom_call", output_to_operand_aliasing={{0}: (0, {})} | custom-call | flops 1073741824 | bytes 9781248 | tf_op jit(solution)/shard_map/pallas_call | solution.py:400
  40.1 34.9 %all_to_all.5 = f32[16,8,128]{2,1,0:T(8,128)S(1)} all-to-all(f32[16,8,128]{2,1,0:T(8,128)S(1)} %bitcast.8), channel_id=1, replica_groups=mesh['span'=8,'pitch'=8,'chord'=16] {'chord'}, dimensions={0} | all-to-all | bytes 131072 | tf_op jit(solution)/shard_map/all_to_all | solution.py:512
  75.0 0.6 reduce_sum.9
Async XLA Ops:
  0.6 15.1 %copy-start.3 = (s32[4096,1]{0,1:T(1,128)S(1)}, s32[4096,1]{0,1:T(1,128)}, u32[]{:S(2)}) copy-start(s32[4096,1]{0,1:T(1,128)} %param.13) | copy-start | bytes 49156
  0.6 15.1 %copy-start.2 = (s32[4096]{0:T(1024)S(1)}, s32[4096]{0:T(1024)}, u32[]{:S(2)}) copy-start(s32[4096]{0:T(1024)} %param.12) | copy-start | bytes 49156
  0.7 31.1 %copy-start.1 = (f32[3,4096]{1,0:T(4,128)S(1)}, f32[3,4096]{1,0:T(4,128)}, u32[]{:S(2)}) copy-start(f32[3,4096]{1,0:T(4,128)} %wall_normal.3) | copy-start | bytes 147460
  3.3 13.5 %collective-permute-start = (f32[56,128]{1,0:T(8,128)S(1)}, f32[56,128]{1,0:T(8,128)S(1)}, u32[]{:S(2)}, u32[]{:S(2)}) collective-permute-start(f32[56,128]{1,0:T(8,128)S(1)} %get-tuple-element.30), channel_id=1, source_target_pairs={{1,0},{2,1},{3,2},{4,3},{5,4},{6,5},{7,6},{8,7},{9,8},{10,9},{11,1... | collective-permute-start | bytes 86024 | tf_op jit(solution)/shard_map/ppermute | solution.py:417
  7.2 10.0 %collective-permute-start.1 = (f32[56,128]{1,0:T(8,128)S(1)}, f32[56,128]{1,0:T(8,128)S(1)}, u32[]{:S(2)}, u32[]{:S(2)}) collective-permute-start(f32[56,128]{1,0:T(8,128)S(1)} %get-tuple-element.33), channel_id=1, source_target_pairs={{0,1},{1,2},{2,3},{3,4},{4,5},{5,6},{6,7},{7,8},{8,9},{9,10},{10,1... | collective-permute-start | bytes 86024 | tf_op jit(solution)/shard_map/ppermute | solution.py:421
  17.5 4.3 %collective-permute-start.2 = (f32[3,3,24,128]{3,2,1,0:T(8,128)S(1)}, f32[3,3,24,128]{3,2,1,0:T(8,128)S(1)}, u32[]{:S(2)}, u32[]{:S(2)}) collective-permute-start(f32[3,3,24,128]{3,2,1,0:T(8,128)S(1)} %get-tuple-element.39), channel_id=1, source_target_pairs={{16,0},{32,16},{48,32},{64,48},{80,64},{96,80},{112,96},{17,1},{33... | collective-permute-start | bytes 331784 | tf_op jit(solution)/shard_map/ppermute | solution.py:417
  19.4 6.1 %collective-permute-start.3 = (f32[3,3,24,128]{3,2,1,0:T(8,128)S(1)}, f32[3,3,24,128]{3,2,1,0:T(8,128)S(1)}, u32[]{:S(2)}, u32[]{:S(2)}) collective-permute-start(f32[3,3,24,128]{3,2,1,0:T(8,128)S(1)} %get-tuple-element.40), channel_id=1, source_target_pairs={{0,16},{16,32},{32,48},{48,64},{64,80},{80,96},{96,112},{1,17},{17... | collective-permute-start | bytes 331784 | tf_op jit(solution)/shard_map/ppermute | solution.py:421
  25.7 10.8 %copy-start = (f32[8,4096]{1,0:T(8,128)S(1)}, f32[8,4096]{1,0:T(8,128)}, u32[]{:S(2)}) copy-start(f32[8,4096]{1,0:T(8,128)} %mode_shape.1) | copy-start | bytes 393220
  25.7 8.7 %collective-permute-start.4 = (f32[3,3,32,128]{3,2,1,0:T(8,128)S(1)}, f32[3,3,32,128]{3,2,1,0:T(8,128)S(1)}, u32[]{:S(2)}, u32[]{:S(2)}) collective-permute-start(f32[3,3,32,128]{3,2,1,0:T(8,128)S(1)} %get-tuple-element.43), channel_id=1, source_target_pairs={{128,0},{256,128},{384,256},{512,384},{640,512},{768,640},{896,768... | collective-permute-start | bytes 442376 | tf_op jit(solution)/shard_map/ppermute | solution.py:417
  28.3 8.2 %collective-permute-start.5 = (f32[3,3,32,128]{3,2,1,0:T(8,128)S(1)}, f32[3,3,32,128]{3,2,1,0:T(8,128)S(1)}, u32[]{:S(2)}, u32[]{:S(2)}) collective-permute-start(f32[3,3,32,128]{3,2,1,0:T(8,128)S(1)} %get-tuple-element.44), channel_id=1, source_target_pairs={{0,128},{128,256},{256,384},{384,512},{512,640},{640,768},{768,896... | collective-permute-start | bytes 442376 | tf_op jit(solution)/shard_map/ppermute | solution.py:421

commit v4 on v3

--- a/solution.py
+++ b/solution.py
@@ -227,7 +227,7 @@
     lax.fori_loop(4, 20, middle, 0, unroll=True)
 
 
-def unpack(z_next, z_prev, columns):
+def unpack(z_prev, z_next, columns):
     _, slot = slots((HALF, CZ))
     for c in range(3):
         rows = slice(HALF * c, HALF * (c + 1))
@@ -244,8 +244,8 @@
     return jnp.where((lane < 3) | (lane >= CZ - 3), placed, 0.0)
 
 
-def pitch_kernel(y_low, y_high, z_next, z_prev, low, high, columns):
-    unpack(z_next, z_prev, columns)
+def pitch_kernel(y_low, y_high, z_prev, z_next, low, high, columns):
+    unpack(z_prev, z_next, columns)
     for c in range(3):
         for x in range(1, 23):
             for tile, out, start, first in ((y_low, low, 0, 5), (y_high, high, 40, 0)):
@@ -266,8 +266,8 @@
     return bottom, top
 
 
-def span_kernel(x_out, z_next, z_prev, y_next, y_prev, low, high, columns):
-    unpack(z_next, z_prev, columns)
+def span_kernel(x_out, z_prev, z_next, y_next, y_prev, low, high, columns):
+    unpack(z_prev, z_next, columns)
     for c in range(3):
         for i, x in enumerate((1, 2, 3, 20, 21, 22)):
             out, j = (low, i) if i < 3 else (high, i - 3)
@@ -280,8 +280,8 @@
             out[c, j, 24:32, :] += top
 
 
-def finish_planes(planes, inner, z_next, z_prev, y_next, y_prev, stiffness, columns, values, part, field, span):
-    unpack(z_next, z_prev, columns)
+def finish_planes(planes, inner, z_prev, z_next, y_next, y_prev, stiffness, columns, values, part, field, span):
+    unpack(z_prev, z_next, columns)
     zeros = jnp.zeros((8, CZ), jnp.float32)
     for i, x in enumerate(planes):
         ratio = 1.0 / stiffness[x]
@@ -326,14 +326,14 @@
 
 
 def middle_kernel(
-    inner, stiffness, z_next, z_prev, y_next, y_prev, wall_cell, wall_normal,
+    inner, stiffness, z_prev, z_next, y_next, y_prev, wall_cell, wall_normal,
     adjoint, share, columns, values, part, field, sem,
 ):
     def as_is(value, c, x):
         return value
 
     finish_planes(
-        range(4, 12), inner, z_next, z_prev, y_next, y_prev,
+        range(4, 12), inner, z_prev, z_next, y_next, y_prev,
         stiffness, columns, values, part, field, as_is,
     )
     copy = pltpu.make_async_copy(values, adjoint.at[:, 4:12], sem)
@@ -348,7 +348,7 @@
 
 
 def wall_kernel(
-    given, inner, stiffness, z_next, z_prev, y_next, y_prev, x_next, x_prev, share,
+    given, inner, stiffness, z_prev, z_next, y_next, y_prev, x_next, x_prev, share,
     wall_cell, patch_owner, wall_normal, mode_shape, planes, patches,
     adjoint, sums, columns, values, part, field, sems,
 ):
@@ -360,7 +360,7 @@
         return value
 
     finish_planes(
-        (0, 1, 2, 3, 12, 13, 14, 15), inner, z_next, z_prev, y_next, y_prev,
+        (0, 1, 2, 3, 12, 13, 14, 15), inner, z_prev, z_next, y_next, y_prev,
         stiffness, columns, values, part, field, span,
     )
     copies = [
@@ -448,7 +448,7 @@
             pltpu.SemaphoreType.DMA,
         ),
     )
-    z_next = from_next(z_low, "chord")
+    z_prev, z_next = from_previous(z_high, "chord"), from_next(z_low, "chord")
     inner, y_low, y_high, x_out = call(
         sweep_kernel,
         (block, (3, GX, 8, CZ), (3, GX, 8, CZ), (3, 6, CY, CZ)),
@@ -457,8 +457,6 @@
         scratch=(grown,) * 5,
         flops=1 << 25,
     )
-    z_high, y_low = lax.optimization_barrier((z_high, y_low))
-    z_prev = from_previous(z_high, "chord")
     cells, owners = wall_cell.reshape(1, WALL), patch_owner.reshape(1, WALL)
     planes, patches = call(
         mark_kernel,
@@ -471,15 +469,15 @@
     y_low, planes, patches = lax.optimization_barrier((y_low, planes, patches))
     slab = (3, 3, GX, CZ)
     low, high = call(
-        pitch_kernel, (slab, slab), (y_low, y_high, z_next, z_prev), "vvvv", scratch=(columns,)
+        pitch_kernel, (slab, slab), (y_low, y_high, z_prev, z_next), "vvvv", scratch=(columns,)
     )
     y_next, y_prev = from_next(low, "pitch"), from_previous(high, "pitch")
     slab = (3, 3, CY, CZ)
     low, high = call(
-        span_kernel, (slab, slab), (x_out, z_next, z_prev, y_next, y_prev), "vvvvv", scratch=(columns,)
+        span_kernel, (slab, slab), (x_out, z_prev, z_next, y_next, y_prev), "vvvvv", scratch=(columns,)
     )
     x_next, x_prev = from_next(low, "span"), from_previous(high, "span")
-    given = (z_next, z_prev, y_next, y_prev)
+    given = (z_prev, z_next, y_next, y_prev)
     work = (
         columns,
         pltpu.VMEM((3, CX // 2, CY, CZ), jnp.float32),

time: 75.9 us -> 75.1 us (0.989)
  the two profiles are of different devices: /device:TPU:56 before, /device:TPU:24 now
where the time goes in v4:
time: 75.1 us; the launch traced here: 74.8 us
  blocking collectives  31.1 us (41%)
  starting transfers between devices  18.9 us (25%)
  Pallas kernels  13 us (17%)
  waiting for transfers between devices  10.4 us (14%)
  between operations  0.81 us (1%)
    all_to_all x1, blocking collectives, body(): lax.all_to_all(sums, 'chord', split_axis=0, concat_axis=0, tiled=True)  31.1 us
    ppermute x3, starting transfers between devices, from_previous(): return lax.ppermute(high, axis, pairs(axis))  13.1 us
    pallas_call x7, Pallas kernels, call(): pl.pallas_call(kernel, out_shape=shapes, in_specs=[spec[space] for space...  13 us
    ppermute x3, starting transfers between devices, from_next(): return lax.ppermute(low, axis, [(j, i) for i, j in pairs(axis)])  5.79 us
    ppermute x3, waiting for transfers between devices, from_previous(): return lax.ppermute(high, axis, pairs(axis))  5.75 us
    ppermute x3, waiting for transfers between devices, from_next(): return lax.ppermute(low, axis, [(j, i) for i, j in pairs(axis)])  4.61 us
  transfers between devices with their start and end apart: 6, of which 3 were waited for; matrix products, arithmetic and copies ran while one was open for 0% of the time, Pallas kernels for 9%

profile of v4, /device:TPU:24, one launch (start us, length us, event | category | flops | bytes accessed | tf_op | source)
XLA Modules:
  0.0 74.8 jit_solution(9288309782751384709)
XLA Ops:
  0.6 0.0 copy-start.3
  0.6 0.0 copy-start.2
  0.7 0.0 copy-start.1
  0.7 2.6 %shard_map.95 = (f32[3,16,32,128]{3,2,1,0:T(8,128)S(1)}, f32[3,16,32,128]{3,2,1,0:T(8,128)S(1)}, f32[16,32,128]{2,1,0:T(8,128)S(1)}, f32[56,128]{1,0:T(8,128)S(1)}, f32[56,128]{1,0:T(8,128)S(1)}) custom-call(f32[8]{0:T(128)} %table_in.1, f32[3,16,32,128]{3,2,1,0:T(8,128)} %start.1, f32[3,16,32,128]{3,2,1,0:T(8,128)} %source.1, s32[16,32,128]{2,1,0:T(8,128)} %classes.1), custom_call_target="tpu_custom_call" | custom-call | bytes 3727392 | tf_op jit(solution)/shard_map/pallas_call | solution.py:400
  3.3 7.3 %collective-permute-start = (f32[56,128]{1,0:T(8,128)S(1)}, f32[56,128]{1,0:T(8,128)S(1)}, u32[]{:S(2)}, u32[]{:S(2)}) collective-permute-start(f32[56,128]{1,0:T(8,128)S(1)} %get-tuple-element.28), channel_id=1, source_target_pairs={{0,1},{1,2},{2,3},{3,4},{4,5},{5,6},{6,7},{7,8},{8,9},{9,10},{10,1... | collective-permute-start | bytes 86024 | tf_op jit(solution)/shard_map/ppermute | solution.py:421
  10.6 1.3 %collective-permute-start.1 = (f32[56,128]{1,0:T(8,128)S(1)}, f32[56,128]{1,0:T(8,128)S(1)}, u32[]{:S(2)}, u32[]{:S(2)}) collective-permute-start(f32[56,128]{1,0:T(8,128)S(1)} %get-tuple-element.29), channel_id=1, source_target_pairs={{1,0},{2,1},{3,2},{4,3},{5,4},{6,5},{7,6},{8,7},{9,8},{10,9},{11,1... | collective-permute-start | bytes 86024 | tf_op jit(solution)/shard_map/ppermute | solution.py:417
  11.9 2.6 %shard_map.96 = (f32[3,16,32,128]{3,2,1,0:T(8,128)S(1)}, f32[3,24,8,128]{3,2,1,0:T(8,128)S(1)}, f32[3,24,8,128]{3,2,1,0:T(8,128)S(1)}, f32[3,6,32,128]{3,2,1,0:T(8,128)S(1)}) custom-call(f32[3,16,32,128]{3,2,1,0:T(8,128)S(1)} %get-tuple-element.24.p0_in, f32[3,16,32,128]{3,2,1,0:T(8,128)S(1)} %get-tuple-element.25.cs_in), custom_call_target="tpu_custom_call" | custom-call | flops 33554432 | bytes 3244032 | tf_op jit(solution)/shard_map/pallas_call | solution.py:400
  14.5 0.0 copy-done.3
  14.5 0.0 copy-done.2
  14.5 1.1 %shard_map.97 = (bf16[256,4096]{1,0:T(8,128)(2,1)S(1)}, bf16[4096,128]{1,0:T(8,128)(2,1)S(1)}) custom-call(s32[1,4096]{1,0:T(1,128)S(1)} %bitcast.3, s32[1,4096]{1,0:T(1,128)S(1)} %bitcast.6, f32[3,24,8,128]{3,2,1,0:T(8,128)S(1)} %get-tuple-element.33.after.y_low), custom_call_target="tpu_custom_call" | custom-call | flops 33554432 | bytes 6619136 | tf_op jit(solution)/shard_map/pallas_call | solution.py:400
  15.7 0.0 collective-permute-done.z_prev
  15.7 4.6 %collective-permute-done.1.z_next = f32[56,128]{1,0:T(8,128)S(1)} collective-permute-done((f32[56,128]{1,0:T(8,128)S(1)}, f32[56,128]{1,0:T(8,128)S(1)}, u32[]{:S(2)}, u32[]{:S(2)}) %collective-permute-start.1) | collective-permute-done | bytes 28704 | tf_op jit(solution)/shard_map/ppermute | solution.py:417
  20.3 0.3 shard_map.98
  20.5 1.9 %collective-permute-start.2 = (f32[3,3,24,128]{3,2,1,0:T(8,128)S(1)}, f32[3,3,24,128]{3,2,1,0:T(8,128)S(1)}, u32[]{:S(2)}, u32[]{:S(2)}) collective-permute-start(f32[3,3,24,128]{3,2,1,0:T(8,128)S(1)} %get-tuple-element.35), channel_id=1, source_target_pairs={{16,0},{32,16},{48,32},{64,48},{80,64},{96,80},{112,96},{17,1},{33... | collective-permute-start | bytes 331784 | tf_op jit(solution)/shard_map/ppermute | solution.py:417
  22.5 2.4 %collective-permute-start.3 = (f32[3,3,24,128]{3,2,1,0:T(8,128)S(1)}, f32[3,3,24,128]{3,2,1,0:T(8,128)S(1)}, u32[]{:S(2)}, u32[]{:S(2)}) collective-permute-start(f32[3,3,24,128]{3,2,1,0:T(8,128)S(1)} %get-tuple-element.36), channel_id=1, source_target_pairs={{0,16},{16,32},{32,48},{48,64},{64,80},{80,96},{96,112},{1,17},{17... | collective-permute-start | bytes 331784 | tf_op jit(solution)/shard_map/ppermute | solution.py:421
  24.9 0.0 collective-permute-done.2.y_next
  24.9 3.6 %collective-permute-done.3.y_prev = f32[3,3,24,128]{3,2,1,0:T(8,128)S(1)} collective-permute-done((f32[3,3,24,128]{3,2,1,0:T(8,128)S(1)}, f32[3,3,24,128]{3,2,1,0:T(8,128)S(1)}, u32[]{:S(2)}, u32[]{:S(2)}) %collective-permute-start.3) | collective-permute-done | bytes 110624 | tf_op jit(solution)/shard_map/ppermute | solution.py:421
  28.5 0.2 shard_map.100
  28.8 0.0 copy-start
  28.8 2.6 %collective-permute-start.4 = (f32[3,3,32,128]{3,2,1,0:T(8,128)S(1)}, f32[3,3,32,128]{3,2,1,0:T(8,128)S(1)}, u32[]{:S(2)}, u32[]{:S(2)}) collective-permute-start(f32[3,3,32,128]{3,2,1,0:T(8,128)S(1)} %get-tuple-element.39), channel_id=1, source_target_pairs={{128,0},{256,128},{384,256},{512,384},{640,512},{768,640},{896,768... | collective-permute-start | bytes 442376 | tf_op jit(solution)/shard_map/ppermute | solution.py:417
  31.3 3.4 %collective-permute-start.5 = (f32[3,3,32,128]{3,2,1,0:T(8,128)S(1)}, f32[3,3,32,128]{3,2,1,0:T(8,128)S(1)}, u32[]{:S(2)}, u32[]{:S(2)}) collective-permute-start(f32[3,3,32,128]{3,2,1,0:T(8,128)S(1)} %get-tuple-element.40), channel_id=1, source_target_pairs={{0,128},{128,256},{256,384},{384,512},{512,640},{640,768},{768,896... | collective-permute-start | bytes 442376 | tf_op jit(solution)/shard_map/ppermute | solution.py:421
  34.8 0.0 copy-done.1
  34.8 2.7 %shard_map.99 = (f32[3,16,32,128]{3,2,1,0:T(8,128)}, f32[1,4096]{1,0:T(1,128)S(1)}) custom-call(f32[3,16,32,128]{3,2,1,0:T(8,128)S(1)} %get-tuple-element.26.inner, f32[16,32,128]{2,1,0:T(8,128)S(1)} %get-tuple-element.27.stiffness, f32[56,128]{1,0:T(8,128)S(1)} %collective-permute-done.z_prev, f32[56,128]{1,0:T(8,128)S(1)} %collective-permute-done.1.z_next, ...), custom_call_target="tpu_custom_call" | custom-call | flops 1073741824 | bytes 2195456 | tf_op jit(solution)/shard_map/pallas_call | solution.py:400
  37.5 0.0 collective-permute-done.4.x_next
  37.5 2.1 %collective-permute-done.5.x_prev = f32[3,3,32,128]{3,2,1,0:T(8,128)S(1)} collective-permute-done((f32[3,3,32,128]{3,2,1,0:T(8,128)S(1)}, f32[3,3,32,128]{3,2,1,0:T(8,128)S(1)}, u32[]{:S(2)}, u32[]{:S(2)}) %collective-permute-start.5) | collective-permute-done | bytes 147488 | tf_op jit(solution)/shard_map/ppermute | solution.py:421
  39.6 0.0 copy-done
  39.6 3.5 %shard_map.101 = (f32[3,16,32,128]{3,2,1,0:T(8,128)}, f32[128,128]{1,0:T(8,128)S(1)}) custom-call(f32[3,16,32,128]{3,2,1,0:T(8,128)} %get-tuple-element.37.given, f32[3,16,32,128]{3,2,1,0:T(8,128)S(1)} %get-tuple-element.26.inner, f32[16,32,128]{2,1,0:T(8,128)S(1)} %get-tuple-element.27.stiffness, ...), custom_call_target="tpu_custom_call", output_to_operand_aliasing={{0}: (0, {})} | custom-call | flops 1073741824 | bytes 9781248 | tf_op jit(solution)/shard_map/pallas_call | solution.py:400
  43.1 31.1 %all_to_all.5 = f32[16,8,128]{2,1,0:T(8,128)S(1)} all-to-all(f32[16,8,128]{2,1,0:T(8,128)S(1)} %bitcast.8), channel_id=1, replica_groups=mesh['span'=8,'pitch'=8,'chord'=16] {'chord'}, dimensions={0} | all-to-all | bytes 131072 | tf_op jit(solution)/shard_map/all_to_all | solution.py:510
  74.2 0.6 reduce_sum.9
Async XLA Ops:
  0.6 13.9 %copy-start.3 = (s32[4096,1]{0,1:T(1,128)S(1)}, s32[4096,1]{0,1:T(1,128)}, u32[]{:S(2)}) copy-start(s32[4096,1]{0,1:T(1,128)} %param.13) | copy-start | bytes 49156
  0.6 13.9 %copy-start.2 = (s32[4096]{0:T(1024)S(1)}, s32[4096]{0:T(1024)}, u32[]{:S(2)}) copy-start(s32[4096]{0:T(1024)} %param.12) | copy-start | bytes 49156
  0.7 34.1 %copy-start.1 = (f32[3,4096]{1,0:T(4,128)S(1)}, f32[3,4096]{1,0:T(4,128)}, u32[]{:S(2)}) copy-start(f32[3,4096]{1,0:T(4,128)} %wall_normal.3) | copy-start | bytes 147460
  3.3 12.4 %collective-permute-start = (f32[56,128]{1,0:T(8,128)S(1)}, f32[56,128]{1,0:T(8,128)S(1)}, u32[]{:S(2)}, u32[]{:S(2)}) collective-permute-start(f32[56,128]{1,0:T(8,128)S(1)} %get-tuple-element.28), channel_id=1, source_target_pairs={{0,1},{1,2},{2,3},{3,4},{4,5},{5,6},{6,7},{7,8},{8,9},{9,10},{10,1... | collective-permute-start | bytes 86024 | tf_op jit(solution)/shard_map/ppermute | solution.py:421
  10.6 9.7 %collective-permute-start.1 = (f32[56,128]{1,0:T(8,128)S(1)}, f32[56,128]{1,0:T(8,128)S(1)}, u32[]{:S(2)}, u32[]{:S(2)}) collective-permute-start(f32[56,128]{1,0:T(8,128)S(1)} %get-tuple-element.29), channel_id=1, source_target_pairs={{1,0},{2,1},{3,2},{4,3},{5,4},{6,5},{7,6},{8,7},{9,8},{10,9},{11,1... | collective-permute-start | bytes 86024 | tf_op jit(solution)/shard_map/ppermute | solution.py:417
  20.5 4.3 %collective-permute-start.2 = (f32[3,3,24,128]{3,2,1,0:T(8,128)S(1)}, f32[3,3,24,128]{3,2,1,0:T(8,128)S(1)}, u32[]{:S(2)}, u32[]{:S(2)}) collective-permute-start(f32[3,3,24,128]{3,2,1,0:T(8,128)S(1)} %get-tuple-element.35), channel_id=1, source_target_pairs={{16,0},{32,16},{48,32},{64,48},{80,64},{96,80},{112,96},{17,1},{33... | collective-permute-start | bytes 331784 | tf_op jit(solution)/shard_map/ppermute | solution.py:417
  22.5 6.1 %collective-permute-start.3 = (f32[3,3,24,128]{3,2,1,0:T(8,128)S(1)}, f32[3,3,24,128]{3,2,1,0:T(8,128)S(1)}, u32[]{:S(2)}, u32[]{:S(2)}) collective-permute-start(f32[3,3,24,128]{3,2,1,0:T(8,128)S(1)} %get-tuple-element.36), channel_id=1, source_target_pairs={{0,16},{16,32},{32,48},{48,64},{64,80},{80,96},{96,112},{1,17},{17... | collective-permute-start | bytes 331784 | tf_op jit(solution)/shard_map/ppermute | solution.py:421
  28.8 10.8 %copy-start = (f32[8,4096]{1,0:T(8,128)S(1)}, f32[8,4096]{1,0:T(8,128)}, u32[]{:S(2)}) copy-start(f32[8,4096]{1,0:T(8,128)} %mode_shape.1) | copy-start | bytes 393220
  28.8 8.7 %collective-permute-start.4 = (f32[3,3,32,128]{3,2,1,0:T(8,128)S(1)}, f32[3,3,32,128]{3,2,1,0:T(8,128)S(1)}, u32[]{:S(2)}, u32[]{:S(2)}) collective-permute-start(f32[3,3,32,128]{3,2,1,0:T(8,128)S(1)} %get-tuple-element.39), channel_id=1, source_target_pairs={{128,0},{256,128},{384,256},{512,384},{640,512},{768,640},{896,768... | collective-permute-start | bytes 442376 | tf_op jit(solution)/shard_map/ppermute | solution.py:417
  31.3 8.2 %collective-permute-start.5 = (f32[3,3,32,128]{3,2,1,0:T(8,128)S(1)}, f32[3,3,32,128]{3,2,1,0:T(8,128)S(1)}, u32[]{:S(2)}, u32[]{:S(2)}) collective-permute-start(f32[3,3,32,128]{3,2,1,0:T(8,128)S(1)} %get-tuple-element.40), channel_id=1, source_target_pairs={{0,128},{128,256},{256,384},{384,512},{512,640},{640,768},{768,896... | collective-permute-start | bytes 442376 | tf_op jit(solution)/shard_map/ppermute | solution.py:421

commit v5 on v3

--- a/solution.py
+++ b/solution.py
@@ -369,20 +369,22 @@
     ]
     for copy in copies:
         copy.start()
-    height = CHORD * MODES
-    total = jnp.zeros((2 * height, PATCH_DEV), jnp.float32)
+    total = jnp.zeros((2 * CHORD * MODES, PATCH_DEV), jnp.float32)
     for step in range(WALL // ROWS):
         here = slice(step * ROWS, (step + 1) * ROWS)
         cell, owner = wall_cell[:, here], patch_owner[:, here]
         normal = share[:, here] + normal_share(field, planes[:, here], cell, wall_normal[:, here])
         parts = mode_shape[:, here] * normal
-        device = owner >> 7
-        spread = jnp.concatenate([jnp.where(device == o, parts, 0.0) for o in range(CHORD)], axis=0)
-        first = spread.astype(jnp.bfloat16)
-        second = (spread - first.astype(jnp.float32)).astype(jnp.bfloat16)
-        both = jnp.concatenate([first, second], axis=0)
+        high = parts.astype(jnp.bfloat16).astype(jnp.float32)
+        pieces = jnp.concatenate([high, parts - high], axis=0).astype(jnp.bfloat16)
+        device = jnp.broadcast_to((owner >> 7).astype(jnp.float32), pieces.shape).astype(jnp.bfloat16)
+        both = jnp.concatenate(
+            [jnp.where(device == o, pieces, jnp.bfloat16(0)) for o in range(CHORD)], axis=0
+        )
         total = total + jnp.dot(both, patches[here, :], preferred_element_type=jnp.float32)
-    sums[...] = total[0:height] + total[height : 2 * height]
+    for o in range(CHORD):
+        first, second = 2 * MODES * o, MODES * (2 * o + 1)
+        sums[MODES * o : MODES * (o + 1), :] = total[first : first + MODES] + total[second : second + MODES]
     for copy in copies:
         copy.wait()
 
@@ -448,7 +450,7 @@
             pltpu.SemaphoreType.DMA,
         ),
     )
-    z_next = from_next(z_low, "chord")
+    z_prev, z_next = from_previous(z_high, "chord"), from_next(z_low, "chord")
     inner, y_low, y_high, x_out = call(
         sweep_kernel,
         (block, (3, GX, 8, CZ), (3, GX, 8, CZ), (3, 6, CY, CZ)),
@@ -457,8 +459,6 @@
         scratch=(grown,) * 5,
         flops=1 << 25,
     )
-    z_high, y_low = lax.optimization_barrier((z_high, y_low))
-    z_prev = from_previous(z_high, "chord")
     cells, owners = wall_cell.reshape(1, WALL), patch_owner.reshape(1, WALL)
     planes, patches = call(
         mark_kernel,

time: 75.9 us -> 74.6 us (0.983)
  the two profiles are of different devices: /device:TPU:56 before, /device:TPU:24 now
where the time goes in v5:
time: 74.6 us; the launch traced here: 74.3 us
  blocking collectives  34.2 us (46%)
  starting transfers between devices  20 us (27%)
  Pallas kernels  12.9 us (17%)
  waiting for transfers between devices  5.76 us (8%)
  between operations  0.82 us (1%)
    all_to_all x1, blocking collectives, body(): lax.all_to_all(sums, 'chord', split_axis=0, concat_axis=0, tiled=True)  34.2 us
    ppermute x3, starting transfers between devices, from_previous(): return lax.ppermute(high, axis, pairs(axis))  14.3 us
    pallas_call x7, Pallas kernels, call(): pl.pallas_call(kernel, out_shape=shapes, in_specs=[spec[space] for space...  12.9 us
    ppermute x3, starting transfers between devices, from_next(): return lax.ppermute(low, axis, [(j, i) for i, j in pairs(axis)])  5.79 us
    ppermute x3, waiting for transfers between devices, from_previous(): return lax.ppermute(high, axis, pairs(axis))  5.75 us
  transfers between devices with their start and end apart: 6, of which 2 were waited for; matrix products, arithmetic and copies ran while one was open for 0% of the time, Pallas kernels for 9%

profile of v5, /device:TPU:24, one launch (start us, length us, event | category | flops | bytes accessed | tf_op | source)
XLA Modules:
  0.0 74.3 jit_solution(12287604000246112927)
XLA Ops:
  0.6 0.0 copy-start.3
  0.6 0.0 copy-start.2
  0.7 0.0 copy-start.1
  0.7 2.6 %shard_map.95 = (f32[3,16,32,128]{3,2,1,0:T(8,128)S(1)}, f32[3,16,32,128]{3,2,1,0:T(8,128)S(1)}, f32[16,32,128]{2,1,0:T(8,128)S(1)}, f32[56,128]{1,0:T(8,128)S(1)}, f32[56,128]{1,0:T(8,128)S(1)}) custom-call(f32[8]{0:T(128)} %table_in.1, f32[3,16,32,128]{3,2,1,0:T(8,128)} %start.1, f32[3,16,32,128]{3,2,1,0:T(8,128)} %source.1, s32[16,32,128]{2,1,0:T(8,128)} %classes.1), custom_call_target="tpu_custom_call" | custom-call | bytes 3727392 | tf_op jit(solution)/shard_map/pallas_call | solution.py:402
  3.3 1.3 %collective-permute-start = (f32[56,128]{1,0:T(8,128)S(1)}, f32[56,128]{1,0:T(8,128)S(1)}, u32[]{:S(2)}, u32[]{:S(2)}) collective-permute-start(f32[56,128]{1,0:T(8,128)S(1)} %get-tuple-element.28), channel_id=1, source_target_pairs={{1,0},{2,1},{3,2},{4,3},{5,4},{6,5},{7,6},{8,7},{9,8},{10,9},{11,1... | collective-permute-start | bytes 86024 | tf_op jit(solution)/shard_map/ppermute | solution.py:419
  4.6 8.5 %collective-permute-start.1 = (f32[56,128]{1,0:T(8,128)S(1)}, f32[56,128]{1,0:T(8,128)S(1)}, u32[]{:S(2)}, u32[]{:S(2)}) collective-permute-start(f32[56,128]{1,0:T(8,128)S(1)} %get-tuple-element.29), channel_id=1, source_target_pairs={{0,1},{1,2},{2,3},{3,4},{4,5},{5,6},{6,7},{7,8},{8,9},{9,10},{10,1... | collective-permute-start | bytes 86024 | tf_op jit(solution)/shard_map/ppermute | solution.py:423
  13.1 2.6 %shard_map.96 = (f32[3,16,32,128]{3,2,1,0:T(8,128)S(1)}, f32[3,24,8,128]{3,2,1,0:T(8,128)S(1)}, f32[3,24,8,128]{3,2,1,0:T(8,128)S(1)}, f32[3,6,32,128]{3,2,1,0:T(8,128)S(1)}) custom-call(f32[3,16,32,128]{3,2,1,0:T(8,128)S(1)} %get-tuple-element.24.p0_in, f32[3,16,32,128]{3,2,1,0:T(8,128)S(1)} %get-tuple-element.25.cs_in), custom_call_target="tpu_custom_call" | custom-call | flops 33554432 | bytes 3244032 | tf_op jit(solution)/shard_map/pallas_call | solution.py:402
  15.7 0.0 copy-done.3
  15.7 0.0 copy-done.2
  15.7 1.1 %shard_map.97 = (bf16[256,4096]{1,0:T(8,128)(2,1)S(1)}, bf16[4096,128]{1,0:T(8,128)(2,1)S(1)}) custom-call(s32[1,4096]{1,0:T(1,128)S(1)} %bitcast.3, s32[1,4096]{1,0:T(1,128)S(1)} %bitcast.6, f32[3,24,8,128]{3,2,1,0:T(8,128)S(1)} %get-tuple-element.33.after.y_low), custom_call_target="tpu_custom_call" | custom-call | flops 33554432 | bytes 6619136 | tf_op jit(solution)/shard_map/pallas_call | solution.py:402
  16.8 0.0 collective-permute-done.z_next
  16.8 0.0 collective-permute-done.1.z_prev
  16.8 0.3 shard_map.98
  17.1 1.9 %collective-permute-start.2 = (f32[3,3,24,128]{3,2,1,0:T(8,128)S(1)}, f32[3,3,24,128]{3,2,1,0:T(8,128)S(1)}, u32[]{:S(2)}, u32[]{:S(2)}) collective-permute-start(f32[3,3,24,128]{3,2,1,0:T(8,128)S(1)} %get-tuple-element.35), channel_id=1, source_target_pairs={{16,0},{32,16},{48,32},{64,48},{80,64},{96,80},{112,96},{17,1},{33... | collective-permute-start | bytes 331784 | tf_op jit(solution)/shard_map/ppermute | solution.py:419
  19.1 2.4 %collective-permute-start.3 = (f32[3,3,24,128]{3,2,1,0:T(8,128)S(1)}, f32[3,3,24,128]{3,2,1,0:T(8,128)S(1)}, u32[]{:S(2)}, u32[]{:S(2)}) collective-permute-start(f32[3,3,24,128]{3,2,1,0:T(8,128)S(1)} %get-tuple-element.36), channel_id=1, source_target_pairs={{0,16},{16,32},{32,48},{48,64},{64,80},{80,96},{96,112},{1,17},{17... | collective-permute-start | bytes 331784 | tf_op jit(solution)/shard_map/ppermute | solution.py:423
  21.5 0.0 collective-permute-done.2.y_next
  21.5 3.6 %collective-permute-done.3.y_prev = f32[3,3,24,128]{3,2,1,0:T(8,128)S(1)} collective-permute-done((f32[3,3,24,128]{3,2,1,0:T(8,128)S(1)}, f32[3,3,24,128]{3,2,1,0:T(8,128)S(1)}, u32[]{:S(2)}, u32[]{:S(2)}) %collective-permute-start.3) | collective-permute-done | bytes 110624 | tf_op jit(solution)/shard_map/ppermute | solution.py:423
  25.1 0.2 shard_map.100
  25.3 0.0 copy-start
  25.3 2.6 %collective-permute-start.4 = (f32[3,3,32,128]{3,2,1,0:T(8,128)S(1)}, f32[3,3,32,128]{3,2,1,0:T(8,128)S(1)}, u32[]{:S(2)}, u32[]{:S(2)}) collective-permute-start(f32[3,3,32,128]{3,2,1,0:T(8,128)S(1)} %get-tuple-element.39), channel_id=1, source_target_pairs={{128,0},{256,128},{384,256},{512,384},{640,512},{768,640},{896,768... | collective-permute-start | bytes 442376 | tf_op jit(solution)/shard_map/ppermute | solution.py:419
  27.9 3.4 %collective-permute-start.5 = (f32[3,3,32,128]{3,2,1,0:T(8,128)S(1)}, f32[3,3,32,128]{3,2,1,0:T(8,128)S(1)}, u32[]{:S(2)}, u32[]{:S(2)}) collective-permute-start(f32[3,3,32,128]{3,2,1,0:T(8,128)S(1)} %get-tuple-element.40), channel_id=1, source_target_pairs={{0,128},{128,256},{256,384},{384,512},{512,640},{640,768},{768,896... | collective-permute-start | bytes 442376 | tf_op jit(solution)/shard_map/ppermute | solution.py:423
  31.3 0.0 copy-done.1
  31.3 2.7 %shard_map.99 = (f32[3,16,32,128]{3,2,1,0:T(8,128)}, f32[1,4096]{1,0:T(1,128)S(1)}) custom-call(f32[3,16,32,128]{3,2,1,0:T(8,128)S(1)} %get-tuple-element.26.inner, f32[16,32,128]{2,1,0:T(8,128)S(1)} %get-tuple-element.27.stiffness, f32[56,128]{1,0:T(8,128)S(1)} %collective-permute-done.z_next, f32[56,128]{1,0:T(8,128)S(1)} %collective-permute-done.1.z_prev, ...), custom_call_target="tpu_custom_call" | custom-call | flops 1073741824 | bytes 2195456 | tf_op jit(solution)/shard_map/pallas_call | solution.py:402
  34.1 0.0 collective-permute-done.4.x_next
  34.1 2.1 %collective-permute-done.5.x_prev = f32[3,3,32,128]{3,2,1,0:T(8,128)S(1)} collective-permute-done((f32[3,3,32,128]{3,2,1,0:T(8,128)S(1)}, f32[3,3,32,128]{3,2,1,0:T(8,128)S(1)}, u32[]{:S(2)}, u32[]{:S(2)}) %collective-permute-start.5) | collective-permute-done | bytes 147488 | tf_op jit(solution)/shard_map/ppermute | solution.py:423
  36.2 0.0 copy-done
  36.2 3.3 %shard_map.101 = (f32[3,16,32,128]{3,2,1,0:T(8,128)}, f32[128,128]{1,0:T(8,128)S(1)}) custom-call(f32[3,16,32,128]{3,2,1,0:T(8,128)} %get-tuple-element.37.given, f32[3,16,32,128]{3,2,1,0:T(8,128)S(1)} %get-tuple-element.26.inner, f32[16,32,128]{2,1,0:T(8,128)S(1)} %get-tuple-element.27.stiffness, ...), custom_call_target="tpu_custom_call", output_to_operand_aliasing={{0}: (0, {})} | custom-call | flops 1073741824 | bytes 9781248 | tf_op jit(solution)/shard_map/pallas_call | solution.py:402
  39.5 34.2 %all_to_all.5 = f32[16,8,128]{2,1,0:T(8,128)S(1)} all-to-all(f32[16,8,128]{2,1,0:T(8,128)S(1)} %bitcast.8), channel_id=1, replica_groups=mesh['span'=8,'pitch'=8,'chord'=16] {'chord'}, dimensions={0} | all-to-all | bytes 131072 | tf_op jit(solution)/shard_map/all_to_all | solution.py:512
  73.7 0.6 reduce_sum.9
Async XLA Ops:
  0.6 15.1 %copy-start.3 = (s32[4096,1]{0,1:T(1,128)S(1)}, s32[4096,1]{0,1:T(1,128)}, u32[]{:S(2)}) copy-start(s32[4096,1]{0,1:T(1,128)} %param.13) | copy-start | bytes 49156
  0.6 15.1 %copy-start.2 = (s32[4096]{0:T(1024)S(1)}, s32[4096]{0:T(1024)}, u32[]{:S(2)}) copy-start(s32[4096]{0:T(1024)} %param.12) | copy-start | bytes 49156
  0.7 30.7 %copy-start.1 = (f32[3,4096]{1,0:T(4,128)S(1)}, f32[3,4096]{1,0:T(4,128)}, u32[]{:S(2)}) copy-start(f32[3,4096]{1,0:T(4,128)} %wall_normal.3) | copy-start | bytes 147460
  3.3 13.5 %collective-permute-start = (f32[56,128]{1,0:T(8,128)S(1)}, f32[56,128]{1,0:T(8,128)S(1)}, u32[]{:S(2)}, u32[]{:S(2)}) collective-permute-start(f32[56,128]{1,0:T(8,128)S(1)} %get-tuple-element.28), channel_id=1, source_target_pairs={{1,0},{2,1},{3,2},{4,3},{5,4},{6,5},{7,6},{8,7},{9,8},{10,9},{11,1... | collective-permute-start | bytes 86024 | tf_op jit(solution)/shard_map/ppermute | solution.py:419
  4.6 12.2 %collective-permute-start.1 = (f32[56,128]{1,0:T(8,128)S(1)}, f32[56,128]{1,0:T(8,128)S(1)}, u32[]{:S(2)}, u32[]{:S(2)}) collective-permute-start(f32[56,128]{1,0:T(8,128)S(1)} %get-tuple-element.29), channel_id=1, source_target_pairs={{0,1},{1,2},{2,3},{3,4},{4,5},{5,6},{6,7},{7,8},{8,9},{9,10},{10,1... | collective-permute-start | bytes 86024 | tf_op jit(solution)/shard_map/ppermute | solution.py:423
  17.1 4.3 %collective-permute-start.2 = (f32[3,3,24,128]{3,2,1,0:T(8,128)S(1)}, f32[3,3,24,128]{3,2,1,0:T(8,128)S(1)}, u32[]{:S(2)}, u32[]{:S(2)}) collective-permute-start(f32[3,3,24,128]{3,2,1,0:T(8,128)S(1)} %get-tuple-element.35), channel_id=1, source_target_pairs={{16,0},{32,16},{48,32},{64,48},{80,64},{96,80},{112,96},{17,1},{33... | collective-permute-start | bytes 331784 | tf_op jit(solution)/shard_map/ppermute | solution.py:419
  19.1 6.1 %collective-permute-start.3 = (f32[3,3,24,128]{3,2,1,0:T(8,128)S(1)}, f32[3,3,24,128]{3,2,1,0:T(8,128)S(1)}, u32[]{:S(2)}, u32[]{:S(2)}) collective-permute-start(f32[3,3,24,128]{3,2,1,0:T(8,128)S(1)} %get-tuple-element.36), channel_id=1, source_target_pairs={{0,16},{16,32},{32,48},{48,64},{64,80},{80,96},{96,112},{1,17},{17... | collective-permute-start | bytes 331784 | tf_op jit(solution)/shard_map/ppermute | solution.py:423
  25.3 10.8 %copy-start = (f32[8,4096]{1,0:T(8,128)S(1)}, f32[8,4096]{1,0:T(8,128)}, u32[]{:S(2)}) copy-start(f32[8,4096]{1,0:T(8,128)} %mode_shape.1) | copy-start | bytes 393220
  25.3 8.7 %collective-permute-start.4 = (f32[3,3,32,128]{3,2,1,0:T(8,128)S(1)}, f32[3,3,32,128]{3,2,1,0:T(8,128)S(1)}, u32[]{:S(2)}, u32[]{:S(2)}) collective-permute-start(f32[3,3,32,128]{3,2,1,0:T(8,128)S(1)} %get-tuple-element.39), channel_id=1, source_target_pairs={{128,0},{256,128},{384,256},{512,384},{640,512},{768,640},{896,768... | collective-permute-start | bytes 442376 | tf_op jit(solution)/shard_map/ppermute | solution.py:419
  27.9 8.2 %collective-permute-start.5 = (f32[3,3,32,128]{3,2,1,0:T(8,128)S(1)}, f32[3,3,32,128]{3,2,1,0:T(8,128)S(1)}, u32[]{:S(2)}, u32[]{:S(2)}) collective-permute-start(f32[3,3,32,128]{3,2,1,0:T(8,128)S(1)} %get-tuple-element.40), channel_id=1, source_target_pairs={{0,128},{128,256},{256,384},{384,512},{512,640},{640,768},{768,896... | collective-permute-start | bytes 442376 | tf_op jit(solution)/shard_map/ppermute | solution.py:423

commit v6 on v5

--- a/solution.py
+++ b/solution.py
@@ -152,7 +152,7 @@
         out[3 * HALF : 56, :] = jnp.zeros((56 - 3 * HALF, CZ), jnp.float32)
 
 
-def sweep_kernel(p0_in, cs_in, inner, y_low, y_high, x_out, p0, p1, p2, q, cs):
+def sweep_kernel(p0_in, cs_in, inner, y_low, y_high, x_out, core, p0, p1, p2, q, cs):
     x_lo, x_hi, y_lo, y_hi, z_lo, z_hi = open_sides()
     shape = (GY, CZ)
     row, lane = iota(shape, 0), iota(shape, 1)
@@ -218,6 +218,8 @@
     for i, x in enumerate((1, 2, 3, 20, 21, 22)):
         for c, value in enumerate(third(x)):
             x_out[c, i] = value
+            if i >= 3:
+                core[c, i - 3] = value[8:24, :]
 
     def middle(x, carry):
         for c, value in enumerate(third(x)):
@@ -268,16 +270,25 @@
 
 def span_kernel(x_out, z_next, z_prev, y_next, y_prev, low, high, columns):
     unpack(z_next, z_prev, columns)
+    lane = iota((CY // 2, CZ), 1)
+    packed = jnp.zeros((CY // 2, CZ), jnp.float32)
+    for c in range(3):
+        placed = pltpu.roll(columns[c, 16:32, :], 12 * c + CZ - 6 * 18, 1)
+        packed = jnp.where((lane >= 12 * c) & (lane < 12 * (c + 1)), placed, packed)
+    high[9] = packed
     for c in range(3):
         for i, x in enumerate((1, 2, 3, 20, 21, 22)):
-            out, j = (low, i) if i < 3 else (high, i - 3)
             value = x_out[c, i]
             if 2 <= x < 22:
                 value = value + chord_part(columns, c, x, 8, CY)
-            out[c, j] = value
             bottom, top = pitch_rows(y_next, y_prev, c, x)
-            out[c, j, 0:8, :] += bottom
-            out[c, j, 24:32, :] += top
+            if i < 3:
+                low[c, i, 0:8, :] = value[0:8, :] + bottom
+                low[c, i, 8:24, :] = value[8:24, :]
+                low[c, i, 24:32, :] = value[24:32, :] + top
+            else:
+                high[3 * c + i - 3, 0:8, :] = value[0:8, :] + bottom
+                high[3 * c + i - 3, 8:16, :] = value[24:32, :] + top
 
 
 def finish_planes(planes, inner, z_next, z_prev, y_next, y_prev, stiffness, columns, values, part, field, span):
@@ -348,13 +359,19 @@
 
 
 def wall_kernel(
-    given, inner, stiffness, z_next, z_prev, y_next, y_prev, x_next, x_prev, share,
+    given, inner, stiffness, z_next, z_prev, y_next, y_prev, x_next, x_prev, x_core, share,
     wall_cell, patch_owner, wall_normal, mode_shape, planes, patches,
     adjoint, sums, columns, values, part, field, sems,
 ):
     def span(value, c, x):
         if x < 3:
-            return value + x_prev[c, x]
+            rows = x_core[c, x]
+            if x < 2:
+                lane = iota(rows.shape, 1)
+                placed = pltpu.roll(x_prev[9], CZ - 3 - 12 * c - 6 * x, 1)
+                rows = rows + jnp.where((lane < 3) | (lane >= CZ - 3), placed, 0.0)
+            parts = [x_prev[3 * c + x, 0:8, :], rows, x_prev[3 * c + x, 8:16, :]]
+            return value + jnp.concatenate(parts, axis=0)
         if x >= CX - 3:
             return value + x_next[c, x - (CX - 3)]
         return value
@@ -451,9 +468,9 @@
         ),
     )
     z_prev, z_next = from_previous(z_high, "chord"), from_next(z_low, "chord")
-    inner, y_low, y_high, x_out = call(
+    inner, y_low, y_high, x_out, core = call(
         sweep_kernel,
-        (block, (3, GX, 8, CZ), (3, GX, 8, CZ), (3, 6, CY, CZ)),
+        (block, (3, GX, 8, CZ), (3, GX, 8, CZ), (3, 6, CY, CZ), (3, 3, CY // 2, CZ)),
         (p0, cs),
         "vv",
         scratch=(grown,) * 5,
@@ -473,10 +490,15 @@
     low, high = call(
         pitch_kernel, (slab, slab), (y_low, y_high, z_next, z_prev), "vvvv", scratch=(columns,)
     )
+    x_core = from_previous(core, "span")
     y_next, y_prev = from_next(low, "pitch"), from_previous(high, "pitch")
-    slab = (3, 3, CY, CZ)
+    y_next, y_prev, x_core = lax.optimization_barrier((y_next, y_prev, x_core))
     low, high = call(
-        span_kernel, (slab, slab), (x_out, z_next, z_prev, y_next, y_prev), "vvvvv", scratch=(columns,)
+        span_kernel,
+        ((3, 3, CY, CZ), (10, CY // 2, CZ)),
+        (x_out, z_next, z_prev, y_next, y_prev),
+        "vvvvv",
+        scratch=(columns,),
     )
     x_next, x_prev = from_next(low, "span"), from_previous(high, "span")
     given = (z_next, z_prev, y_next, y_prev)
@@ -499,10 +521,10 @@
         wall_kernel,
         (block, (CHORD * MODES, PATCH_DEV)),
         (
-            adjoint, inner, stiffness, *given, x_next, x_prev, share,
+            adjoint, inner, stiffness, *given, x_next, x_prev, x_core, share,
             cells, owners, wall_normal, mode_shape, planes, patches,
         ),
-        "hvvvvvvvvvvvvvvv",
+        "hvvvvvvvvvvvvvvvv",
         scratch=(*work, pltpu.SemaphoreType.DMA((2,))),
         out_spaces="hv",
         aliases={0: 0},

time: 74.6 us -> 78.6 us (1.054)
  the two profiles are of different devices: /device:TPU:24 before, /device:TPU:10 now
where the time goes in v6:
time: 78.6 us; the launch traced here: 78.3 us
  blocking collectives  34.2 us (44%)
  starting transfers between devices  23.5 us (30%)
  Pallas kernels  13 us (17%)
  waiting for transfers between devices  6.2 us (8%)
  between operations  0.81 us (1%)
    all_to_all x1, blocking collectives, body(): lax.all_to_all(sums, 'chord', split_axis=0, concat_axis=0, tiled=True)  34.2 us
    ppermute x4, starting transfers between devices, from_previous(): return lax.ppermute(high, axis, pairs(axis))  16.3 us
    pallas_call x7, Pallas kernels, call(): pl.pallas_call(kernel, out_shape=shapes, in_specs=[spec[space] for space...  13 us
    ppermute x3, starting transfers between devices, from_next(): return lax.ppermute(low, axis, [(j, i) for i, j in pairs(axis)])  7.27 us
    ppermute x4, waiting for transfers between devices, from_previous(): return lax.ppermute(high, axis, pairs(axis))  6.19 us
  transfers between devices with their start and end apart: 7, of which 2 were waited for; matrix products, arithmetic and copies ran while one was open for 0% of the time, Pallas kernels for 8%

profile of v6, /device:TPU:10, one launch (start us, length us, event | category | flops | bytes accessed | tf_op | source)
XLA Modules:
  0.0 78.3 jit_solution(13894357491731389867)
XLA Ops:
  0.6 0.0 copy-start.3
  0.6 0.0 copy-start.2
  0.7 0.0 copy-start.1
  0.7 2.6 %shard_map.95 = (f32[3,16,32,128]{3,2,1,0:T(8,128)S(1)}, f32[3,16,32,128]{3,2,1,0:T(8,128)S(1)}, f32[16,32,128]{2,1,0:T(8,128)S(1)}, f32[56,128]{1,0:T(8,128)S(1)}, f32[56,128]{1,0:T(8,128)S(1)}) custom-call(f32[8]{0:T(128)} %table_in.1, f32[3,16,32,128]{3,2,1,0:T(8,128)} %start.1, f32[3,16,32,128]{3,2,1,0:T(8,128)} %source.1, s32[16,32,128]{2,1,0:T(8,128)} %classes.1), custom_call_target="tpu_custom_call" | custom-call | bytes 3727392 | tf_op jit(solution)/shard_map/pallas_call | solution.py:419
  3.3 1.3 %collective-permute-start = (f32[56,128]{1,0:T(8,128)S(1)}, f32[56,128]{1,0:T(8,128)S(1)}, u32[]{:S(2)}, u32[]{:S(2)}) collective-permute-start(f32[56,128]{1,0:T(8,128)S(1)} %get-tuple-element.32), channel_id=1, source_target_pairs={{1,0},{2,1},{3,2},{4,3},{5,4},{6,5},{7,6},{8,7},{9,8},{10,9},{11,1... | collective-permute-start | bytes 86024 | tf_op jit(solution)/shard_map/ppermute | solution.py:436
  4.6 8.8 %collective-permute-start.1 = (f32[56,128]{1,0:T(8,128)S(1)}, f32[56,128]{1,0:T(8,128)S(1)}, u32[]{:S(2)}, u32[]{:S(2)}) collective-permute-start(f32[56,128]{1,0:T(8,128)S(1)} %get-tuple-element.33), channel_id=1, source_target_pairs={{0,1},{1,2},{2,3},{3,4},{4,5},{5,6},{6,7},{7,8},{8,9},{9,10},{10,1... | collective-permute-start | bytes 86024 | tf_op jit(solution)/shard_map/ppermute | solution.py:440
  13.4 2.6 %shard_map.96 = (f32[3,16,32,128]{3,2,1,0:T(8,128)S(1)}, f32[3,24,8,128]{3,2,1,0:T(8,128)S(1)}, f32[3,24,8,128]{3,2,1,0:T(8,128)S(1)}, f32[3,6,32,128]{3,2,1,0:T(8,128)S(1)}, f32[3,3,16,128]{3,2,1,0:T(8,128)S(1)}) custom-call(f32[3,16,32,128]{3,2,1,0:T(8,128)S(1)} %get-tuple-element.28.p0_in, f32[3,16,32,128]{3,2,1,0:T(8,128)S(1)} %get-tuple-element.29.cs_in), custom_call_target="tpu_custom_call" | custom-call | flops 33554432 | bytes 3317760 | tf_op jit(solution)/shard_map/pallas_call | solution.py:419
  16.1 0.0 copy-done.3
  16.1 0.0 copy-done.2
  16.1 1.1 %shard_map.97 = (bf16[256,4096]{1,0:T(8,128)(2,1)S(1)}, bf16[4096,128]{1,0:T(8,128)(2,1)S(1)}) custom-call(s32[1,4096]{1,0:T(1,128)S(1)} %bitcast.3, s32[1,4096]{1,0:T(1,128)S(1)} %bitcast.6, f32[3,24,8,128]{3,2,1,0:T(8,128)S(1)} %get-tuple-element.37.after.y_low), custom_call_target="tpu_custom_call" | custom-call | flops 33554432 | bytes 6619136 | tf_op jit(solution)/shard_map/pallas_call | solution.py:419
  17.2 0.0 collective-permute-done.z_next
  17.2 0.0 collective-permute-done.1.z_prev
  17.2 0.3 shard_map.98
  17.5 1.3 %collective-permute-start.2 = (f32[3,3,24,128]{3,2,1,0:T(8,128)S(1)}, f32[3,3,24,128]{3,2,1,0:T(8,128)S(1)}, u32[]{:S(2)}, u32[]{:S(2)}) collective-permute-start(f32[3,3,24,128]{3,2,1,0:T(8,128)S(1)} %get-tuple-element.39), channel_id=1, source_target_pairs={{16,0},{32,16},{48,32},{64,48},{80,64},{96,80},{112,96},{17,1},{33... | collective-permute-start | bytes 331784 | tf_op jit(solution)/shard_map/ppermute | solution.py:436
  18.8 3.0 %collective-permute-start.3 = (f32[3,3,24,128]{3,2,1,0:T(8,128)S(1)}, f32[3,3,24,128]{3,2,1,0:T(8,128)S(1)}, u32[]{:S(2)}, u32[]{:S(2)}) collective-permute-start(f32[3,3,24,128]{3,2,1,0:T(8,128)S(1)} %get-tuple-element.40), channel_id=1, source_target_pairs={{0,16},{16,32},{32,48},{48,64},{64,80},{80,96},{96,112},{1,17},{17... | collective-permute-start | bytes 331784 | tf_op jit(solution)/shard_map/ppermute | solution.py:440
  21.8 2.5 %collective-permute-start.4 = (f32[3,3,16,128]{3,2,1,0:T(8,128)S(1)}, f32[3,3,16,128]{3,2,1,0:T(8,128)S(1)}, u32[]{:S(2)}, u32[]{:S(2)}) collective-permute-start(f32[3,3,16,128]{3,2,1,0:T(8,128)S(1)} %get-tuple-element.41), channel_id=1, source_target_pairs={{0,128},{128,256},{256,384},{384,512},{512,640},{640,768},{768,896... | collective-permute-start | bytes 221192 | tf_op jit(solution)/shard_map/ppermute | solution.py:440
  24.3 4.5 %collective-permute-done.4.x_core = f32[3,3,16,128]{3,2,1,0:T(8,128)S(1)} collective-permute-done((f32[3,3,16,128]{3,2,1,0:T(8,128)S(1)}, f32[3,3,16,128]{3,2,1,0:T(8,128)S(1)}, u32[]{:S(2)}, u32[]{:S(2)}) %collective-permute-start.4) | collective-permute-done | bytes 73760 | tf_op jit(solution)/shard_map/ppermute | solution.py:440
  28.8 0.0 collective-permute-done.2.y_next
  28.8 0.0 collective-permute-done.3.y_prev
  28.8 0.2 shard_map.100
  29.1 0.0 copy-start
  29.1 4.7 %collective-permute-start.5 = (f32[3,3,32,128]{3,2,1,0:T(8,128)S(1)}, f32[3,3,32,128]{3,2,1,0:T(8,128)S(1)}, u32[]{:S(2)}, u32[]{:S(2)}) collective-permute-start(f32[3,3,32,128]{3,2,1,0:T(8,128)S(1)} %get-tuple-element.46), channel_id=1, source_target_pairs={{128,0},{256,128},{384,256},{512,384},{640,512},{768,640},{896,768... | collective-permute-start | bytes 442376 | tf_op jit(solution)/shard_map/ppermute | solution.py:436
  33.8 1.9 %collective-permute-start.6 = (f32[10,16,128]{2,1,0:T(8,128)S(1)}, f32[10,16,128]{2,1,0:T(8,128)S(1)}, u32[]{:S(2)}, u32[]{:S(2)}) collective-permute-start(f32[10,16,128]{2,1,0:T(8,128)S(1)} %get-tuple-element.47), channel_id=1, source_target_pairs={{0,128},{128,256},{256,384},{384,512},{512,640},{640,768},{768,896... | collective-permute-start | bytes 245768 | tf_op jit(solution)/shard_map/ppermute | solution.py:440
  35.7 0.0 copy-done.1
  35.7 2.7 %shard_map.99 = (f32[3,16,32,128]{3,2,1,0:T(8,128)}, f32[1,4096]{1,0:T(1,128)S(1)}) custom-call(f32[3,16,32,128]{3,2,1,0:T(8,128)S(1)} %get-tuple-element.30.inner, f32[16,32,128]{2,1,0:T(8,128)S(1)} %get-tuple-element.31.stiffness, f32[56,128]{1,0:T(8,128)S(1)} %collective-permute-done.z_next, f32[56,128]{1,0:T(8,128)S(1)} %collective-permute-done.1.z_prev, ...), custom_call_target="tpu_custom_call" | custom-call | flops 1073741824 | bytes 2195456 | tf_op jit(solution)/shard_map/pallas_call | solution.py:419
  38.4 1.7 %collective-permute-done.6.x_prev = f32[10,16,128]{2,1,0:T(8,128)S(1)} collective-permute-done((f32[10,16,128]{2,1,0:T(8,128)S(1)}, f32[10,16,128]{2,1,0:T(8,128)S(1)}, u32[]{:S(2)}, u32[]{:S(2)}) %collective-permute-start.6) | collective-permute-done | bytes 81952 | tf_op jit(solution)/shard_map/ppermute | solution.py:440
  40.1 0.0 collective-permute-done.5.x_next
  40.1 0.0 copy-done
  40.1 3.4 %shard_map.101 = (f32[3,16,32,128]{3,2,1,0:T(8,128)}, f32[128,128]{1,0:T(8,128)S(1)}) custom-call(f32[3,16,32,128]{3,2,1,0:T(8,128)} %get-tuple-element.44.given, f32[3,16,32,128]{3,2,1,0:T(8,128)S(1)} %get-tuple-element.30.inner, f32[16,32,128]{2,1,0:T(8,128)S(1)} %get-tuple-element.31.stiffness, ...), custom_call_target="tpu_custom_call", output_to_operand_aliasing={{0}: (0, {})} | custom-call | flops 1073741824 | bytes 9789440 | tf_op jit(solution)/shard_map/pallas_call | solution.py:419
  43.5 34.2 %all_to_all.5 = f32[16,8,128]{2,1,0:T(8,128)S(1)} all-to-all(f32[16,8,128]{2,1,0:T(8,128)S(1)} %bitcast.8), channel_id=1, replica_groups=mesh['span'=8,'pitch'=8,'chord'=16] {'chord'}, dimensions={0} | all-to-all | bytes 131072 | tf_op jit(solution)/shard_map/all_to_all | solution.py:534
  77.7 0.6 reduce_sum.9
Async XLA Ops:
  0.6 15.4 %copy-start.3 = (s32[4096,1]{0,1:T(1,128)S(1)}, s32[4096,1]{0,1:T(1,128)}, u32[]{:S(2)}) copy-start(s32[4096,1]{0,1:T(1,128)} %param.13) | copy-start | bytes 49156
  0.6 15.4 %copy-start.2 = (s32[4096]{0:T(1024)S(1)}, s32[4096]{0:T(1024)}, u32[]{:S(2)}) copy-start(s32[4096]{0:T(1024)} %param.12) | copy-start | bytes 49156
  0.7 35.0 %copy-start.1 = (f32[3,4096]{1,0:T(4,128)S(1)}, f32[3,4096]{1,0:T(4,128)}, u32[]{:S(2)}) copy-start(f32[3,4096]{1,0:T(4,128)} %wall_normal.3) | copy-start | bytes 147460
  3.3 13.9 %collective-permute-start = (f32[56,128]{1,0:T(8,128)S(1)}, f32[56,128]{1,0:T(8,128)S(1)}, u32[]{:S(2)}, u32[]{:S(2)}) collective-permute-start(f32[56,128]{1,0:T(8,128)S(1)} %get-tuple-element.32), channel_id=1, source_target_pairs={{1,0},{2,1},{3,2},{4,3},{5,4},{6,5},{7,6},{8,7},{9,8},{10,9},{11,1... | collective-permute-start | bytes 86024 | tf_op jit(solution)/shard_map/ppermute | solution.py:436
  4.6 12.6 %collective-permute-start.1 = (f32[56,128]{1,0:T(8,128)S(1)}, f32[56,128]{1,0:T(8,128)S(1)}, u32[]{:S(2)}, u32[]{:S(2)}) collective-permute-start(f32[56,128]{1,0:T(8,128)S(1)} %get-tuple-element.33), channel_id=1, source_target_pairs={{0,1},{1,2},{2,3},{3,4},{4,5},{5,6},{6,7},{7,8},{8,9},{9,10},{10,1... | collective-permute-start | bytes 86024 | tf_op jit(solution)/shard_map/ppermute | solution.py:440
  17.5 11.4 %collective-permute-start.2 = (f32[3,3,24,128]{3,2,1,0:T(8,128)S(1)}, f32[3,3,24,128]{3,2,1,0:T(8,128)S(1)}, u32[]{:S(2)}, u32[]{:S(2)}) collective-permute-start(f32[3,3,24,128]{3,2,1,0:T(8,128)S(1)} %get-tuple-element.39), channel_id=1, source_target_pairs={{16,0},{32,16},{48,32},{64,48},{80,64},{96,80},{112,96},{17,1},{33... | collective-permute-start | bytes 331784 | tf_op jit(solution)/shard_map/ppermute | solution.py:436
  18.8 10.1 %collective-permute-start.3 = (f32[3,3,24,128]{3,2,1,0:T(8,128)S(1)}, f32[3,3,24,128]{3,2,1,0:T(8,128)S(1)}, u32[]{:S(2)}, u32[]{:S(2)}) collective-permute-start(f32[3,3,24,128]{3,2,1,0:T(8,128)S(1)} %get-tuple-element.40), channel_id=1, source_target_pairs={{0,16},{16,32},{32,48},{48,64},{64,80},{80,96},{96,112},{1,17},{17... | collective-permute-start | bytes 331784 | tf_op jit(solution)/shard_map/ppermute | solution.py:440
  21.8 7.0 %collective-permute-start.4 = (f32[3,3,16,128]{3,2,1,0:T(8,128)S(1)}, f32[3,3,16,128]{3,2,1,0:T(8,128)S(1)}, u32[]{:S(2)}, u32[]{:S(2)}) collective-permute-start(f32[3,3,16,128]{3,2,1,0:T(8,128)S(1)} %get-tuple-element.41), channel_id=1, source_target_pairs={{0,128},{128,256},{256,384},{384,512},{512,640},{640,768},{768,896... | collective-permute-start | bytes 221192 | tf_op jit(solution)/shard_map/ppermute | solution.py:440
  29.1 11.0 %copy-start = (f32[8,4096]{1,0:T(8,128)S(1)}, f32[8,4096]{1,0:T(8,128)}, u32[]{:S(2)}) copy-start(f32[8,4096]{1,0:T(8,128)} %mode_shape.1) | copy-start | bytes 393220
  29.1 11.0 %collective-permute-start.5 = (f32[3,3,32,128]{3,2,1,0:T(8,128)S(1)}, f32[3,3,32,128]{3,2,1,0:T(8,128)S(1)}, u32[]{:S(2)}, u32[]{:S(2)}) collective-permute-start(f32[3,3,32,128]{3,2,1,0:T(8,128)S(1)} %get-tuple-element.46), channel_id=1, source_target_pairs={{128,0},{256,128},{384,256},{512,384},{640,512},{768,640},{896,768... | collective-permute-start | bytes 442376 | tf_op jit(solution)/shard_map/ppermute | solution.py:436
  33.8 6.3 %collective-permute-start.6 = (f32[10,16,128]{2,1,0:T(8,128)S(1)}, f32[10,16,128]{2,1,0:T(8,128)S(1)}, u32[]{:S(2)}, u32[]{:S(2)}) collective-permute-start(f32[10,16,128]{2,1,0:T(8,128)S(1)} %get-tuple-element.47), channel_id=1, source_target_pairs={{0,128},{128,256},{256,384},{384,512},{512,640},{640,768},{768,896... | collective-permute-start | bytes 245768 | tf_op jit(solution)/shard_map/ppermute | solution.py:440

commit v7 on v5

--- a/solution.py
+++ b/solution.py
@@ -25,8 +25,9 @@
 GX, GY = 24, 48
 FIRST, MIDDLE, LAST = 6, 24, 42
 HALF = MIDDLE - FIRST
+SLAB = 168
 ROWS = 2048
-STEP_X = 4
+STEP_X = 8
 
 VMEM = pl.BlockSpec(memory_space=pltpu.VMEM)
 SMEM = pl.BlockSpec(memory_space=pltpu.SMEM)
@@ -71,18 +72,18 @@
 ):
     table_copy = pltpu.make_async_copy(table_in, table, table_sem)
     table_copy.start()
-    copies = []
+    early, late = [], []
     for g in range(CX // STEP_X):
         part = pl.ds(g * STEP_X, STEP_X)
-        copies.append(
+        early.append(
             [
                 pltpu.make_async_copy(classes.at[part], c_in.at[part], sems.at[0, g]),
                 pltpu.make_async_copy(start.at[:, part], y_in.at[:, part], sems.at[1, g]),
-                pltpu.make_async_copy(source.at[:, part], s_in.at[:, part], sems.at[2, g]),
             ]
         )
-        for copy in copies[-1]:
-            copy.start()
+        late.append(pltpu.make_async_copy(source.at[:, part], s_in.at[:, part], sems.at[2, g]))
+    for copy in [copy for group in early for copy in group] + late:
+        copy.start()
     x_lo, x_hi, y_lo, y_hi, z_lo, z_hi = open_sides()
 
     lane = iota((CY, CZ), 1)
@@ -92,18 +93,14 @@
     table_copy.wait()
     for x in range(CX):
         if x % STEP_X == 0:
-            for copy in copies[x // STEP_X]:
+            for copy in early[x // STEP_X]:
                 copy.wait()
         k = pick(table, c_in[x])
         stiffness[x] = k
-        shift = (6 * (x + 2) + 3) % CZ
         for c in range(3):
             value = k * y_in[c, x]
-            push = STEP * s_in[c, x]
             p0[c, x] = value
-            cs[c, x] = push
-            values[c] = values[c] + pltpu.roll(jnp.where(edge, value, 0.0), shift, 1)
-            pushes[c] = pushes[c] + pltpu.roll(jnp.where(edge, push, 0.0), shift, 1)
+            values[c] = values[c] + pltpu.roll(jnp.where(edge, value, 0.0), (6 * (x + 2) + 3) % CZ, 1)
 
     shape = (GY, CZ)
     plane, slot = slots(shape)
@@ -117,26 +114,37 @@
     pad = jnp.zeros((8, CZ), jnp.float32)
     _, packed_slot = slots((HALF, CZ))
 
+    def flat(v, c):
+        planes = pltpu.roll(v, 6, 1) + pltpu.roll(v, CZ - 6, 1)
+        lines = pltpu.roll(v, 1, 0) + pltpu.roll(v, GY - 1, 0)
+        return (OWN * v + PULL[c][0] * planes + PULL[c][1] * lines) * side
+
+    def beside(v, c):
+        before = jnp.where(no_before, 0.0, pltpu.roll(v, 1, 1))
+        after = jnp.where(no_after, 0.0, pltpu.roll(v, CZ - 1, 1))
+        return PULL[c][2] * (before + after)
+
+    v0s = [jnp.concatenate([pad, values[c], pad], axis=0) for c in range(3)]
+    t1s = [flat(v0s[c], c) for c in range(3)]
+    unpushed = [t1s[c] + beside(v0s[c], c) for c in range(3)]
+    twice = [flat(t1s[c], c) for c in range(3)]
+
+    for x in range(CX):
+        if x % STEP_X == 0:
+            late[x // STEP_X].wait()
+        for c in range(3):
+            push = STEP * s_in[c, x]
+            cs[c, x] = push
+            pushes[c] = pushes[c] + pltpu.roll(jnp.where(edge, push, 0.0), (6 * (x + 2) + 3) % CZ, 1)
+
     for c in range(3):
         along = PULL[c][2]
-
-        def flat(v):
-            planes = pltpu.roll(v, 6, 1) + pltpu.roll(v, CZ - 6, 1)
-            lines = pltpu.roll(v, 1, 0) + pltpu.roll(v, GY - 1, 0)
-            return (OWN * v + PULL[c][0] * planes + PULL[c][1] * lines) * side
-
-        def beside(v):
-            before = jnp.where(no_before, 0.0, pltpu.roll(v, 1, 1))
-            after = jnp.where(no_after, 0.0, pltpu.roll(v, CZ - 1, 1))
-            return along * (before + after)
-
-        v0 = jnp.concatenate([pad, values[c], pad], axis=0)
+        v0, t1 = v0s[c], t1s[c]
         push = jnp.concatenate([pad, pushes[c], pad], axis=0)
-        t1 = flat(v0)
-        v1 = t1 + beside(v0) + push
-        t2 = flat(v1)
-        v2 = t2 + beside(v1) + push + (along * along) * gate * v0
-        out1 = along * gate * (flat(t1) + t2 + v2 + (along * along) * v0)
+        v1 = unpushed[c] + push
+        t2 = flat(v1, c)
+        v2 = t2 + beside(v1, c) + push + (along * along) * gate * v0
+        out1 = along * gate * (twice[c] + t2 + v2 + (along * along) * v0)
         out2 = (along * along) * gate * (2.0 * t1 + v1)
         out3 = (along * along * along) * gate * v0
         given = jnp.zeros(shape, jnp.float32)
@@ -244,6 +252,12 @@
     return jnp.where((lane < 3) | (lane >= CZ - 3), placed, 0.0)
 
 
+def slab_row(c, far, x):
+    place = x - (1 + far)
+    count = 22 - 2 * far
+    return 54 * c + (0, 20, 38)[far - 1] + place if 0 <= place < count else None
+
+
 def pitch_kernel(y_low, y_high, z_next, z_prev, low, high, columns):
     unpack(z_next, z_prev, columns)
     for c in range(3):
@@ -253,7 +267,12 @@
                 if 2 <= x < 22:
                     value = value + chord_part(columns, c, x, start, 8)
                 for j in range(3):
-                    out[c, j, x : x + 1, :] = value[first + j : first + j + 1, :]
+                    far = 3 - j if first else j + 1
+                    place = slab_row(c, far, x)
+                    if place is not None:
+                        out[place : place + 1, :] = value[first + j : first + j + 1, :]
+    for out in (low, high):
+        out[SLAB - 6 : SLAB, :] = jnp.zeros((6, CZ), jnp.float32)
 
 
 def pitch_rows(y_next, y_prev, c, x):
@@ -261,8 +280,11 @@
     bottom = jnp.zeros((8, CZ), jnp.float32)
     top = jnp.zeros((8, CZ), jnp.float32)
     for j in range(3):
-        bottom = jnp.where(row == j, y_prev[c, j, x : x + 1, :], bottom)
-        top = jnp.where(row == 5 + j, y_next[c, j, x : x + 1, :], top)
+        low, high = slab_row(c, j + 1, x), slab_row(c, 3 - j, x)
+        if low is not None:
+            bottom = jnp.where(row == j, y_prev[low : low + 1, :], bottom)
+        if high is not None:
+            top = jnp.where(row == 5 + j, y_next[high : high + 1, :], top)
     return bottom, top
 
 
@@ -469,7 +491,7 @@
         kind=jnp.bfloat16,
     )
     y_low, planes, patches = lax.optimization_barrier((y_low, planes, patches))
-    slab = (3, 3, GX, CZ)
+    slab = (SLAB, CZ)
     low, high = call(
         pitch_kernel, (slab, slab), (y_low, y_high, z_next, z_prev), "vvvv", scratch=(columns,)
     )

time: 74.6 us -> 74.3 us (level)
  no operation moved by 1% of the time
where the time goes in v7:
time: 74.3 us; the launch traced here: 74 us
  blocking collectives  34.2 us (46%)
  starting transfers between devices  20 us (27%)
  Pallas kernels  12.8 us (17%)
  waiting for transfers between devices  5.49 us (7%)
  between operations  0.82 us (1%)
    all_to_all x1, blocking collectives, body(): lax.all_to_all(sums, 'chord', split_axis=0, concat_axis=0, tiled=True)  34.2 us
    ppermute x3, starting transfers between devices, from_previous(): return lax.ppermute(high, axis, pairs(axis))  14.3 us
    pallas_call x7, Pallas kernels, call(): pl.pallas_call(kernel, out_shape=shapes, in_specs=[spec[space] for space...  12.8 us
    ppermute x3, starting transfers between devices, from_next(): return lax.ppermute(low, axis, [(j, i) for i, j in pairs(axis)])  5.79 us
    ppermute x3, waiting for transfers between devices, from_previous(): return lax.ppermute(high, axis, pairs(axis))  5.48 us
  transfers between devices with their start and end apart: 6, of which 2 were waited for; matrix products, arithmetic and copies ran while one was open for 0% of the time, Pallas kernels for 9%

profile of v7, /device:TPU:24, one launch (start us, length us, event | category | flops | bytes accessed | tf_op | source)
XLA Modules:
  0.0 74.0 jit_solution(14062132644229892841)
XLA Ops:
  0.6 0.0 copy-start.3
  0.6 0.0 copy-start.2
  0.7 0.0 copy-start.1
  0.7 2.6 %shard_map.95 = (f32[3,16,32,128]{3,2,1,0:T(8,128)S(1)}, f32[3,16,32,128]{3,2,1,0:T(8,128)S(1)}, f32[16,32,128]{2,1,0:T(8,128)S(1)}, f32[56,128]{1,0:T(8,128)S(1)}, f32[56,128]{1,0:T(8,128)S(1)}) custom-call(f32[8]{0:T(128)} %table_in.1, f32[3,16,32,128]{3,2,1,0:T(8,128)} %start.1, f32[3,16,32,128]{3,2,1,0:T(8,128)} %source.1, s32[16,32,128]{2,1,0:T(8,128)} %classes.1), custom_call_target="tpu_custom_call" | custom-call | bytes 3727392 | tf_op jit(solution)/shard_map/pallas_call | solution.py:424
  3.2 1.3 %collective-permute-start = (f32[56,128]{1,0:T(8,128)S(1)}, f32[56,128]{1,0:T(8,128)S(1)}, u32[]{:S(2)}, u32[]{:S(2)}) collective-permute-start(f32[56,128]{1,0:T(8,128)S(1)} %get-tuple-element.28), channel_id=1, source_target_pairs={{1,0},{2,1},{3,2},{4,3},{5,4},{6,5},{7,6},{8,7},{9,8},{10,9},{11,1... | collective-permute-start | bytes 86024 | tf_op jit(solution)/shard_map/ppermute | solution.py:441
  4.5 8.5 %collective-permute-start.1 = (f32[56,128]{1,0:T(8,128)S(1)}, f32[56,128]{1,0:T(8,128)S(1)}, u32[]{:S(2)}, u32[]{:S(2)}) collective-permute-start(f32[56,128]{1,0:T(8,128)S(1)} %get-tuple-element.29), channel_id=1, source_target_pairs={{0,1},{1,2},{2,3},{3,4},{4,5},{5,6},{6,7},{7,8},{8,9},{9,10},{10,1... | collective-permute-start | bytes 86024 | tf_op jit(solution)/shard_map/ppermute | solution.py:445
  13.0 2.6 %shard_map.96 = (f32[3,16,32,128]{3,2,1,0:T(8,128)S(1)}, f32[3,24,8,128]{3,2,1,0:T(8,128)S(1)}, f32[3,24,8,128]{3,2,1,0:T(8,128)S(1)}, f32[3,6,32,128]{3,2,1,0:T(8,128)S(1)}) custom-call(f32[3,16,32,128]{3,2,1,0:T(8,128)S(1)} %get-tuple-element.24.p0_in, f32[3,16,32,128]{3,2,1,0:T(8,128)S(1)} %get-tuple-element.25.cs_in), custom_call_target="tpu_custom_call" | custom-call | flops 33554432 | bytes 3244032 | tf_op jit(solution)/shard_map/pallas_call | solution.py:424
  15.6 0.0 copy-done.3
  15.6 0.0 copy-done.2
  15.6 1.1 %shard_map.97 = (bf16[256,4096]{1,0:T(8,128)(2,1)S(1)}, bf16[4096,128]{1,0:T(8,128)(2,1)S(1)}) custom-call(s32[1,4096]{1,0:T(1,128)S(1)} %bitcast.3, s32[1,4096]{1,0:T(1,128)S(1)} %bitcast.6, f32[3,24,8,128]{3,2,1,0:T(8,128)S(1)} %get-tuple-element.33.after.y_low), custom_call_target="tpu_custom_call" | custom-call | flops 33554432 | bytes 6619136 | tf_op jit(solution)/shard_map/pallas_call | solution.py:424
  16.8 0.0 collective-permute-done.z_next
  16.8 0.0 collective-permute-done.1.z_prev
  16.8 0.3 shard_map.98
  17.1 1.9 %collective-permute-start.2 = (f32[168,128]{1,0:T(8,128)S(1)}, f32[168,128]{1,0:T(8,128)S(1)}, u32[]{:S(2)}, u32[]{:S(2)}) collective-permute-start(f32[168,128]{1,0:T(8,128)S(1)} %get-tuple-element.35), channel_id=1, source_target_pairs={{16,0},{32,16},{48,32},{64,48},{80,64},{96,80},{112,96},{17,1},{33... | collective-permute-start | bytes 258056 | tf_op jit(solution)/shard_map/ppermute | solution.py:441
  19.0 2.4 %collective-permute-start.3 = (f32[168,128]{1,0:T(8,128)S(1)}, f32[168,128]{1,0:T(8,128)S(1)}, u32[]{:S(2)}, u32[]{:S(2)}) collective-permute-start(f32[168,128]{1,0:T(8,128)S(1)} %get-tuple-element.36), channel_id=1, source_target_pairs={{0,16},{16,32},{32,48},{48,64},{64,80},{80,96},{96,112},{1,17},{17... | collective-permute-start | bytes 258056 | tf_op jit(solution)/shard_map/ppermute | solution.py:445
  21.4 0.0 collective-permute-done.2.y_next
  21.4 3.4 %collective-permute-done.3.y_prev = f32[168,128]{1,0:T(8,128)S(1)} collective-permute-done((f32[168,128]{1,0:T(8,128)S(1)}, f32[168,128]{1,0:T(8,128)S(1)}, u32[]{:S(2)}, u32[]{:S(2)}) %collective-permute-start.3) | collective-permute-done | bytes 86048 | tf_op jit(solution)/shard_map/ppermute | solution.py:445
  24.8 0.2 shard_map.100
  25.0 0.0 copy-start
  25.0 2.6 %collective-permute-start.4 = (f32[3,3,32,128]{3,2,1,0:T(8,128)S(1)}, f32[3,3,32,128]{3,2,1,0:T(8,128)S(1)}, u32[]{:S(2)}, u32[]{:S(2)}) collective-permute-start(f32[3,3,32,128]{3,2,1,0:T(8,128)S(1)} %get-tuple-element.39), channel_id=1, source_target_pairs={{128,0},{256,128},{384,256},{512,384},{640,512},{768,640},{896,768... | collective-permute-start | bytes 442376 | tf_op jit(solution)/shard_map/ppermute | solution.py:441
  27.6 3.4 %collective-permute-start.5 = (f32[3,3,32,128]{3,2,1,0:T(8,128)S(1)}, f32[3,3,32,128]{3,2,1,0:T(8,128)S(1)}, u32[]{:S(2)}, u32[]{:S(2)}) collective-permute-start(f32[3,3,32,128]{3,2,1,0:T(8,128)S(1)} %get-tuple-element.40), channel_id=1, source_target_pairs={{0,128},{128,256},{256,384},{384,512},{512,640},{640,768},{768,896... | collective-permute-start | bytes 442376 | tf_op jit(solution)/shard_map/ppermute | solution.py:445
  31.0 0.0 copy-done.1
  31.0 2.7 %shard_map.99 = (f32[3,16,32,128]{3,2,1,0:T(8,128)}, f32[1,4096]{1,0:T(1,128)S(1)}) custom-call(f32[3,16,32,128]{3,2,1,0:T(8,128)S(1)} %get-tuple-element.26.inner, f32[16,32,128]{2,1,0:T(8,128)S(1)} %get-tuple-element.27.stiffness, f32[56,128]{1,0:T(8,128)S(1)} %collective-permute-done.z_next, f32[56,128]{1,0:T(8,128)S(1)} %collective-permute-done.1.z_prev, ...), custom_call_target="tpu_custom_call" | custom-call | flops 1073741824 | bytes 2146304 | tf_op jit(solution)/shard_map/pallas_call | solution.py:424
  33.7 0.0 collective-permute-done.4.x_next
  33.7 2.1 %collective-permute-done.5.x_prev = f32[3,3,32,128]{3,2,1,0:T(8,128)S(1)} collective-permute-done((f32[3,3,32,128]{3,2,1,0:T(8,128)S(1)}, f32[3,3,32,128]{3,2,1,0:T(8,128)S(1)}, u32[]{:S(2)}, u32[]{:S(2)}) %collective-permute-start.5) | collective-permute-done | bytes 147488 | tf_op jit(solution)/shard_map/ppermute | solution.py:445
  35.8 0.0 copy-done
  35.8 3.3 %shard_map.101 = (f32[3,16,32,128]{3,2,1,0:T(8,128)}, f32[128,128]{1,0:T(8,128)S(1)}) custom-call(f32[3,16,32,128]{3,2,1,0:T(8,128)} %get-tuple-element.37.given, f32[3,16,32,128]{3,2,1,0:T(8,128)S(1)} %get-tuple-element.26.inner, f32[16,32,128]{2,1,0:T(8,128)S(1)} %get-tuple-element.27.stiffness, ...), custom_call_target="tpu_custom_call", output_to_operand_aliasing={{0}: (0, {})} | custom-call | flops 1073741824 | bytes 9732096 | tf_op jit(solution)/shard_map/pallas_call | solution.py:424
  39.2 34.2 %all_to_all.5 = f32[16,8,128]{2,1,0:T(8,128)S(1)} all-to-all(f32[16,8,128]{2,1,0:T(8,128)S(1)} %bitcast.8), channel_id=1, replica_groups=mesh['span'=8,'pitch'=8,'chord'=16] {'chord'}, dimensions={0} | all-to-all | bytes 131072 | tf_op jit(solution)/shard_map/all_to_all | solution.py:534
  73.4 0.6 reduce_sum.9
Async XLA Ops:
  0.6 15.0 %copy-start.3 = (s32[4096,1]{0,1:T(1,128)S(1)}, s32[4096,1]{0,1:T(1,128)}, u32[]{:S(2)}) copy-start(s32[4096,1]{0,1:T(1,128)} %param.13) | copy-start | bytes 49156
  0.6 15.0 %copy-start.2 = (s32[4096]{0:T(1024)S(1)}, s32[4096]{0:T(1024)}, u32[]{:S(2)}) copy-start(s32[4096]{0:T(1024)} %param.12) | copy-start | bytes 49156
  0.7 30.3 %copy-start.1 = (f32[3,4096]{1,0:T(4,128)S(1)}, f32[3,4096]{1,0:T(4,128)}, u32[]{:S(2)}) copy-start(f32[3,4096]{1,0:T(4,128)} %wall_normal.3) | copy-start | bytes 147460
  3.2 13.5 %collective-permute-start = (f32[56,128]{1,0:T(8,128)S(1)}, f32[56,128]{1,0:T(8,128)S(1)}, u32[]{:S(2)}, u32[]{:S(2)}) collective-permute-start(f32[56,128]{1,0:T(8,128)S(1)} %get-tuple-element.28), channel_id=1, source_target_pairs={{1,0},{2,1},{3,2},{4,3},{5,4},{6,5},{7,6},{8,7},{9,8},{10,9},{11,1... | collective-permute-start | bytes 86024 | tf_op jit(solution)/shard_map/ppermute | solution.py:441
  4.5 12.2 %collective-permute-start.1 = (f32[56,128]{1,0:T(8,128)S(1)}, f32[56,128]{1,0:T(8,128)S(1)}, u32[]{:S(2)}, u32[]{:S(2)}) collective-permute-start(f32[56,128]{1,0:T(8,128)S(1)} %get-tuple-element.29), channel_id=1, source_target_pairs={{0,1},{1,2},{2,3},{3,4},{4,5},{5,6},{6,7},{7,8},{8,9},{9,10},{10,1... | collective-permute-start | bytes 86024 | tf_op jit(solution)/shard_map/ppermute | solution.py:445
  17.1 4.3 %collective-permute-start.2 = (f32[168,128]{1,0:T(8,128)S(1)}, f32[168,128]{1,0:T(8,128)S(1)}, u32[]{:S(2)}, u32[]{:S(2)}) collective-permute-start(f32[168,128]{1,0:T(8,128)S(1)} %get-tuple-element.35), channel_id=1, source_target_pairs={{16,0},{32,16},{48,32},{64,48},{80,64},{96,80},{112,96},{17,1},{33... | collective-permute-start | bytes 258056 | tf_op jit(solution)/shard_map/ppermute | solution.py:441
  19.0 5.8 %collective-permute-start.3 = (f32[168,128]{1,0:T(8,128)S(1)}, f32[168,128]{1,0:T(8,128)S(1)}, u32[]{:S(2)}, u32[]{:S(2)}) collective-permute-start(f32[168,128]{1,0:T(8,128)S(1)} %get-tuple-element.36), channel_id=1, source_target_pairs={{0,16},{16,32},{32,48},{48,64},{64,80},{80,96},{96,112},{1,17},{17... | collective-permute-start | bytes 258056 | tf_op jit(solution)/shard_map/ppermute | solution.py:445
  25.0 10.8 %copy-start = (f32[8,4096]{1,0:T(8,128)S(1)}, f32[8,4096]{1,0:T(8,128)}, u32[]{:S(2)}) copy-start(f32[8,4096]{1,0:T(8,128)} %mode_shape.1) | copy-start | bytes 393220
  25.0 8.7 %collective-permute-start.4 = (f32[3,3,32,128]{3,2,1,0:T(8,128)S(1)}, f32[3,3,32,128]{3,2,1,0:T(8,128)S(1)}, u32[]{:S(2)}, u32[]{:S(2)}) collective-permute-start(f32[3,3,32,128]{3,2,1,0:T(8,128)S(1)} %get-tuple-element.39), channel_id=1, source_target_pairs={{128,0},{256,128},{384,256},{512,384},{640,512},{768,640},{896,768... | collective-permute-start | bytes 442376 | tf_op jit(solution)/shard_map/ppermute | solution.py:441
  27.6 8.2 %collective-permute-start.5 = (f32[3,3,32,128]{3,2,1,0:T(8,128)S(1)}, f32[3,3,32,128]{3,2,1,0:T(8,128)S(1)}, u32[]{:S(2)}, u32[]{:S(2)}) collective-permute-start(f32[3,3,32,128]{3,2,1,0:T(8,128)S(1)} %get-tuple-element.40), channel_id=1, source_target_pairs={{0,128},{128,256},{256,384},{384,512},{512,640},{640,768},{768,896... | collective-permute-start | bytes 442376 | tf_op jit(solution)/shard_map/ppermute | solution.py:445

commit v8 on v5

--- a/solution.py
+++ b/solution.py
@@ -348,7 +348,7 @@
 
 
 def wall_kernel(
-    given, inner, stiffness, z_next, z_prev, y_next, y_prev, x_next, x_prev, share,
+    given, inner, stiffness, z_next, z_prev, y_next, y_prev, x_prev, x_next, share,
     wall_cell, patch_owner, wall_normal, mode_shape, planes, patches,
     adjoint, sums, columns, values, part, field, sems,
 ):
@@ -478,7 +478,7 @@
     low, high = call(
         span_kernel, (slab, slab), (x_out, z_next, z_prev, y_next, y_prev), "vvvvv", scratch=(columns,)
     )
-    x_next, x_prev = from_next(low, "span"), from_previous(high, "span")
+    x_prev, x_next = from_previous(high, "span"), from_next(low, "span")
     given = (z_next, z_prev, y_next, y_prev)
     work = (
         columns,
@@ -499,7 +499,7 @@
         wall_kernel,
         (block, (CHORD * MODES, PATCH_DEV)),
         (
-            adjoint, inner, stiffness, *given, x_next, x_prev, share,
+            adjoint, inner, stiffness, *given, x_prev, x_next, share,
             cells, owners, wall_normal, mode_shape, planes, patches,
         ),
         "hvvvvvvvvvvvvvvv",

time: 74.6 us -> 76.8 us (1.029)
  the two profiles are of different devices: /device:TPU:24 before, /device:TPU:22 now
where the time goes in v8:
time: 76.8 us; the launch traced here: 76.5 us
  blocking collectives  34.2 us (45%)
  starting transfers between devices  20.7 us (27%)
  Pallas kernels  12.9 us (17%)
  waiting for transfers between devices  7.24 us (9%)
  between operations  0.82 us (1%)
    all_to_all x1, blocking collectives, body(): lax.all_to_all(sums, 'chord', split_axis=0, concat_axis=0, tiled=True)  34.2 us
    ppermute x3, starting transfers between devices, from_previous(): return lax.ppermute(high, axis, pairs(axis))  15.6 us
    pallas_call x7, Pallas kernels, call(): pl.pallas_call(kernel, out_shape=shapes, in_specs=[spec[space] for space...  12.9 us
    ppermute x3, starting transfers between devices, from_next(): return lax.ppermute(low, axis, [(j, i) for i, j in pairs(axis)])  5.13 us
    ppermute x3, waiting for transfers between devices, from_previous(): return lax.ppermute(high, axis, pairs(axis))  3.65 us
    ppermute x3, waiting for transfers between devices, from_next(): return lax.ppermute(low, axis, [(j, i) for i, j in pairs(axis)])  3.59 us
  transfers between devices with their start and end apart: 6, of which 2 were waited for; matrix products, arithmetic and copies ran while one was open for 0% of the time, Pallas kernels for 8%

profile of v8, /device:TPU:22, one launch (start us, length us, event | category | flops | bytes accessed | tf_op | source)
XLA Modules:
  0.0 76.5 jit_solution(9743509914551569197)
XLA Ops:
  0.6 0.0 copy-start.3
  0.6 0.0 copy-start.2
  0.7 0.0 copy-start.1
  0.7 2.6 %shard_map.95 = (f32[3,16,32,128]{3,2,1,0:T(8,128)S(1)}, f32[3,16,32,128]{3,2,1,0:T(8,128)S(1)}, f32[16,32,128]{2,1,0:T(8,128)S(1)}, f32[56,128]{1,0:T(8,128)S(1)}, f32[56,128]{1,0:T(8,128)S(1)}) custom-call(f32[8]{0:T(128)} %table_in.1, f32[3,16,32,128]{3,2,1,0:T(8,128)} %start.1, f32[3,16,32,128]{3,2,1,0:T(8,128)} %source.1, s32[16,32,128]{2,1,0:T(8,128)} %classes.1), custom_call_target="tpu_custom_call" | custom-call | bytes 3727392 | tf_op jit(solution)/shard_map/pallas_call | solution.py:402
  3.3 1.3 %collective-permute-start = (f32[56,128]{1,0:T(8,128)S(1)}, f32[56,128]{1,0:T(8,128)S(1)}, u32[]{:S(2)}, u32[]{:S(2)}) collective-permute-start(f32[56,128]{1,0:T(8,128)S(1)} %get-tuple-element.28), channel_id=1, source_target_pairs={{1,0},{2,1},{3,2},{4,3},{5,4},{6,5},{7,6},{8,7},{9,8},{10,9},{11,1... | collective-permute-start | bytes 86024 | tf_op jit(solution)/shard_map/ppermute | solution.py:419
  4.6 8.5 %collective-permute-start.1 = (f32[56,128]{1,0:T(8,128)S(1)}, f32[56,128]{1,0:T(8,128)S(1)}, u32[]{:S(2)}, u32[]{:S(2)}) collective-permute-start(f32[56,128]{1,0:T(8,128)S(1)} %get-tuple-element.29), channel_id=1, source_target_pairs={{0,1},{1,2},{2,3},{3,4},{4,5},{5,6},{6,7},{7,8},{8,9},{9,10},{10,1... | collective-permute-start | bytes 86024 | tf_op jit(solution)/shard_map/ppermute | solution.py:423
  13.1 2.6 %shard_map.96 = (f32[3,16,32,128]{3,2,1,0:T(8,128)S(1)}, f32[3,24,8,128]{3,2,1,0:T(8,128)S(1)}, f32[3,24,8,128]{3,2,1,0:T(8,128)S(1)}, f32[3,6,32,128]{3,2,1,0:T(8,128)S(1)}) custom-call(f32[3,16,32,128]{3,2,1,0:T(8,128)S(1)} %get-tuple-element.24.p0_in, f32[3,16,32,128]{3,2,1,0:T(8,128)S(1)} %get-tuple-element.25.cs_in), custom_call_target="tpu_custom_call" | custom-call | flops 33554432 | bytes 3244032 | tf_op jit(solution)/shard_map/pallas_call | solution.py:402
  15.7 0.0 copy-done.3
  15.7 0.0 copy-done.2
  15.7 1.1 %shard_map.97 = (bf16[256,4096]{1,0:T(8,128)(2,1)S(1)}, bf16[4096,128]{1,0:T(8,128)(2,1)S(1)}) custom-call(s32[1,4096]{1,0:T(1,128)S(1)} %bitcast.3, s32[1,4096]{1,0:T(1,128)S(1)} %bitcast.6, f32[3,24,8,128]{3,2,1,0:T(8,128)S(1)} %get-tuple-element.33.after.y_low), custom_call_target="tpu_custom_call" | custom-call | flops 33554432 | bytes 6619136 | tf_op jit(solution)/shard_map/pallas_call | solution.py:402
  16.8 0.0 collective-permute-done.z_next
  16.8 0.0 collective-permute-done.1.z_prev
  16.8 0.3 shard_map.98
  17.1 1.9 %collective-permute-start.2 = (f32[3,3,24,128]{3,2,1,0:T(8,128)S(1)}, f32[3,3,24,128]{3,2,1,0:T(8,128)S(1)}, u32[]{:S(2)}, u32[]{:S(2)}) collective-permute-start(f32[3,3,24,128]{3,2,1,0:T(8,128)S(1)} %get-tuple-element.35), channel_id=1, source_target_pairs={{16,0},{32,16},{48,32},{64,48},{80,64},{96,80},{112,96},{17,1},{33... | collective-permute-start | bytes 331784 | tf_op jit(solution)/shard_map/ppermute | solution.py:419
  19.1 2.4 %collective-permute-start.3 = (f32[3,3,24,128]{3,2,1,0:T(8,128)S(1)}, f32[3,3,24,128]{3,2,1,0:T(8,128)S(1)}, u32[]{:S(2)}, u32[]{:S(2)}) collective-permute-start(f32[3,3,24,128]{3,2,1,0:T(8,128)S(1)} %get-tuple-element.36), channel_id=1, source_target_pairs={{0,16},{16,32},{32,48},{48,64},{64,80},{80,96},{96,112},{1,17},{17... | collective-permute-start | bytes 331784 | tf_op jit(solution)/shard_map/ppermute | solution.py:423
  21.5 0.0 collective-permute-done.2.y_next
  21.5 3.6 %collective-permute-done.3.y_prev = f32[3,3,24,128]{3,2,1,0:T(8,128)S(1)} collective-permute-done((f32[3,3,24,128]{3,2,1,0:T(8,128)S(1)}, f32[3,3,24,128]{3,2,1,0:T(8,128)S(1)}, u32[]{:S(2)}, u32[]{:S(2)}) %collective-permute-start.3) | collective-permute-done | bytes 110624 | tf_op jit(solution)/shard_map/ppermute | solution.py:423
  25.1 0.2 shard_map.100
  25.3 0.0 copy-start
  25.3 4.7 %collective-permute-start.4 = (f32[3,3,32,128]{3,2,1,0:T(8,128)S(1)}, f32[3,3,32,128]{3,2,1,0:T(8,128)S(1)}, u32[]{:S(2)}, u32[]{:S(2)}) collective-permute-start(f32[3,3,32,128]{3,2,1,0:T(8,128)S(1)} %get-tuple-element.39), channel_id=1, source_target_pairs={{0,128},{128,256},{256,384},{384,512},{512,640},{640,768},{768,896... | collective-permute-start | bytes 442376 | tf_op jit(solution)/shard_map/ppermute | solution.py:423
  30.1 1.9 %collective-permute-start.5 = (f32[3,3,32,128]{3,2,1,0:T(8,128)S(1)}, f32[3,3,32,128]{3,2,1,0:T(8,128)S(1)}, u32[]{:S(2)}, u32[]{:S(2)}) collective-permute-start(f32[3,3,32,128]{3,2,1,0:T(8,128)S(1)} %get-tuple-element.40), channel_id=1, source_target_pairs={{128,0},{256,128},{384,256},{512,384},{640,512},{768,640},{896,768... | collective-permute-start | bytes 442376 | tf_op jit(solution)/shard_map/ppermute | solution.py:419
  32.0 0.0 copy-done.1
  32.0 2.7 %shard_map.99 = (f32[3,16,32,128]{3,2,1,0:T(8,128)}, f32[1,4096]{1,0:T(1,128)S(1)}) custom-call(f32[3,16,32,128]{3,2,1,0:T(8,128)S(1)} %get-tuple-element.26.inner, f32[16,32,128]{2,1,0:T(8,128)S(1)} %get-tuple-element.27.stiffness, f32[56,128]{1,0:T(8,128)S(1)} %collective-permute-done.z_next, f32[56,128]{1,0:T(8,128)S(1)} %collective-permute-done.1.z_prev, ...), custom_call_target="tpu_custom_call" | custom-call | flops 1073741824 | bytes 2195456 | tf_op jit(solution)/shard_map/pallas_call | solution.py:402
  34.7 0.0 collective-permute-done.4.x_prev
  34.8 3.6 %collective-permute-done.5.x_next = f32[3,3,32,128]{3,2,1,0:T(8,128)S(1)} collective-permute-done((f32[3,3,32,128]{3,2,1,0:T(8,128)S(1)}, f32[3,3,32,128]{3,2,1,0:T(8,128)S(1)}, u32[]{:S(2)}, u32[]{:S(2)}) %collective-permute-start.5) | collective-permute-done | bytes 147488 | tf_op jit(solution)/shard_map/ppermute | solution.py:419
  38.3 0.0 copy-done
  38.3 3.3 %shard_map.101 = (f32[3,16,32,128]{3,2,1,0:T(8,128)}, f32[128,128]{1,0:T(8,128)S(1)}) custom-call(f32[3,16,32,128]{3,2,1,0:T(8,128)} %get-tuple-element.37.given, f32[3,16,32,128]{3,2,1,0:T(8,128)S(1)} %get-tuple-element.26.inner, f32[16,32,128]{2,1,0:T(8,128)S(1)} %get-tuple-element.27.stiffness, ...), custom_call_target="tpu_custom_call", output_to_operand_aliasing={{0}: (0, {})} | custom-call | flops 1073741824 | bytes 9781248 | tf_op jit(solution)/shard_map/pallas_call | solution.py:402
  41.7 34.2 %all_to_all.5 = f32[16,8,128]{2,1,0:T(8,128)S(1)} all-to-all(f32[16,8,128]{2,1,0:T(8,128)S(1)} %bitcast.8), channel_id=1, replica_groups=mesh['span'=8,'pitch'=8,'chord'=16] {'chord'}, dimensions={0} | all-to-all | bytes 131072 | tf_op jit(solution)/shard_map/all_to_all | solution.py:512
  75.9 0.6 reduce_sum.9
Async XLA Ops:
  0.6 15.1 %copy-start.3 = (s32[4096,1]{0,1:T(1,128)S(1)}, s32[4096,1]{0,1:T(1,128)}, u32[]{:S(2)}) copy-start(s32[4096,1]{0,1:T(1,128)} %param.13) | copy-start | bytes 49156
  0.6 15.1 %copy-start.2 = (s32[4096]{0:T(1024)S(1)}, s32[4096]{0:T(1024)}, u32[]{:S(2)}) copy-start(s32[4096]{0:T(1024)} %param.12) | copy-start | bytes 49156
  0.7 31.4 %copy-start.1 = (f32[3,4096]{1,0:T(4,128)S(1)}, f32[3,4096]{1,0:T(4,128)}, u32[]{:S(2)}) copy-start(f32[3,4096]{1,0:T(4,128)} %wall_normal.3) | copy-start | bytes 147460
  3.3 13.5 %collective-permute-start = (f32[56,128]{1,0:T(8,128)S(1)}, f32[56,128]{1,0:T(8,128)S(1)}, u32[]{:S(2)}, u32[]{:S(2)}) collective-permute-start(f32[56,128]{1,0:T(8,128)S(1)} %get-tuple-element.28), channel_id=1, source_target_pairs={{1,0},{2,1},{3,2},{4,3},{5,4},{6,5},{7,6},{8,7},{9,8},{10,9},{11,1... | collective-permute-start | bytes 86024 | tf_op jit(solution)/shard_map/ppermute | solution.py:419
  4.6 12.2 %collective-permute-start.1 = (f32[56,128]{1,0:T(8,128)S(1)}, f32[56,128]{1,0:T(8,128)S(1)}, u32[]{:S(2)}, u32[]{:S(2)}) collective-permute-start(f32[56,128]{1,0:T(8,128)S(1)} %get-tuple-element.29), channel_id=1, source_target_pairs={{0,1},{1,2},{2,3},{3,4},{4,5},{5,6},{6,7},{7,8},{8,9},{9,10},{10,1... | collective-permute-start | bytes 86024 | tf_op jit(solution)/shard_map/ppermute | solution.py:423
  17.1 4.3 %collective-permute-start.2 = (f32[3,3,24,128]{3,2,1,0:T(8,128)S(1)}, f32[3,3,24,128]{3,2,1,0:T(8,128)S(1)}, u32[]{:S(2)}, u32[]{:S(2)}) collective-permute-start(f32[3,3,24,128]{3,2,1,0:T(8,128)S(1)} %get-tuple-element.35), channel_id=1, source_target_pairs={{16,0},{32,16},{48,32},{64,48},{80,64},{96,80},{112,96},{17,1},{33... | collective-permute-start | bytes 331784 | tf_op jit(solution)/shard_map/ppermute | solution.py:419
  19.1 6.1 %collective-permute-start.3 = (f32[3,3,24,128]{3,2,1,0:T(8,128)S(1)}, f32[3,3,24,128]{3,2,1,0:T(8,128)S(1)}, u32[]{:S(2)}, u32[]{:S(2)}) collective-permute-start(f32[3,3,24,128]{3,2,1,0:T(8,128)S(1)} %get-tuple-element.36), channel_id=1, source_target_pairs={{0,16},{16,32},{32,48},{48,64},{64,80},{80,96},{96,112},{1,17},{17... | collective-permute-start | bytes 331784 | tf_op jit(solution)/shard_map/ppermute | solution.py:423
  25.3 13.0 %copy-start = (f32[8,4096]{1,0:T(8,128)S(1)}, f32[8,4096]{1,0:T(8,128)}, u32[]{:S(2)}) copy-start(f32[8,4096]{1,0:T(8,128)} %mode_shape.1) | copy-start | bytes 393220
  25.3 9.4 %collective-permute-start.4 = (f32[3,3,32,128]{3,2,1,0:T(8,128)S(1)}, f32[3,3,32,128]{3,2,1,0:T(8,128)S(1)}, u32[]{:S(2)}, u32[]{:S(2)}) collective-permute-start(f32[3,3,32,128]{3,2,1,0:T(8,128)S(1)} %get-tuple-element.39), channel_id=1, source_target_pairs={{0,128},{128,256},{256,384},{384,512},{512,640},{640,768},{768,896... | collective-permute-start | bytes 442376 | tf_op jit(solution)/shard_map/ppermute | solution.py:423
  30.1 8.2 %collective-permute-start.5 = (f32[3,3,32,128]{3,2,1,0:T(8,128)S(1)}, f32[3,3,32,128]{3,2,1,0:T(8,128)S(1)}, u32[]{:S(2)}, u32[]{:S(2)}) collective-permute-start(f32[3,3,32,128]{3,2,1,0:T(8,128)S(1)} %get-tuple-element.40), channel_id=1, source_target_pairs={{128,0},{256,128},{384,256},{512,384},{640,512},{768,640},{896,768... | collective-permute-start | bytes 442376 | tf_op jit(solution)/shard_map/ppermute | solution.py:419
